TPU v7x, 32 devices: a whole 2x2x4 slice. The times are simulated.
32 devices in a mesh: expert: 4 (over y, core), shard: 8 (over z, x).
Axes of the slice: x: 2, y: 2, z: 4, core: 2. Of those that a mesh axis runs over, the one named last changes fastest.
Arguments:
- tokens: bfloat16 [8192, 1536], P(('expert', 'shard')), may hold values from -6 to 6
- lengths: int32 [32], P(('expert', 'shard')), may hold values from 64 to 256, as said below
- routes: int32 [8192, 8], P(('expert', 'shard')), may hold values from 0 to 19, all different within a row; in each aligned block of 256 rows (0 to 255, 256 to 511, ...) at most 104 rows name the same one
- cotangent: bfloat16 [8192, 1536], P(('expert', 'shard')), may hold values from -6 to 6
- first_gain: bfloat16 [1536], P('shard'), may hold values from 0.5 to 1.5
- query_weight: bfloat16 [1536, 1536], P('shard'), may hold values from -0.15625 to 0.15625
- key_matrix: bfloat16 [1536, 512], P('shard'), may hold values from -0.15625 to 0.15625
- value_matrix: bfloat16 [1536, 512], P('shard'), may hold values from -0.15625 to 0.15625
- output_weight: bfloat16 [1536, 1536], P('shard'), may hold values from -1.25 to 1.25
- second_gain: bfloat16 [1536], P('shard'), may hold values from 0.5 to 1.5
- router_weight: bfloat16 [1536, 20], P('shard'), may hold values from -0.078125 to 0.078125
- gate_up_weight: bfloat16 [1536, 20, 1024], P('shard', 'expert'), may hold values from -0.15625 to 0.15625
- down_weight: bfloat16 [1536, 20, 512], P('shard', 'expert'), may hold values from -1 to 1
Outputs:
- layer_out: bfloat16 [8192, 1536], P(('expert', 'shard'))
- tokens_grad: float32 [8192, 1536], P(('expert', 'shard'))
- first_gain_grad: float32 [1536], P('shard')
- query_grad: float32 [1536, 1536], P('shard')
- key_grad: float32 [1536, 512], P('shard')
- value_grad: float32 [1536, 512], P('shard')
- output_grad: float32 [1536, 1536], P('shard')
- second_gain_grad: float32 [1536], P('shard')
- router_grad: float32 [1536, 20], P('shard')
- gate_up_grad: float32 [1536, 20, 1024], P('shard', 'expert')
- down_grad: float32 [1536, 20, 512], P('shard', 'expert')
Inputs may be any that keep to these rules, and one draw needn't show every extreme that they name: `lengths`: some sequence has 256 valid tokens and some 256 // 4. `routes`: each row names 8 different experts; among the 256 rows of one sequence no expert is named more than 104 times, a bound that some block reaches.
All inputs are finite; a program needn't handle non-finite values.
Results may differ from a plain program's by a relative error of at most 0.02.
Values may be sent and summed in bfloat16 or wider, within the bound.
A program may use at most 320 MiB of HBM per device.

v0:
```python
import jax
import jax.numpy as jnp
from jax import lax
from jax.sharding import PartitionSpec as P

HEAD_DIM = 64


norm_eps = 1e-06


def product(form, left, right):
    return jnp.einsum(form, left, right, preferred_element_type=jnp.float32)


def rope_tables(row_count, head_width):
    half_width = head_width // 2
    frequency = 10000.0 ** (-(jnp.arange(half_width, dtype=jnp.float32) * (2.0 / head_width)))
    angles = jnp.arange(row_count, dtype=jnp.float32)[:, None] * frequency[None, :]
    return (jnp.cos(angles)[:, None, :], jnp.sin(angles)[:, None, :])


def rotate(values_in, cosine, sine_table):
    half_width = values_in.shape[-1] // 2
    first_half = values_in[..., :half_width]
    second_half = values_in[..., half_width:]
    return jnp.concatenate(
        [
            first_half * cosine - second_half * sine_table,
            second_half * cosine + first_half * sine_table,
        ],
        axis=-1,
    )


def unrotate(grad_in, cosine, sine_table):
    half_width = grad_in.shape[-1] // 2
    first_half = grad_in[..., :half_width]
    second_half = grad_in[..., half_width:]
    return jnp.concatenate(
        [
            first_half * cosine + second_half * sine_table,
            second_half * cosine - first_half * sine_table,
        ],
        axis=-1,
    )


def norm_back(upstream, source, inv_scale, gain_vec):
    scaled = upstream * gain_vec
    gain_grad = jnp.sum(upstream * source * inv_scale, axis=0)
    grad_out = inv_scale * (
        scaled - source * inv_scale * inv_scale * jnp.mean(scaled * source, axis=-1, keepdims=True)
    )
    return (grad_out, gain_grad)


def on_device(
    tokens,
    lengths,
    routes,
    cotangent,
    first_gain,
    query_weight,
    key_matrix,
    value_matrix,
    output_weight,
    second_gain,
    router_weight,
    gate_up_weight,
    down_weight,
):
    seq_len, model_width = tokens.shape
    route_width = routes.shape[1]
    q_heads = query_weight.shape[1] // HEAD_DIM
    kv_heads = key_matrix.shape[1] // HEAD_DIM
    group_size = q_heads // kv_heads
    experts_all = router_weight.shape[1]
    local_experts = gate_up_weight.shape[1]
    inner_width = down_weight.shape[2]
    owners = lax.axis_size("expert")
    slot_count = 8 * max(
        seq_len // 32, (seq_len * route_width + 8 * experts_all - 1) // (8 * experts_all)
    )
    score_factor = HEAD_DIM ** (-0.5)
    gain_one, query_full, key_complete, value_complete, output_full, gain_two, router_full = (
        lax.all_gather(first_gain, "shard", axis=0, tiled=True),
        lax.all_gather(query_weight, "shard", axis=0, tiled=True),
        lax.all_gather(key_matrix, "shard", axis=0, tiled=True),
        lax.all_gather(value_matrix, "shard", axis=0, tiled=True),
        lax.all_gather(output_weight, "shard", axis=0, tiled=True),
        lax.all_gather(second_gain, "shard", axis=0, tiled=True),
        lax.all_gather(router_weight, "shard", axis=0, tiled=True),
    )
    gate_up_full, down_full = (
        lax.all_gather(gate_up_weight, "shard", axis=0, tiled=True),
        lax.all_gather(down_weight, "shard", axis=0, tiled=True),
    )
    gain_one = gain_one.astype(jnp.float32)
    gain_two = gain_two.astype(jnp.float32)
    cosine, sine_table = rope_tables(seq_len, HEAD_DIM)
    source = tokens.astype(jnp.float32)
    first_scale = lax.rsqrt(jnp.mean(source * source, axis=-1, keepdims=True) + norm_eps)
    first_norm_output = (source * first_scale * gain_one).astype(jnp.bfloat16)
    queries = rotate(
        product("za,ao->zo", first_norm_output, query_full).reshape(seq_len, q_heads, HEAD_DIM),
        cosine,
        sine_table,
    )
    queries = queries.astype(jnp.bfloat16).reshape(seq_len, kv_heads, group_size, HEAD_DIM)
    key_row_block = rotate(
        product("za,ao->zo", first_norm_output, key_complete).reshape(seq_len, kv_heads, HEAD_DIM),
        cosine,
        sine_table,
    ).astype(jnp.bfloat16)
    value_row_block = (
        product("za,ao->zo", first_norm_output, value_complete)
        .astype(jnp.bfloat16)
        .reshape(seq_len, kv_heads, HEAD_DIM)
    )
    position = jnp.arange(seq_len, dtype=jnp.int32)
    length = lengths[0]
    allowed = (position[None, :] <= position[:, None]) & (position[None, :] < length)
    scores = jnp.where(
        allowed, product("qhgd,khd->hgqk", queries, key_row_block) * score_factor, -1e30
    )
    row_max = jnp.max(scores, axis=-1, keepdims=True)
    shifted = jnp.exp(scores - row_max)
    row_total = jnp.sum(shifted, axis=-1, keepdims=True)
    log_total = row_max + jnp.log(row_total)
    probs_low = (shifted / row_total).astype(jnp.bfloat16)
    mixed_heads = (
        product("hgqk,khd->qhgd", probs_low, value_row_block)
        .reshape(seq_len, q_heads * HEAD_DIM)
        .astype(jnp.bfloat16)
    )
    hidden = source + product("sf,df->sd", mixed_heads, output_full)
    second_scale = lax.rsqrt(jnp.mean(hidden * hidden, axis=-1, keepdims=True) + norm_eps)
    second_normed = (hidden * second_scale * gain_two).astype(jnp.bfloat16)
    logits = product("sd,de->se", second_normed, router_full)
    chosen = (routes[:, :, None] == jnp.arange(experts_all, dtype=jnp.int32)).astype(jnp.float32)
    picked = jnp.sum(chosen * logits[:, None, :], axis=-1)
    gate_soft = jax.nn.softmax(picked, axis=-1)
    valid_rows = (position < length).astype(jnp.float32)
    routed = jnp.sum(chosen, axis=1) * valid_rows[:, None]
    earlier = (position[None, :] < position[:, None]).astype(jnp.bfloat16)
    rank_rows = product("st,te->se", earlier, routed.astype(jnp.bfloat16))
    slot_ids = jnp.arange(slot_count, dtype=jnp.float32)
    placing = (routed.T[:, None, :] * (rank_rows.T[:, None, :] == slot_ids[None, :, None])).astype(
        jnp.bfloat16
    )
    outgoing = (
        product("ems,sd->emd", placing, second_normed)
        .astype(jnp.bfloat16)
        .reshape(owners, local_experts, slot_count, model_width)
    )
    row_block = lax.all_to_all(outgoing, "expert", split_axis=0, concat_axis=0, tiled=True)
    both_pre = product("oemd,def->oemf", row_block, gate_up_full)
    active = (jax.nn.silu(both_pre[..., :inner_width]) * both_pre[..., inner_width:]).astype(
        jnp.bfloat16
    )
    answer = product("oemf,def->oemd", active, down_full).astype(jnp.bfloat16)
    returned = lax.all_to_all(answer, "expert", split_axis=0, concat_axis=0, tiled=True).reshape(
        experts_all, slot_count, model_width
    )
    gate_full = product("ske,sk->se", chosen.astype(jnp.bfloat16), gate_soft.astype(jnp.bfloat16))
    placing_float = placing.astype(jnp.float32)
    combine = (placing_float * gate_full.T[:, None, :]).astype(jnp.bfloat16)
    output = (hidden + product("ems,emd->sd", combine, returned)).astype(jnp.bfloat16)
    dout_full = cotangent.astype(jnp.float32) * valid_rows[:, None]
    dout_low = dout_full.astype(jnp.bfloat16)
    grad_rows = (
        product("ems,sd->emd", combine, dout_low)
        .astype(jnp.bfloat16)
        .reshape(owners, local_experts, slot_count, model_width)
    )
    incoming = lax.all_to_all(grad_rows, "expert", split_axis=0, concat_axis=0, tiled=True)
    answer_dot = product("emd,sd->ems", returned, dout_low)
    gate_grad_full = jnp.sum(placing_float * answer_dot, axis=1)
    gate_grad = jnp.sum(chosen * gate_grad_full.T[:, None, :], axis=-1)
    inner_sum = jnp.sum(gate_soft * gate_grad, axis=-1, keepdims=True)
    picked_grad = gate_soft * (gate_grad - inner_sum)
    logits_grad = jnp.sum(chosen * picked_grad[:, :, None], axis=1).astype(jnp.bfloat16)
    router_term = product("sd,se->de", second_normed, logits_grad)
    gate_up_full, down_full = (
        lax.all_gather(gate_up_weight, "shard", axis=0, tiled=True),
        lax.all_gather(down_weight, "shard", axis=0, tiled=True),
    )
    gate_part = both_pre[..., :inner_width]
    up_part = both_pre[..., inner_width:]
    sigmoid_gate = jax.nn.sigmoid(gate_part)
    silu_gate = gate_part * sigmoid_gate
    active_again = (silu_gate * up_part).astype(jnp.bfloat16)
    active_grad = product("oemd,def->oemf", incoming, down_full)
    both_grad = jnp.concatenate(
        [
            active_grad * up_part * sigmoid_gate * (1.0 + gate_part * (1.0 - sigmoid_gate)),
            active_grad * silu_gate,
        ],
        axis=-1,
    ).astype(jnp.bfloat16)
    row_grad = product("oemf,def->oemd", both_grad, gate_up_full).astype(jnp.bfloat16)
    gate_up_term = product("oemd,oemf->def", row_block, both_grad)
    down_term = product("oemd,oemf->def", incoming, active_again)
    back_rows = lax.all_to_all(row_grad, "expert", split_axis=0, concat_axis=0, tiled=True).reshape(
        experts_all, slot_count, model_width
    )
    gate_up_total, down_total = (
        lax.psum_scatter(
            gate_up_term.astype(jnp.bfloat16), "shard", scatter_dimension=0, tiled=True
        ).astype(jnp.float32),
        lax.psum_scatter(
            down_term.astype(jnp.bfloat16), "shard", scatter_dimension=0, tiled=True
        ).astype(jnp.float32),
    )
    normed_grad = product("ems,emd->sd", placing, back_rows) + product(
        "se,de->sd", logits_grad, router_full
    )
    hidden_grad, second_gain_term = norm_back(normed_grad, hidden, second_scale, gain_two)
    hidden_grad = hidden_grad + dout_full
    attn_grad = hidden_grad.astype(jnp.bfloat16)
    output_term = product("sd,sf->df", attn_grad, mixed_heads)
    mixed_grad = (
        product("za,ao->zo", attn_grad, output_full)
        .astype(jnp.bfloat16)
        .reshape(seq_len, kv_heads, group_size, HEAD_DIM)
    )
    scores_again = jnp.where(
        allowed, product("qhgd,khd->hgqk", queries, key_row_block) * score_factor, -1e30
    )
    probs_again = jnp.exp(scores_again - log_total)
    probs_grad = product("qhgd,khd->hgqk", mixed_grad, value_row_block)
    row_inner = jnp.sum(probs_again * probs_grad, axis=-1, keepdims=True)
    scores_grad = (probs_again * (probs_grad - row_inner)).astype(jnp.bfloat16)
    query_back = product("hgqk,khd->qhgd", scores_grad, key_row_block) * score_factor
    key_back = product("hgqk,qhgd->khd", scores_grad, queries) * score_factor
    value_back = product("hgqk,qhgd->khd", probs_again.astype(jnp.bfloat16), mixed_grad)
    query_pre = (
        unrotate(query_back.reshape(seq_len, q_heads, HEAD_DIM), cosine, sine_table)
        .astype(jnp.bfloat16)
        .reshape(seq_len, q_heads * HEAD_DIM)
    )
    key_pre = (
        unrotate(key_back, cosine, sine_table)
        .astype(jnp.bfloat16)
        .reshape(seq_len, kv_heads * HEAD_DIM)
    )
    value_pre = value_back.astype(jnp.bfloat16).reshape(seq_len, kv_heads * HEAD_DIM)
    query_term = product("sd,sf->df", first_norm_output, query_pre)
    key_term = product("sd,sf->df", first_norm_output, key_pre)
    value_term = product("sd,sf->df", first_norm_output, value_pre)
    normed1_grad = (
        product("sf,df->sd", query_pre, query_full)
        + product("sf,df->sd", key_pre, key_complete)
        + product("sf,df->sd", value_pre, value_complete)
    )
    tokens_grad, first_gain_term = norm_back(normed1_grad, source, first_scale, gain_one)
    tokens_grad = tokens_grad + hidden_grad
    mixer_sums = (
        lax.psum_scatter(
            first_gain_term.astype(jnp.bfloat16), "shard", scatter_dimension=0, tiled=True
        ).astype(jnp.float32),
        lax.psum_scatter(
            query_term.astype(jnp.bfloat16), "shard", scatter_dimension=0, tiled=True
        ).astype(jnp.float32),
        lax.psum_scatter(
            key_term.astype(jnp.bfloat16), "shard", scatter_dimension=0, tiled=True
        ).astype(jnp.float32),
        lax.psum_scatter(
            value_term.astype(jnp.bfloat16), "shard", scatter_dimension=0, tiled=True
        ).astype(jnp.float32),
        lax.psum_scatter(
            output_term.astype(jnp.bfloat16), "shard", scatter_dimension=0, tiled=True
        ).astype(jnp.float32),
        lax.psum_scatter(
            second_gain_term.astype(jnp.bfloat16), "shard", scatter_dimension=0, tiled=True
        ).astype(jnp.float32),
        lax.psum_scatter(
            router_term.astype(jnp.bfloat16), "shard", scatter_dimension=0, tiled=True
        ).astype(jnp.float32),
    )
    mixer_sums = (
        lax.psum(mixer_sums[0].astype(jnp.bfloat16), "expert").astype(jnp.float32),
        lax.psum(mixer_sums[1].astype(jnp.bfloat16), "expert").astype(jnp.float32),
        lax.psum(mixer_sums[2].astype(jnp.bfloat16), "expert").astype(jnp.float32),
        lax.psum(mixer_sums[3].astype(jnp.bfloat16), "expert").astype(jnp.float32),
        lax.psum(mixer_sums[4].astype(jnp.bfloat16), "expert").astype(jnp.float32),
        lax.psum(mixer_sums[5].astype(jnp.bfloat16), "expert").astype(jnp.float32),
        lax.psum(mixer_sums[6].astype(jnp.bfloat16), "expert").astype(jnp.float32),
    )
    return (
        output,
        tokens_grad,
        mixer_sums[0],
        mixer_sums[1],
        mixer_sums[2],
        mixer_sums[3],
        mixer_sums[4],
        mixer_sums[5],
        mixer_sums[6],
        gate_up_total,
        down_total,
    )


def solution(mesh):
    placed = (
        P(("expert", "shard"), None),
        P(("expert", "shard")),
        P(("expert", "shard"), None),
        P(("expert", "shard"), None),
        P("shard"),
        P("shard", None),
        P("shard", None),
        P("shard", None),
        P("shard", None),
        P("shard"),
        P("shard", None),
        P("shard", "expert", None),
        P("shard", "expert", None),
    )
    return jax.shard_map(
        on_device,
        mesh=mesh,
        in_specs=placed,
        out_specs=(
            P(("expert", "shard"), None),
            P(("expert", "shard"), None),
            P("shard"),
            P("shard", None),
            P("shard", None),
            P("shard", None),
            P("shard", None),
            P("shard"),
            P("shard", None),
            P("shard", "expert", None),
            P("shard", "expert", None),
        ),
        check_vma=False,
    )
```

profile of v0, /device:TPU:10, one launch (start us, length us, event | category | flops | bytes accessed | tf_op | source)
XLA Modules:
  0.0 1749.3 jit_solution(12676118598216443781)
XLA Ops:
  13.8 15.4 all-reduce.5
  30.1 24.9 %all-gather.8.cloned.1.call-done = bf16[1536,512]{1,0:T(8,128)(2,1)} async-done(((bf16[192,512]{1,0:T(8,128)(2,1)}), bf16[1536,512]{1,0:T(8,128)(2,1)}) %all-gather.8.cloned.1.call-update) | async-done | bytes 1572880 | tf_op jit(solution)/shard_map/all_gather | solution.py:90
  57.2 42.6 %all-gather.10.cloned.1.call-done = bf16[1536,512]{1,0:T(8,128)(2,1)} async-done(((bf16[192,512]{1,0:T(8,128)(2,1)}), bf16[1536,512]{1,0:T(8,128)(2,1)}) %all-gather.10.cloned.1.call-update) | async-done | bytes 1572880 | tf_op jit(solution)/shard_map/all_gather | solution.py:89
  102.1 77.1 %all-gather.12.cloned.1.call-done = bf16[1536,1536]{1,0:T(8,128)(2,1)} async-done(((bf16[192,1536]{1,0:T(8,128)(2,1)}), bf16[1536,1536]{1,0:T(8,128)(2,1)}) %all-gather.12.cloned.1.call-update) | async-done | bytes 4718608 | tf_op jit(solution)/shard_map/all_gather | solution.py:88
  188.7 70.1 %all-gather.14.cloned.1.call-done = bf16[1536,1536]{1,0:T(8,128)(2,1)} async-done(((bf16[192,1536]{1,0:T(8,128)(2,1)}), bf16[1536,1536]{1,0:T(8,128)(2,1)}) %all-gather.14.cloned.1.call-update) | async-done | bytes 4718608 | tf_op jit(solution)/shard_map/all_gather | solution.py:91
  264.8 75.5 %all_to_all.20 = bf16[4,5,104,1536]{3,2,1,0:T(8,128)(2,1)} all-to-all(bf16[4,5,104,1536]{3,2,1,0:T(8,128)(2,1)S(1)} %bitcast.174), channel_id=1, replica_groups=mesh['expert'=4,'shard'=8] {'expert'}, dimensions={0} | all-to-all | bytes 12779520 | tf_op jit(solution)/shard_map/all_to_all | solution.py:157
  340.3 132.2 %all-gather.16.cloned.1.call-done = bf16[1536,5,1024]{2,0,1:T(8,128)(2,1)} async-done(((bf16[192,5,1024]{2,0,1:T(8,128)(2,1)}), bf16[1536,5,1024]{2,0,1:T(8,128)(2,1)}) %all-gather.16.cloned.1.call-update) | async-done | bytes 15728656 | tf_op jit(solution)/shard_map/all_gather | solution.py:96
  472.5 12.1 fusion.26
  490.8 100.0 %all-gather.18.cloned.1.call-done = bf16[1536,5,512]{2,0,1:T(8,128)(2,1)} async-done(((bf16[192,5,512]{2,0,1:T(8,128)(2,1)}), bf16[1536,5,512]{2,0,1:T(8,128)(2,1)}) %all-gather.18.cloned.1.call-update) | async-done | bytes 7864336 | tf_op jit(solution)/shard_map/all_gather | solution.py:97
  590.9 10.0 convert_bitcast_fusion.1
  600.9 6.1 copy.89
  612.3 27.8 %all-gather = bf16[8,192,20]{1,2,0:T(8,128)(2,1)S(1)} all-gather(bf16[1,192,20]{1,2,0:T(8,128)(2,1)S(1)} %bitcast.202), channel_id=1, replica_groups=mesh['expert'=4,'shard'=8] {'shard'}, dimensions={0}, use_global_device_ids=true | all-gather | bytes 69120 | tf_op jit(solution)/shard_map/all_gather | solution.py:93
  640.5 43.5 %all-to-all-done.1 = bf16[4,5,104,1536]{3,2,1,0:T(8,128)(2,1)} async-done(((bf16[4,5,104,1536]{3,2,1,0:T(8,128)(2,1)}), bf16[4,5,104,1536]{3,2,1,0:T(8,128)(2,1)}, u32[]{:S(2)}, u32[]{:S(2)}) %all-to-all-start.1) | async-done | bytes 6389792 | tf_op jit(solution)/shard_map/all_to_all | solution.py:163
  692.4 75.7 %all_to_all.21 = bf16[4,5,104,1536]{3,2,1,0:T(8,128)(2,1)} all-to-all(bf16[4,5,104,1536]{3,2,1,0:T(8,128)(2,1)S(1)} %bitcast.180), channel_id=1, replica_groups=mesh['expert'=4,'shard'=8] {'expert'}, dimensions={0} | all-to-all | bytes 12779520 | tf_op jit(solution)/shard_map/all_to_all | solution.py:177
  768.1 14.0 fusion.23
  782.0 13.4 convert_bitcast_fusion
  795.4 6.0 copy.91
  806.9 71.5 %all-to-all-done.3 = bf16[4,5,104,1536]{3,2,1,0:T(8,128)(2,1)} async-done(((bf16[4,5,104,1536]{3,2,1,0:T(8,128)(2,1)}), bf16[4,5,104,1536]{3,2,1,0:T(8,128)(2,1)}, u32[]{:S(2)}, u32[]{:S(2)}) %all-to-all-start.3) | async-done | bytes 6389792 | tf_op jit(solution)/shard_map/all_to_all | solution.py:205
  927.7 36.9 %reduce-scatter.18.cloned.1.call-done = bf16[192,512]{1,0:T(8,128)(2,1)} async-done(((bf16[1536,512]{1,0:T(8,128)(2,1)}), bf16[192,512]{1,0:T(8,128)(2,1)}) %reduce-scatter.18.cloned.1.call-update) | async-done | bytes 196624 | tf_op jit(solution)/shard_map/reduce_scatter | solution.py:269
  964.6 68.3 %reduce-scatter.16.cloned.1.call-done = bf16[192,512]{1,0:T(8,128)(2,1)} async-done(((bf16[1536,512]{1,0:T(8,128)(2,1)}), bf16[192,512]{1,0:T(8,128)(2,1)}) %reduce-scatter.16.cloned.1.call-update) | async-done | bytes 196624 | tf_op jit(solution)/shard_map/reduce_scatter | solution.py:266
  1032.9 98.9 %reduce-scatter.20.cloned.1.call-done = bf16[192,1536]{1,0:T(8,128)(2,1)} async-done(((bf16[1536,1536]{1,0:T(8,128)(2,1)}), bf16[192,1536]{1,0:T(8,128)(2,1)}) %reduce-scatter.20.cloned.1.call-update) | async-done | bytes 589840 | tf_op jit(solution)/shard_map/reduce_scatter | solution.py:272
  1131.8 98.8 %reduce-scatter.14.cloned.1.call-done = bf16[192,1536]{1,0:T(8,128)(2,1)} async-done(((bf16[1536,1536]{1,0:T(8,128)(2,1)}), bf16[192,1536]{1,0:T(8,128)(2,1)}) %reduce-scatter.14.cloned.1.call-update) | async-done | bytes 589840 | tf_op jit(solution)/shard_map/reduce_scatter | solution.py:263
  1230.7 10.8 bitcast_convert_fusion.1
  1241.5 10.7 copy.126
  1252.5 15.1 bitcast_convert_fusion
  1267.6 20.8 %copy.124 = bf16[1536,5120]{1,0:T(8,128)(2,1)} copy(bf16[1536,5120]{0,1:T(8,128)(2,1)} %bitcast.175) | data formatting | bytes 31457280
  1289.2 6.3 fusion.36
  1304.4 15.3 all-reduce.4
  1319.9 10.7 all-reduce.6
  1335.3 5.4 all-reduce.10.cloned.1.call-done
  1347.6 136.1 %reduce-scatter.26.cloned.1.call-done = bf16[192,2560]{1,0:T(8,128)(2,1)} async-done(((bf16[1536,2560]{1,0:T(8,128)(2,1)}), bf16[192,2560]{1,0:T(8,128)(2,1)}) %reduce-scatter.26.cloned.1.call-update) | async-done | bytes 983056
  1486.9 249.8 %reduce-scatter.24.cloned.1.call-done = bf16[192,5120]{1,0:T(8,128)(2,1)} async-done(((bf16[1536,5120]{1,0:T(8,128)(2,1)}), bf16[192,5120]{1,0:T(8,128)(2,1)}) %reduce-scatter.24.cloned.1.call-update) | async-done | bytes 1966096
  (196 shorter events, 130.5 us)
Async XLA Ops:
  7.2 47.8 %all-gather.8.cloned.1.call-start = ((), (), s32[]{:S(2)}) async-start(), calls=%async_computation.11 | async-start | bytes 1769472 | tf_op jit(solution)/shard_map/all_gather | solution.py:90
  7.9 91.8 %all-gather.10.cloned.1.call-start = ((), (), s32[]{:S(2)}) async-start(), calls=%async_computation.12 | async-start | bytes 1769472 | tf_op jit(solution)/shard_map/all_gather | solution.py:89
  8.7 20.5 %copy-start.23 = (s32[256,8]{0,1:T(8,128)S(1)}, s32[256,8]{0,1:T(8,128)}, u32[]{:S(2)}) copy-start(s32[256,8]{0,1:T(8,128)} %param.15) | copy-start | bytes 24580
  8.7 20.6 %copy-start.1 = (bf16[256,1536]{1,0:T(8,128)(2,1)S(1)}, bf16[256,1536]{1,0:T(8,128)(2,1)}, u32[]{:S(2)}) copy-start(bf16[256,1536]{1,0:T(8,128)(2,1)} %param.13) | copy-start | bytes 2359300
  8.7 170.4 %all-gather.12.cloned.1.call-start = ((), (), s32[]{:S(2)}) async-start(), calls=%async_computation.13 | async-start | bytes 5308416 | tf_op jit(solution)/shard_map/all_gather | solution.py:88
  9.4 249.4 %all-gather.14.cloned.1.call-start = ((), (), s32[]{:S(2)}) async-start(), calls=%async_computation.14 | async-start | bytes 5308416 | tf_op jit(solution)/shard_map/all_gather | solution.py:91
  10.0 462.5 %all-gather.16.cloned.1.call-start = ((), (), s32[]{:S(2)}) async-start(), calls=%async_computation.15 | async-start | bytes 17694720 | tf_op jit(solution)/shard_map/all_gather | solution.py:96
  10.6 580.2 %all-gather.18.cloned.1.call-start = ((), (), s32[]{:S(2)}) async-start(), calls=%async_computation.16 | async-start | bytes 8847360 | tf_op jit(solution)/shard_map/all_gather | solution.py:97
  11.9 672.2 %copy-start.36 = (f32[256]{0:T(256)}, f32[256]{0:T(256)S(1)}, u32[]{:S(2)}) copy-start(f32[256]{0:T(256)S(1)} %fusion.100) | copy-start | bytes 3076
  29.5 891.7 %copy-start.24 = (f32[256]{0:T(256)}, f32[256]{0:T(256)S(1)}, u32[]{:S(2)}) copy-start(f32[256]{0:T(256)S(1)} %add_rsqrt_fusion.1) | copy-start | bytes 3076
  29.6 848.8 %copy-start.26 = (bf16[20,256]{1,0:T(8,128)(2,1)}, bf16[20,256]{1,0:T(8,128)(2,1)S(1)}, u32[]{:S(2)}) copy-start(bf16[20,256]{1,0:T(8,128)(2,1)S(1)} %multiply_bitcast_fusion) | copy-start | bytes 30724
  29.7 848.7 %copy-start.28 = (f32[20,256]{1,0:T(8,128)}, f32[20,256]{1,0:T(8,128)S(1)}, u32[]{:S(2)}) copy-start(f32[20,256]{1,0:T(8,128)S(1)} %fusion.83) | copy-start | bytes 61444
  57.1 128.9 %copy-start.15 = (bf16[256,512]{0,1:T(8,128)(2,1)}, bf16[256,512]{0,1:T(8,128)(2,1)S(1)}, u32[]{:S(2)}) copy-start(bf16[256,512]{0,1:T(8,128)(2,1)S(1)} %copy.83) | copy-start | bytes 786436
  102.0 81.7 %copy-start.19 = (bf16[256,8,32]{0,2,1:T(8,128)(2,1)}, bf16[256,8,32]{0,2,1:T(8,128)(2,1)S(1)}, u32[]{:S(2)}) copy-start(bf16[256,8,32]{0,2,1:T(8,128)(2,1)S(1)} %get-tuple-element.82) | copy-start | bytes 393220
  102.0 81.7 %copy-start.20 = (bf16[256,8,32]{0,2,1:T(8,128)(2,1)}, bf16[256,8,32]{0,2,1:T(8,128)(2,1)S(1)}, u32[]{:S(2)}) copy-start(bf16[256,8,32]{0,2,1:T(8,128)(2,1)S(1)} %get-tuple-element.83) | copy-start | bytes 393220
  188.7 74.0 %copy-start.17 = (bf16[8,64,3,256]{3,1,2,0:T(8,128)(2,1)}, bf16[8,64,3,256]{3,1,2,0:T(8,128)(2,1)S(1)}, u32[]{:S(2)}) copy-start(bf16[8,64,3,256]{3,1,2,0:T(8,128)(2,1)S(1)} %fusion.51) | copy-start | bytes 2359300
  262.8 620.5 %copy-start.3 = (f32[256,1536]{1,0:T(8,128)}, f32[256,1536]{1,0:T(8,128)S(1)}, u32[]{:S(2)}) copy-start(f32[256,1536]{1,0:T(8,128)S(1)} %get-tuple-element.93) | copy-start | bytes 4718596
  606.9 5.4 copy-start.35
  606.9 77.1 %all-to-all-start.1 = ((bf16[4,5,104,1536]{3,2,1,0:T(8,128)(2,1)}), bf16[4,5,104,1536]{3,2,1,0:T(8,128)(2,1)}, u32[]{:S(2)}, u32[]{:S(2)}) async-start(bf16[4,5,104,1536]{3,2,1,0:T(8,128)(2,1)} %copy.89), calls=%async_computation.1 | async-start | bytes 12779520 | tf_op jit(solution)/shard_map/all_to_all | solution.py:163
  689.3 194.0 %copy-start.21 = (bf16[256,20]{0,1:T(8,128)(2,1)}, bf16[256,20]{0,1:T(8,128)(2,1)S(1)}, u32[]{:S(2)}) copy-start(bf16[256,20]{0,1:T(8,128)(2,1)S(1)} %get-tuple-element.59) | copy-start | bytes 30724
  801.4 77.0 %all-to-all-start.3 = ((bf16[4,5,104,1536]{3,2,1,0:T(8,128)(2,1)}), bf16[4,5,104,1536]{3,2,1,0:T(8,128)(2,1)}, u32[]{:S(2)}, u32[]{:S(2)}) async-start(bf16[4,5,104,1536]{3,2,1,0:T(8,128)(2,1)} %copy.91), calls=%async_computation.3 | async-start | bytes 12779520 | tf_op jit(solution)/shard_map/all_to_all | solution.py:205
  806.7 157.9 %reduce-scatter.18.cloned.1.call-start = ((), (), s32[]{:S(2)}) async-start(), calls=%async_computation.19 | async-start | bytes 1769472 | tf_op jit(solution)/shard_map/reduce_scatter | solution.py:269
  878.4 4.9 copy-start.34
  899.5 133.4 %reduce-scatter.16.cloned.1.call-start = ((), (), s32[]{:S(2)}) async-start(), calls=%async_computation.18 | async-start | bytes 1769472 | tf_op jit(solution)/shard_map/reduce_scatter | solution.py:266
  913.0 218.8 %reduce-scatter.20.cloned.1.call-start = ((), (), s32[]{:S(2)}) async-start(), calls=%async_computation.20 | async-start | bytes 5308416 | tf_op jit(solution)/shard_map/reduce_scatter | solution.py:272
  917.8 312.8 %reduce-scatter.14.cloned.1.call-start = ((), (), s32[]{:S(2)}) async-start(), calls=%async_computation.17 | async-start | bytes 5308416 | tf_op jit(solution)/shard_map/reduce_scatter | solution.py:263
  925.8 370.4 %reduce-scatter.22.cloned.1.call-start = ((), (), s32[]{:S(2)}) async-start(), calls=%async_computation.21 | async-start | bytes 442368
  927.7 413.0 %all-reduce.10.cloned.1.call-start = ((), (), s32[]{:S(2)}) async-start(), calls=%async_computation.24 | async-start | bytes 3145728 | tf_op jit(solution)/shard_map/psum | solution.py:284
  1230.7 253.0 %reduce-scatter.26.cloned.1.call-start = ((), (), s32[]{:S(2)}) async-start(), calls=%async_computation.23 | async-start | bytes 8847360
  1252.2 484.5 %reduce-scatter.24.cloned.1.call-start = ((), (), s32[]{:S(2)}) async-start(), calls=%async_computation.22 | async-start | bytes 17694720
  1289.1 7.9 copy-start.6
  1340.7 5.7 copy-start.18
  (25 other events, 56.5 us)
Sparse Core Ops, SparseCore 0:
  10.2 44.7 all-gather.7
  57.2 42.5 all-gather.9
  101.9 77.1 all-gather.11
  181.2 77.6 all-gather.13
  260.9 211.5 all-gather.15
  474.5 116.2 all-gather.17
  899.6 64.9 reduce-scatter.17
  968.6 64.3 reduce-scatter.15
  1036.6 95.1 reduce-scatter.19
  1135.3 95.3 reduce-scatter.13
  1234.5 61.6 reduce-scatter.21
  1298.6 42.1 all-reduce.9
  1344.4 139.2 reduce-scatter.25
  1487.1 249.4 reduce-scatter.23
where the time goes:
time: 1760 us; the launch traced here: 1750 us
  waiting for transfers between devices  1260 us (72%)
  blocking collectives  220 us (12%)
  matrix products  149 us (8%)
  local copies, waits for them, and re-layouts  66.5 us (4%)
  other arithmetic  24 us (1%)
    unnamed x17, waiting for transfers between devices  390 us
    dot_general x33, matrix products, product(): return jnp.einsum(form, left, right, preferred_element_type=jnp.float32)  149 us
    all_gather x1, waiting for transfers between devices, on_device(): lax.all_gather(gate_up_weight, 'shard', axis=0, tiled=True)  132 us
    all_gather x1, waiting for transfers between devices, on_device(): lax.all_gather(down_weight, 'shard', axis=0, tiled=True)  100 us
    reduce_scatter x1, waiting for transfers between devices, on_device(): lax.psum_scatter(output_term.astype(jnp.bfloat16), 'shard', scatter_dimen...  98.9 us
    reduce_scatter x1, waiting for transfers between devices, on_device(): lax.psum_scatter(query_term.astype(jnp.bfloat16), 'shard', scatter_dimens...  98.8 us
    all_gather x1, waiting for transfers between devices, on_device(): lax.all_gather(query_weight, 'shard', axis=0, tiled=True)  77.1 us
    all_to_all x1, blocking collectives, on_device(): lax.all_to_all(grad_rows, 'expert', split_axis=0, concat_axis=0, tiled=True)  75.7 us
  transfers between devices with their start and end apart: 16, of which 16 were waited for; matrix products, arithmetic and copies ran while one was open for 8% of the time, Pallas kernels for 0%

commit v1 on v0

--- a/solution.py
+++ b/solution.py
@@ -1,9 +1,15 @@
+import functools
+import itertools
+
 import jax
 import jax.numpy as jnp
 from jax import lax
+from jax.experimental import pallas as pl
+from jax.experimental.pallas import tpu as pltpu
 from jax.sharding import PartitionSpec as P
 
 HEAD_DIM = 64
+EXPERT, SHARD = "expert", "shard"
 
 
 norm_eps = 1e-06
@@ -78,23 +84,23 @@
     experts_all = router_weight.shape[1]
     local_experts = gate_up_weight.shape[1]
     inner_width = down_weight.shape[2]
-    owners = lax.axis_size("expert")
+    owners = lax.axis_size(EXPERT)
     slot_count = 8 * max(
         seq_len // 32, (seq_len * route_width + 8 * experts_all - 1) // (8 * experts_all)
     )
     score_factor = HEAD_DIM ** (-0.5)
     gain_one, query_full, key_complete, value_complete, output_full, gain_two, router_full = (
-        lax.all_gather(first_gain, "shard", axis=0, tiled=True),
-        lax.all_gather(query_weight, "shard", axis=0, tiled=True),
-        lax.all_gather(key_matrix, "shard", axis=0, tiled=True),
-        lax.all_gather(value_matrix, "shard", axis=0, tiled=True),
-        lax.all_gather(output_weight, "shard", axis=0, tiled=True),
-        lax.all_gather(second_gain, "shard", axis=0, tiled=True),
-        lax.all_gather(router_weight, "shard", axis=0, tiled=True),
+        lax.all_gather(first_gain, SHARD, axis=0, tiled=True),
+        lax.all_gather(query_weight, SHARD, axis=0, tiled=True),
+        lax.all_gather(key_matrix, SHARD, axis=0, tiled=True),
+        lax.all_gather(value_matrix, SHARD, axis=0, tiled=True),
+        lax.all_gather(output_weight, SHARD, axis=0, tiled=True),
+        lax.all_gather(second_gain, SHARD, axis=0, tiled=True),
+        lax.all_gather(router_weight, SHARD, axis=0, tiled=True),
     )
     gate_up_full, down_full = (
-        lax.all_gather(gate_up_weight, "shard", axis=0, tiled=True),
-        lax.all_gather(down_weight, "shard", axis=0, tiled=True),
+        lax.all_gather(gate_up_weight, SHARD, axis=0, tiled=True),
+        lax.all_gather(down_weight, SHARD, axis=0, tiled=True),
     )
     gain_one = gain_one.astype(jnp.float32)
     gain_two = gain_two.astype(jnp.float32)
@@ -154,13 +160,13 @@
         .astype(jnp.bfloat16)
         .reshape(owners, local_experts, slot_count, model_width)
     )
-    row_block = lax.all_to_all(outgoing, "expert", split_axis=0, concat_axis=0, tiled=True)
+    row_block = lax.all_to_all(outgoing, EXPERT, split_axis=0, concat_axis=0, tiled=True)
     both_pre = product("oemd,def->oemf", row_block, gate_up_full)
     active = (jax.nn.silu(both_pre[..., :inner_width]) * both_pre[..., inner_width:]).astype(
         jnp.bfloat16
     )
     answer = product("oemf,def->oemd", active, down_full).astype(jnp.bfloat16)
-    returned = lax.all_to_all(answer, "expert", split_axis=0, concat_axis=0, tiled=True).reshape(
+    returned = lax.all_to_all(answer, EXPERT, split_axis=0, concat_axis=0, tiled=True).reshape(
         experts_all, slot_count, model_width
     )
     gate_full = product("ske,sk->se", chosen.astype(jnp.bfloat16), gate_soft.astype(jnp.bfloat16))
@@ -174,7 +180,7 @@
         .astype(jnp.bfloat16)
         .reshape(owners, local_experts, slot_count, model_width)
     )
-    incoming = lax.all_to_all(grad_rows, "expert", split_axis=0, concat_axis=0, tiled=True)
+    incoming = lax.all_to_all(grad_rows, EXPERT, split_axis=0, concat_axis=0, tiled=True)
     answer_dot = product("emd,sd->ems", returned, dout_low)
     gate_grad_full = jnp.sum(placing_float * answer_dot, axis=1)
     gate_grad = jnp.sum(chosen * gate_grad_full.T[:, None, :], axis=-1)
@@ -183,8 +189,8 @@
     logits_grad = jnp.sum(chosen * picked_grad[:, :, None], axis=1).astype(jnp.bfloat16)
     router_term = product("sd,se->de", second_normed, logits_grad)
     gate_up_full, down_full = (
-        lax.all_gather(gate_up_weight, "shard", axis=0, tiled=True),
-        lax.all_gather(down_weight, "shard", axis=0, tiled=True),
+        lax.all_gather(gate_up_weight, SHARD, axis=0, tiled=True),
+        lax.all_gather(down_weight, SHARD, axis=0, tiled=True),
     )
     gate_part = both_pre[..., :inner_width]
     up_part = both_pre[..., inner_width:]
@@ -202,15 +208,15 @@
     row_grad = product("oemf,def->oemd", both_grad, gate_up_full).astype(jnp.bfloat16)
     gate_up_term = product("oemd,oemf->def", row_block, both_grad)
     down_term = product("oemd,oemf->def", incoming, active_again)
-    back_rows = lax.all_to_all(row_grad, "expert", split_axis=0, concat_axis=0, tiled=True).reshape(
+    back_rows = lax.all_to_all(row_grad, EXPERT, split_axis=0, concat_axis=0, tiled=True).reshape(
         experts_all, slot_count, model_width
     )
     gate_up_total, down_total = (
         lax.psum_scatter(
-            gate_up_term.astype(jnp.bfloat16), "shard", scatter_dimension=0, tiled=True
+            gate_up_term.astype(jnp.bfloat16), SHARD, scatter_dimension=0, tiled=True
         ).astype(jnp.float32),
         lax.psum_scatter(
-            down_term.astype(jnp.bfloat16), "shard", scatter_dimension=0, tiled=True
+            down_term.astype(jnp.bfloat16), SHARD, scatter_dimension=0, tiled=True
         ).astype(jnp.float32),
     )
     normed_grad = product("ems,emd->sd", placing, back_rows) + product(
@@ -258,35 +264,35 @@
     tokens_grad = tokens_grad + hidden_grad
     mixer_sums = (
         lax.psum_scatter(
-            first_gain_term.astype(jnp.bfloat16), "shard", scatter_dimension=0, tiled=True
+            first_gain_term.astype(jnp.bfloat16), SHARD, scatter_dimension=0, tiled=True
         ).astype(jnp.float32),
         lax.psum_scatter(
-            query_term.astype(jnp.bfloat16), "shard", scatter_dimension=0, tiled=True
+            query_term.astype(jnp.bfloat16), SHARD, scatter_dimension=0, tiled=True
         ).astype(jnp.float32),
         lax.psum_scatter(
-            key_term.astype(jnp.bfloat16), "shard", scatter_dimension=0, tiled=True
+            key_term.astype(jnp.bfloat16), SHARD, scatter_dimension=0, tiled=True
         ).astype(jnp.float32),
         lax.psum_scatter(
-            value_term.astype(jnp.bfloat16), "shard", scatter_dimension=0, tiled=True
+            value_term.astype(jnp.bfloat16), SHARD, scatter_dimension=0, tiled=True
         ).astype(jnp.float32),
         lax.psum_scatter(
-            output_term.astype(jnp.bfloat16), "shard", scatter_dimension=0, tiled=True
+            output_term.astype(jnp.bfloat16), SHARD, scatter_dimension=0, tiled=True
         ).astype(jnp.float32),
         lax.psum_scatter(
-            second_gain_term.astype(jnp.bfloat16), "shard", scatter_dimension=0, tiled=True
+            second_gain_term.astype(jnp.bfloat16), SHARD, scatter_dimension=0, tiled=True
         ).astype(jnp.float32),
         lax.psum_scatter(
-            router_term.astype(jnp.bfloat16), "shard", scatter_dimension=0, tiled=True
+            router_term.astype(jnp.bfloat16), SHARD, scatter_dimension=0, tiled=True
         ).astype(jnp.float32),
     )
     mixer_sums = (
-        lax.psum(mixer_sums[0].astype(jnp.bfloat16), "expert").astype(jnp.float32),
-        lax.psum(mixer_sums[1].astype(jnp.bfloat16), "expert").astype(jnp.float32),
-        lax.psum(mixer_sums[2].astype(jnp.bfloat16), "expert").astype(jnp.float32),
-        lax.psum(mixer_sums[3].astype(jnp.bfloat16), "expert").astype(jnp.float32),
-        lax.psum(mixer_sums[4].astype(jnp.bfloat16), "expert").astype(jnp.float32),
-        lax.psum(mixer_sums[5].astype(jnp.bfloat16), "expert").astype(jnp.float32),
-        lax.psum(mixer_sums[6].astype(jnp.bfloat16), "expert").astype(jnp.float32),
+        lax.psum(mixer_sums[0].astype(jnp.bfloat16), EXPERT).astype(jnp.float32),
+        lax.psum(mixer_sums[1].astype(jnp.bfloat16), EXPERT).astype(jnp.float32),
+        lax.psum(mixer_sums[2].astype(jnp.bfloat16), EXPERT).astype(jnp.float32),
+        lax.psum(mixer_sums[3].astype(jnp.bfloat16), EXPERT).astype(jnp.float32),
+        lax.psum(mixer_sums[4].astype(jnp.bfloat16), EXPERT).astype(jnp.float32),
+        lax.psum(mixer_sums[5].astype(jnp.bfloat16), EXPERT).astype(jnp.float32),
+        lax.psum(mixer_sums[6].astype(jnp.bfloat16), EXPERT).astype(jnp.float32),
     )
     return (
         output,
@@ -303,38 +309,993 @@
     )
 
 
+MESH_IDS = pl.DeviceIdType.MESH
+
+
+class Place:
+    def __init__(self):
+        e, s = lax.axis_index(EXPERT), lax.axis_index(SHARD)
+        self.y, self.c = lax.div(e, 2), lax.rem(e, 2)
+        self.z, self.x = lax.div(s, 2), lax.rem(s, 2)
+        self.ox, self.oy, self.oc = 1 - self.x, 1 - self.y, 1 - self.c
+        self.to_x = (e, s + 1 - 2 * self.x)
+        self.to_y = (e + 2 - 4 * self.y, s)
+        self.to_c = (e + 1 - 2 * self.c, s)
+        z = self.z
+        self.zs = (z, z + 1 - 2 * lax.rem(z, 2), lax.rem(z + 2, 4), 3 - z)
+        self.to_z = [None] + [(e, self.zs[d] * 2 + self.x) for d in (1, 2, 3)]
+
+
+class Sender:
+    def __init__(self, send_sem, recv_sem):
+        self.send_sem, self.recv_sem, self.started = send_sem, recv_sem, []
+
+    def __call__(self, source, target, device):
+        number = len(self.started)
+        assert number < self.send_sem.shape[0]
+        copy = pltpu.make_async_remote_copy(
+            src_ref=source,
+            dst_ref=target,
+            send_sem=self.send_sem.at[number],
+            recv_sem=self.recv_sem.at[number],
+            device_id=device,
+            device_id_type=MESH_IDS,
+        )
+        copy.start()
+        self.started.append(copy)
+        return copy
+
+    def finish(self):
+        for copy in self.started:
+            copy.wait_send()
+
+
+def greet(devices):
+    barrier = pltpu.get_barrier_semaphore()
+    for device in devices:
+        pl.semaphore_signal(barrier, inc=1, device_id=device, device_id_type=MESH_IDS)
+    pl.semaphore_wait(barrier, len(devices))
+
+
+def gather_in_plane(place, send, items, beside=lambda: None):
+    x, y, c = place.x, place.y, place.c
+    ox, oy = place.ox, place.oy
+    first = []
+    for view, source, ready, own in items:
+        for copy in ready:
+            copy.wait_recv()
+        block = source(y, None)
+        by_x = send(block, view(x, y, c, None), place.to_x)
+        by_y, back = None, None
+        if own:
+            back = send(source(oy, 1), view(x, oy, c, 1), place.to_x)
+        else:
+            by_y = send(block, view(x, y, c, None), place.to_y)
+        first.append((by_x, by_y, back))
+    result = beside()
+    landed = []
+    for (view, source, ready, own), (by_x, by_y, back) in zip(items, first):
+        if not own:
+            landed.append(send(source(y, None), view(x, y, c, None), place.to_c))
+        by_x.wait_recv()
+        over_y = send(view(ox, y, c, 0), view(ox, y, c, 0), place.to_y)
+        landed.append(send(view(ox, y, c, None), view(ox, y, c, None), place.to_c))
+        if not own:
+            by_y.wait_recv()
+            back = send(view(x, oy, c, 1), view(x, oy, c, 1), place.to_x)
+            landed.append(send(view(x, oy, c, None), view(x, oy, c, None), place.to_c))
+        landed.append((view, over_y, back))
+    final = []
+    for entry in landed:
+        if isinstance(entry, tuple):
+            view, over_y, back = entry
+            over_y.wait_recv()
+            back.wait_recv()
+            final.append(send(view(ox, oy, c, None), view(ox, oy, c, None), place.to_c))
+        else:
+            final.append(entry)
+    for copy in final:
+        copy.wait_recv()
+    return result
+
+
+def half_rows(half, rows):
+    return pl.ds(0, rows) if half is None else pl.ds(half * (rows // 2), rows // 2)
+
+
+def halves_kernel(first, count, *refs):
+    up_ref, down_ref = refs[:2]
+    outs, (send_sem, recv_sem, copy_sem) = refs[2 : 2 + count], refs[2 + count :]
+    place = Place()
+    send = Sender(send_sem, recv_sem)
+    greet([place.to_x])
+    sent, local = start_halves(place, send, copy_sem, up_ref, down_ref, outs, first)
+    for copy in sent:
+        copy.wait_recv()
+    for copy in local:
+        copy.wait()
+    send.finish()
+
+
+def start_halves(place, send, copy_sem, up_ref, down_ref, outs, first):
+    x, ox = place.x, place.ox
+    half = down_ref.shape[2] // 2
+    sent, local = [], []
+    for number, out in enumerate(outs):
+        expert = first + number
+
+        def pieces(xx):
+            at = pl.ds(pl.multiple_of(xx * half, half), half)
+            later = pl.ds(pl.multiple_of((xx + 2) * half, half), half)
+            return (up_ref.at[expert, :, at], up_ref.at[expert, :, later], down_ref.at[expert, :, at])
+
+        for index, piece in enumerate(pieces(ox)):
+            sent.append(send(piece, out.at[x, :, index * half : (index + 1) * half], place.to_x))
+        for index, piece in enumerate(pieces(x)):
+            copy = pltpu.make_async_copy(
+                piece, out.at[x, :, index * half : (index + 1) * half], copy_sem.at[3 * number + index]
+            )
+            copy.start()
+            local.append(copy)
+    return sent, local
+
+
+def exchange_halves(up, down, count):
+    depth, inner = down.shape[1:]
+    return pl.pallas_call(
+        functools.partial(halves_kernel, 0, count),
+        out_shape=(jax.ShapeDtypeStruct((2, depth, 3 * inner // 2), up.dtype),) * count,
+        in_specs=[pl.BlockSpec(memory_space=pltpu.VMEM)] * 2,
+        out_specs=(pl.BlockSpec(memory_space=pl.ANY),) * count,
+        scratch_shapes=[pltpu.SemaphoreType.DMA((3 * count,))] * 3,
+        compiler_params=pltpu.CompilerParams(collective_id=4, has_side_effects=True),
+        cost_estimate=pl.CostEstimate(flops=0, bytes_accessed=40_000_000, transcendentals=0),
+        name="exchange_halves",
+    )(up, down)
+
+
+def weights_kernel(
+    first, count, up_ref, down_ref, w_ref, o_ref, small_ref, rows_ref, w_out, o_out, small_out, rows_out, *refs
+):
+    outs, (send_sem, recv_sem, copy_sem, half_sem) = refs[:count], refs[count:]
+    place = Place()
+    send = Sender(send_sem, recv_sem)
+    x, y, c, z = place.x, place.y, place.c, place.z
+    depth = w_ref.shape[0]
+    piece = depth // 4
+    blocks = rows_ref.shape[0]
+    greet([place.to_x, place.to_y, place.to_c] + place.to_z[1:])
+
+    def columns(ref, yy, cc):
+        part = ref.shape[1] // 4
+        return pl.ds(pl.multiple_of((yy * 2 + cc) * part, part), part)
+
+    def pieces(yy, cc, half):
+        start = (yy * 2 + cc) * piece
+        if half is None:
+            return pl.ds(pl.multiple_of(start, piece), piece)
+        return pl.ds(pl.multiple_of(start + half * (piece // 2), piece // 2), piece // 2)
+
+    wide = [(w_ref, w_out), (o_ref, o_out)]
+    from_z = {}
+    for d in (1, 2, 3):
+        from_z[d] = [
+            send(ref.at[:, columns(ref, y, c)], out.at[z, x, :, columns(ref, y, c)], place.to_z[d])
+            for ref, out in wide
+        ] + [send(small_ref.at[pieces(y, c, None)], small_out.at[z, x, pieces(y, c, None)], place.to_z[d])]
+    local = [
+        pltpu.make_async_copy(w_ref, w_out.at[z, x], copy_sem.at[0]),
+        pltpu.make_async_copy(o_ref, o_out.at[z, x], copy_sem.at[1]),
+        pltpu.make_async_copy(small_ref, small_out.at[z, x], copy_sem.at[2]),
+        pltpu.make_async_copy(rows_ref, rows_out.at[c, x, y], copy_sem.at[3]),
+    ]
+    for copy in local:
+        copy.start()
+
+    def wide_view(ref, out, zz):
+        return lambda xx, yy, cc, half: out.at[zz, xx, half_rows(half, depth), columns(ref, yy, cc)]
+
+    def small_view(zz):
+        return lambda xx, yy, cc, half: small_out.at[zz, xx, pieces(yy, cc, half)]
+
+    def rows_view(xx, yy, cc, half):
+        return rows_out.at[cc, xx, yy, half_rows(half, blocks)]
+
+    items = [
+        (
+            wide_view(ref, out, z),
+            lambda yy, half, ref=ref: ref.at[half_rows(half, depth), columns(ref, yy, c)],
+            [],
+            True,
+        )
+        for ref, out in wide
+    ]
+    items.append((small_view(z), lambda yy, half: small_ref.at[pieces(yy, c, half)], [], True))
+    for d in (1, 2, 3):
+        zz = place.zs[d]
+        views = [wide_view(ref, out, zz) for ref, out in wide] + [small_view(zz)]
+        for view, copy in zip(views, from_z[d]):
+            items.append((view, lambda yy, half, view=view: view(x, yy, c, half), [copy], False))
+    items.append((rows_view, lambda yy, half: rows_ref.at[half_rows(half, blocks)], [], False))
+    sent, kept = gather_in_plane(
+        place, send, items, lambda: start_halves(place, send, half_sem, up_ref, down_ref, outs, first)
+    )
+    for copy in sent:
+        copy.wait_recv()
+    for copy in local + kept:
+        copy.wait()
+    send.finish()
+
+
+def gather_weights(w, o, small, rows, up, down, first):
+    depth, inner = down.shape[1:]
+    count = up.shape[0] - first
+    copies = 128
+    arrays = (w, o, small)
+    return pl.pallas_call(
+        functools.partial(weights_kernel, first, count),
+        out_shape=tuple(jax.ShapeDtypeStruct((4, 2) + a.shape, a.dtype) for a in arrays)
+        + (jax.ShapeDtypeStruct((2, 2, 2) + rows.shape, rows.dtype),)
+        + (jax.ShapeDtypeStruct((2, depth, 3 * inner // 2), up.dtype),) * count,
+        in_specs=[pl.BlockSpec(memory_space=pltpu.VMEM)] * 6,
+        out_specs=(pl.BlockSpec(memory_space=pl.ANY),) * (4 + count),
+        scratch_shapes=[
+            pltpu.SemaphoreType.DMA((copies,)),
+            pltpu.SemaphoreType.DMA((copies,)),
+            pltpu.SemaphoreType.DMA((4,)),
+            pltpu.SemaphoreType.DMA((3 * count,)),
+        ],
+        compiler_params=pltpu.CompilerParams(collective_id=0, has_side_effects=True),
+        cost_estimate=pl.CostEstimate(flops=0, bytes_accessed=200_000_000, transcendentals=0),
+        name="gather_weights",
+    )(up, down, w, o, small, rows)
+
+
+def rows_kernel(a_ref, b_ref, a_out, b_out, send_sem, recv_sem, copy_sem):
+    place = Place()
+    send = Sender(send_sem, recv_sem)
+    x, y, c = place.x, place.y, place.c
+    rows = a_ref.shape[0]
+    greet([place.to_x, place.to_y, place.to_c])
+    local = [
+        pltpu.make_async_copy(a_ref, a_out.at[c, x, y], copy_sem.at[0]),
+        pltpu.make_async_copy(b_ref, b_out.at[c, x, y], copy_sem.at[1]),
+    ]
+    for copy in local:
+        copy.start()
+
+    def item(source, out):
+        return (
+            lambda xx, yy, cc, half: out.at[cc, xx, yy, half_rows(half, rows)],
+            lambda yy, half: source.at[half_rows(half, rows)],
+            [],
+            False,
+        )
+
+    gather_in_plane(place, send, [item(b_ref, b_out), item(a_ref, a_out)])
+    for copy in local:
+        copy.wait()
+    send.finish()
+
+
+def gather_rows(a, b):
+    return pl.pallas_call(
+        rows_kernel,
+        out_shape=(
+            jax.ShapeDtypeStruct((2, 2, 2) + a.shape, a.dtype),
+            jax.ShapeDtypeStruct((2, 2, 2) + b.shape, b.dtype),
+        ),
+        in_specs=[pl.BlockSpec(memory_space=pltpu.VMEM)] * 2,
+        out_specs=(pl.BlockSpec(memory_space=pl.ANY),) * 2,
+        scratch_shapes=[
+            pltpu.SemaphoreType.DMA((16,)),
+            pltpu.SemaphoreType.DMA((16,)),
+            pltpu.SemaphoreType.DMA((2,)),
+        ],
+        compiler_params=pltpu.CompilerParams(collective_id=1, has_side_effects=True),
+        cost_estimate=pl.CostEstimate(flops=0, bytes_accessed=90_000_000, transcendentals=0),
+        name="gather_rows",
+    )(a, b)
+
+
+def add_into(target, left, right):
+    lead = target.shape[:-2]
+    rows = target.shape[-2]
+    step = 16 if rows % 16 == 0 else 8
+    count = rows // step
+
+    def body(i, carry):
+        at = pl.ds(pl.multiple_of(i * step, step), step)
+        for index in itertools.product(*(range(n) for n in lead)):
+            at_all = index + (at,)
+            total = left[at_all].astype(jnp.float32) + right[at_all].astype(jnp.float32)
+            target[at_all] = total.astype(target.dtype)
+        return carry
+
+    lax.fori_loop(0, count, body, 0)
+
+
+class Part:
+    def __init__(self, take, half, held, from_c, from_first, from_second):
+        self.take, self.half, self.held, self.from_c = take, half, held, from_c
+        self.from_first, self.from_second = from_first, from_second
+
+
+def add_in_plane(place, send, parts, finish):
+    x, y, c = place.x, place.y, place.c
+    ox, oy, oc = place.ox, place.oy, place.oc
+    from_core = []
+    for part in parts:
+        copies = {}
+        for dx, dy in ((1, 1), (1, 0), (0, 1), (0, 0)):
+            xx, yy = (ox if dx else x), (oy if dy else y)
+            copies[dx, dy] = send(part.take(xx, yy, oc), part.from_c.at[xx, yy], place.to_c)
+        from_core.append(copies)
+    over = []
+    for part, copies in zip(parts, from_core):
+        for dx, dy in ((1, 1), (1, 0), (0, 1), (0, 0)):
+            xx, yy = (ox if dx else x), (oy if dy else y)
+            copies[dx, dy].wait_recv()
+            add_into(part.held.at[xx, yy], part.take(xx, yy, c), part.from_c.at[xx, yy])
+            if (dx, dy) == (1, 1):
+                a0 = send(part.half(xx, yy, 0), part.from_first.at[0, 1], place.to_y)
+                b0 = send(part.half(xx, yy, 1), part.from_first.at[1, 1], place.to_x)
+            elif (dx, dy) == (1, 0):
+                b1 = send(part.half(xx, yy, 1), part.from_first.at[1, 0], place.to_x)
+            elif (dx, dy) == (0, 1):
+                a1 = send(part.half(xx, yy, 0), part.from_first.at[0, 0], place.to_y)
+        over.append((a0, b0, a1, b1))
+    second = []
+    for part, (a0, b0, a1, b1) in zip(parts, over):
+        a0.wait_recv()
+        add_into(part.half(ox, y, 0), part.half(ox, y, 0), part.from_first.at[0, 1])
+        a2 = send(part.half(ox, y, 0), part.from_second.at[0], place.to_x)
+        b0.wait_recv()
+        add_into(part.half(x, oy, 1), part.half(x, oy, 1), part.from_first.at[1, 1])
+        b2 = send(part.half(x, oy, 1), part.from_second.at[1], place.to_y)
+        a1.wait_recv()
+        add_into(part.half(x, y, 0), part.half(x, y, 0), part.from_first.at[0, 0])
+        b1.wait_recv()
+        add_into(part.half(x, y, 1), part.half(x, y, 1), part.from_first.at[1, 0])
+        second.append((a2, b2))
+    results = []
+    for number, (part, (a2, b2)) in enumerate(zip(parts, second)):
+        a2.wait_recv()
+        b2.wait_recv()
+        results.append(finish(number, part))
+    return results
+
+
+def rows_sum_kernel(
+    grad_ref, value_ref, dots_ref, grad_out, value_out, dots_out,
+    grad_held, value_held, dots_held, grad_c, value_c, dots_c,
+    grad_first, value_first, dots_first, grad_second, value_second, dots_second,
+    send_sem, recv_sem,
+):
+    place = Place()
+    send = Sender(send_sem, recv_sem)
+    x, y = place.x, place.y
+    rows = grad_out.shape[0]
+    greet([place.to_x, place.to_y, place.to_c])
+
+    def part(ref, held, from_c, from_first, from_second):
+        return Part(
+            lambda xx, yy, cc: ref.at[cc, xx, yy],
+            lambda xx, yy, half: held.at[xx, yy, half_rows(half, rows)],
+            held, from_c, from_first, from_second,
+        )
+
+    parts = [
+        part(dots_ref, dots_held, dots_c, dots_first, dots_second),
+        part(grad_ref, grad_held, grad_c, grad_first, grad_second),
+        part(value_ref, value_held, value_c, value_first, value_second),
+    ]
+    outs = [dots_out, grad_out, value_out]
+
+    def finish(number, part):
+        for half in (0, 1):
+            add_into(outs[number].at[half_rows(half, rows)], part.half(x, y, half), part.from_second.at[half])
+
+    add_in_plane(place, send, parts, finish)
+    send.finish()
+
+
+def sum_rows(grad, value, dots):
+    rows = grad.shape[3]
+    arrays = (grad, value, dots)
+
+    def scratch(lead, height):
+        return [pltpu.VMEM(lead + (height, a.shape[4]), a.dtype) for a in arrays]
+
+    return pl.pallas_call(
+        rows_sum_kernel,
+        out_shape=tuple(jax.ShapeDtypeStruct(a.shape[3:], jnp.float32) for a in arrays),
+        in_specs=[pl.BlockSpec(memory_space=pltpu.VMEM)] * 3,
+        out_specs=(pl.BlockSpec(memory_space=pltpu.VMEM),) * 3,
+        scratch_shapes=scratch((2, 2), rows)
+        + scratch((2, 2), rows)
+        + scratch((2, 2), rows // 2)
+        + scratch((2,), rows // 2)
+        + [pltpu.SemaphoreType.DMA((32,)), pltpu.SemaphoreType.DMA((32,))],
+        compiler_params=pltpu.CompilerParams(
+            collective_id=2, has_side_effects=True, vmem_limit_bytes=60 * 2**20
+        ),
+        cost_estimate=pl.CostEstimate(flops=0, bytes_accessed=150_000_000, transcendentals=0),
+        name="sum_rows",
+    )(*arrays)
+
+
+def grads_kernel(count, *refs):
+    total_refs, refs = refs[:count], refs[count:]
+    ins, refs = refs[:3], refs[3:]
+    outs, got_refs, refs = refs[:3], refs[3 : 3 + count], refs[3 + count :]
+    held, from_c, from_first, from_second, own, from_z, alls = (refs[3 * i : 3 * i + 3] for i in range(7))
+    send_sem, recv_sem = refs[21:]
+    place = Place()
+    send = Sender(send_sem, recv_sem)
+    x, y, c, z = place.x, place.y, place.c, place.z
+    greet([place.to_x, place.to_y, place.to_c] + place.to_z[1:])
+    depth = ins[1].shape[2]
+    piece = depth // 4
+    heights = [piece, depth, depth]
+
+    def take(number):
+        ref = ins[number]
+        if number == 0:
+            return lambda xx, yy, cc: ref.at[:, xx, pl.ds(pl.multiple_of((yy * 2 + cc) * piece, piece), piece)]
+        wide = ref.shape[3] // 4
+        return lambda xx, yy, cc: ref.at[:, xx, :, pl.ds(pl.multiple_of((yy * 2 + cc) * wide, wide), wide)]
+
+    def half_of(number):
+        return lambda xx, yy, half: held[number].at[xx, yy, :, half_rows(half, heights[number])]
+
+    parts = [
+        Part(take(i), half_of(i), held[i], from_c[i], from_first[i], from_second[i]) for i in range(3)
+    ]
+
+    def finish(number, part):
+        for half in (0, 1):
+            add_into(
+                own[number].at[:, half_rows(half, heights[number])],
+                part.half(x, y, half),
+                part.from_second.at[half],
+            )
+        return [send(own[number].at[place.zs[d]], from_z[number].at[d - 1], place.to_z[d]) for d in (1, 2, 3)]
+
+    arriving = add_in_plane(place, send, parts, finish)
+    swapped = [send(total.at[place.ox], got, place.to_x) for total, got in zip(total_refs, got_refs)]
+    spread = []
+    for number in range(3):
+        mine, arrived = alls[number].at[y, c], from_z[number]
+        for copy in arriving[number]:
+            copy.wait_recv()
+        add_into(arrived.at[0], arrived.at[0], arrived.at[1])
+        add_into(arrived.at[2], arrived.at[2], own[number].at[z])
+        add_into(mine, arrived.at[0], arrived.at[2])
+        over_y = send(mine, mine, place.to_y)
+        spread.append((over_y, send(mine, mine, place.to_c)))
+    last = []
+    for number in range(3):
+        over_y, over_c = spread[number]
+        over_y.wait_recv()
+        other = alls[number].at[place.oy, c]
+        last.append((over_c, send(other, other, place.to_c)))
+    for number in range(3):
+        for copy in last[number]:
+            copy.wait_recv()
+        for yy, cc in itertools.product((0, 1), (0, 1)):
+            if number == 0:
+                at = (yy * 2 + cc) * piece
+                outs[0][at : at + piece, :] = alls[0][yy, cc]
+                continue
+            wide = alls[number].shape[3]
+            at = (yy * 2 + cc) * wide
+
+            def body(i, carry, number=number, at=at, yy=yy, cc=cc, wide=wide):
+                rows = pl.ds(pl.multiple_of(i * 16, 16), 16)
+                outs[number][rows, at : at + wide] = alls[number][yy, cc, rows, :].astype(jnp.float32)
+                return carry
+
+            lax.fori_loop(0, depth // 16, body, 0)
+    for copy in swapped:
+        copy.wait_recv()
+    send.finish()
+
+
+def sum_grads(small, output, mixer, totals):
+    depth = output.shape[2]
+    arrays = (small, output, mixer)
+    shapes = [((depth // 4, small.shape[3]), small.dtype)]
+    shapes += [((depth, a.shape[3] // 4), a.dtype) for a in arrays[1:]]
+    count = len(totals)
+
+    def scratch(lead, cut=1):
+        return [pltpu.VMEM(lead + (height // cut, wide), kind) for (height, wide), kind in shapes]
+
+    return pl.pallas_call(
+        functools.partial(grads_kernel, count),
+        out_shape=tuple(jax.ShapeDtypeStruct(a.shape[2:], jnp.float32) for a in arrays)
+        + tuple(jax.ShapeDtypeStruct(t.shape[1:], t.dtype) for t in totals),
+        in_specs=[pl.BlockSpec(memory_space=pl.ANY)] * count + [pl.BlockSpec(memory_space=pltpu.VMEM)] * 3,
+        out_specs=(pl.BlockSpec(memory_space=pltpu.VMEM),) * 3 + (pl.BlockSpec(memory_space=pl.ANY),) * count,
+        scratch_shapes=scratch((2, 2, 4))
+        + scratch((2, 2, 4))
+        + scratch((2, 2, 4), 2)
+        + scratch((2, 4), 2)
+        + scratch((4,))
+        + scratch((3,))
+        + scratch((2, 2))
+        + [pltpu.SemaphoreType.DMA((64,)), pltpu.SemaphoreType.DMA((64,))],
+        compiler_params=pltpu.CompilerParams(
+            collective_id=3, has_side_effects=True, vmem_limit_bytes=60 * 2**20
+        ),
+        cost_estimate=pl.CostEstimate(flops=0, bytes_accessed=300_000_000, transcendentals=0),
+        name="sum_grads",
+    )(*totals, *arrays)
+
+
+def swap_kernel(count, *refs):
+    total_refs, got_refs, (send_sem, recv_sem) = refs[:count], refs[count : 2 * count], refs[2 * count :]
+    place = Place()
+    send = Sender(send_sem, recv_sem)
+    greet([place.to_x])
+    for total, got in zip(total_refs, got_refs):
+        send(total.at[place.ox], got, place.to_x)
+    for copy in send.started:
+        copy.wait_recv()
+    send.finish()
+
+
+def swap_totals(totals):
+    count = len(totals)
+    return pl.pallas_call(
+        functools.partial(swap_kernel, count),
+        out_shape=tuple(jax.ShapeDtypeStruct(t.shape[1:], t.dtype) for t in totals),
+        in_specs=[pl.BlockSpec(memory_space=pl.ANY)] * count,
+        out_specs=(pl.BlockSpec(memory_space=pl.ANY),) * count,
+        scratch_shapes=[pltpu.SemaphoreType.DMA((count,))] * 2,
+        compiler_params=pltpu.CompilerParams(collective_id=5, has_side_effects=True),
+        cost_estimate=pl.CostEstimate(flops=0, bytes_accessed=40_000_000, transcendentals=0),
+        name="swap_totals",
+    )(*totals)
+
+
+def place_kernel(count, side_ref, *refs):
+    kept_refs, got_refs = refs[:count], refs[count : 2 * count]
+    up_out, down_out = refs[2 * count :]
+    half = down_out.shape[2] // 2
+    first = side_ref[0] == 0
+    for expert in range(count):
+        kept = kept_refs[expert][0].astype(jnp.float32)
+        got = got_refs[expert][...].astype(jnp.float32)
+        low, high = jnp.where(first, kept, got), jnp.where(first, got, kept)
+        for index, part in enumerate((low, high)):
+            for group in (0, 1):
+                at = (2 * group + index) * half
+                up_out[expert, :, at : at + half] = part[:, group * half : (group + 1) * half]
+            down_out[expert, :, index * half : (index + 1) * half] = part[:, 2 * half :]
+
+
+def place_sums(side, totals, got):
+    count = len(totals)
+    depth, width = got[0].shape
+    step = depth // 4
+    half = width // 3
+    return pl.pallas_call(
+        functools.partial(place_kernel, count),
+        out_shape=(
+            jax.ShapeDtypeStruct((count, depth, 4 * half), jnp.float32),
+            jax.ShapeDtypeStruct((count, depth, 2 * half), jnp.float32),
+        ),
+        grid_spec=pltpu.PrefetchScalarGridSpec(
+            num_scalar_prefetch=1,
+            grid=(4,),
+            in_specs=[pl.BlockSpec((1, step, width), lambda i, side: (side[0], i, 0))] * count
+            + [pl.BlockSpec((step, width), lambda i, side: (i, 0))] * count,
+            out_specs=(
+                pl.BlockSpec((count, step, 4 * half), lambda i, side: (0, i, 0)),
+                pl.BlockSpec((count, step, 2 * half), lambda i, side: (0, i, 0)),
+            ),
+        ),
+        cost_estimate=pl.CostEstimate(flops=0, bytes_accessed=9_000_000, transcendentals=0),
+        name="place_sums",
+    )(side, *totals, *got)
+
+
+def expert_kernel(slots_ref, gates_ref, rows_ref, dout_ref, w_ref, answer_ref, row_ref, w_out, dots_ref, total, picked, picked_dout):
+    group, slot_rows, width = answer_ref.shape
+    half = w_ref.shape[1] // 3
+    seq_len = rows_ref.shape[1]
+    step = pl.program_id(0)
+    slot_ids = lax.broadcasted_iota(jnp.int32, (slot_rows, seq_len), 0).astype(jnp.float32)
+    gate_parts = []
+    for q in range(group):
+        placing = (slot_ids == slots_ref[q]).astype(jnp.float32)
+        gate_parts.append(jnp.sum(placing * gates_ref[q], axis=1, keepdims=True))
+        low = placing.astype(jnp.bfloat16)
+        at = slice(q * slot_rows, (q + 1) * slot_rows)
+        picked[at, :] = jnp.dot(low, rows_ref[q], preferred_element_type=jnp.float32).astype(jnp.bfloat16)
+        picked_dout[at, :] = jnp.dot(low, dout_ref[q], preferred_element_type=jnp.float32).astype(jnp.bfloat16)
+    gate = jnp.concatenate(gate_parts, axis=0)
+    both = jnp.dot(picked[...], w_ref[:, : 2 * half], preferred_element_type=jnp.float32)
+    gate_part, up_part = both[:, :half], both[:, half:]
+    sigmoid = 1.0 / (1.0 + jnp.exp(-gate_part))
+    silu = gate_part * sigmoid
+    active = (silu * up_part).astype(jnp.bfloat16)
+    across = (((1,), (1,)), ((), ()))
+    down = (((0,), (0,)), ((), ()))
+    answer = lax.dot_general(active, w_ref[:, 2 * half :], across, preferred_element_type=jnp.float32)
+    answer = answer.astype(jnp.bfloat16)
+    dots = jnp.sum(picked_dout[...].astype(jnp.float32) * answer.astype(jnp.float32), axis=1, keepdims=True)
+    for q in range(group):
+        at = slice(q * slot_rows, (q + 1) * slot_rows)
+        answer_ref[q] = answer[at, :]
+        placing = (slot_ids == slots_ref[q]).astype(jnp.float32)
+        dots_ref[q] = jnp.sum(placing * dots[at, :], axis=0, keepdims=True)
+    picked_dout[...] = (picked_dout[...].astype(jnp.float32) * gate).astype(jnp.bfloat16)
+    active_grad = jnp.dot(picked_dout[...], w_ref[:, 2 * half :], preferred_element_type=jnp.float32)
+    both_grad = jnp.concatenate(
+        [
+            active_grad * up_part * sigmoid * (1.0 + gate_part * (1.0 - sigmoid)),
+            active_grad * silu,
+        ],
+        axis=1,
+    ).astype(jnp.bfloat16)
+    row = lax.dot_general(both_grad, w_ref[:, : 2 * half], across, preferred_element_type=jnp.float32)
+    row = row.astype(jnp.bfloat16)
+    for q in range(group):
+        row_ref[q] = row[q * slot_rows : (q + 1) * slot_rows, :]
+    up_term = lax.dot_general(picked[...], both_grad, down, preferred_element_type=jnp.float32)
+    down_term = lax.dot_general(picked_dout[...], active, down, preferred_element_type=jnp.float32)
+
+    @pl.when(step == 0)
+    def _():
+        total[:, : 2 * half] = up_term
+        total[:, 2 * half :] = down_term
+
+    @pl.when(step > 0)
+    def _():
+        total[:, : 2 * half] += up_term
+        total[:, 2 * half :] += down_term
+
+    @pl.when(step == pl.num_programs(0) - 1)
+    def _():
+        w_out[...] = total[...].astype(w_out.dtype)
+
+
+def run_expert(slots, gates, rows, dout, weights, slot_rows):
+    count, seq_len, width = rows.shape
+    group = count // 2
+    wide = weights.shape[1]
+    one = pl.BlockSpec((group, 1, seq_len), lambda i: (i, 0, 0))
+    tall = pl.BlockSpec((group, seq_len, width), lambda i: (i, 0, 0))
+    slot = pl.BlockSpec((group, slot_rows, width), lambda i: (i, 0, 0))
+    whole = pl.BlockSpec(weights.shape, lambda i: (0, 0))
+    flops = 2 * count * slot_rows * width * (2 * seq_len + 3 * wide)
+    return pl.pallas_call(
+        expert_kernel,
+        grid=(2,),
+        out_shape=(
+            jax.ShapeDtypeStruct((count, slot_rows, width), jnp.bfloat16),
+            jax.ShapeDtypeStruct((count, slot_rows, width), jnp.bfloat16),
+            jax.ShapeDtypeStruct(weights.shape, jnp.bfloat16),
+            jax.ShapeDtypeStruct((count, 1, seq_len), jnp.float32),
+        ),
+        in_specs=[one, one, tall, tall, whole],
+        out_specs=(slot, slot, whole, one),
+        scratch_shapes=[
+            pltpu.VMEM(weights.shape, jnp.float32),
+            pltpu.VMEM((group * slot_rows, width), jnp.bfloat16),
+            pltpu.VMEM((group * slot_rows, width), jnp.bfloat16),
+        ],
+        compiler_params=pltpu.CompilerParams(vmem_limit_bytes=60 * 2**20),
+        cost_estimate=pl.CostEstimate(flops=flops, bytes_accessed=25_000_000, transcendentals=0),
+        name="run_expert",
+    )(slots, gates, rows, dout, weights)
+
+
+def combine_kernel(experts, table_ref, *refs):
+    answers, rows = refs[:experts], refs[experts : 2 * experts]
+    value_ref, grad_ref = refs[2 * experts :]
+    slot_rows = answers[0].shape[1]
+    table = table_ref[0]
+    seq_len, lanes = table.shape
+    slot_ids = lax.broadcasted_iota(jnp.int32, (seq_len, slot_rows), 1).astype(jnp.float32)
+    placings, combines = [], []
+    for expert in range(experts):
+        placing = (slot_ids == table[:, experts + expert : experts + expert + 1]).astype(jnp.float32)
+        placings.append(placing)
+        combines.append(placing * table[:, expert : expert + 1])
+    placing = jnp.concatenate(placings, axis=1).astype(jnp.bfloat16)
+    combine = jnp.concatenate(combines, axis=1).astype(jnp.bfloat16)
+    answer = jnp.concatenate([ref[0] for ref in answers], axis=0)
+    row = jnp.concatenate([ref[0] for ref in rows], axis=0)
+    value_ref[0] = jnp.dot(combine, answer, preferred_element_type=jnp.float32).astype(value_ref.dtype)
+    grad_ref[0] = jnp.dot(placing, row, preferred_element_type=jnp.float32).astype(grad_ref.dtype)
+
+
+def combine_experts(table, answers, rows):
+    experts = len(answers)
+    count, slot_rows, width = answers[0].shape
+    seq_len = table.shape[1]
+    slot = pl.BlockSpec((1, slot_rows, width), lambda i: (i, 0, 0))
+    tall = pl.BlockSpec((1, seq_len, width), lambda i: (i, 0, 0))
+    return pl.pallas_call(
+        functools.partial(combine_kernel, experts),
+        grid=(count,),
+        out_shape=(jax.ShapeDtypeStruct((count, seq_len, width), jnp.bfloat16),) * 2,
+        in_specs=[pl.BlockSpec((1,) + table.shape[1:], lambda i: (i, 0, 0))] + [slot] * (2 * experts),
+        out_specs=(tall, tall),
+        compiler_params=pltpu.CompilerParams(vmem_limit_bytes=60 * 2**20),
+        cost_estimate=pl.CostEstimate(
+            flops=4 * count * seq_len * width * experts * slot_rows, bytes_accessed=40_000_000, transcendentals=0
+        ),
+        name="combine_experts",
+    )(table, *answers, *rows)
+
+
+def layer_on_device(
+    tokens,
+    lengths,
+    routes,
+    cotangent,
+    first_gain,
+    query_weight,
+    key_matrix,
+    value_matrix,
+    output_weight,
+    second_gain,
+    router_weight,
+    gate_up_weight,
+    down_weight,
+):
+    seq_len, model_width = tokens.shape
+    q_heads = query_weight.shape[1] // HEAD_DIM
+    kv_heads = key_matrix.shape[1] // HEAD_DIM
+    group_size = q_heads // kv_heads
+    experts_all = router_weight.shape[1]
+    local_experts = gate_up_weight.shape[1]
+    inner_width = down_weight.shape[2]
+    half_inner = inner_width // 2
+    q_width, kv_width = query_weight.shape[1], key_matrix.shape[1]
+    slot_count = 8 * max(
+        seq_len // 32, (seq_len * routes.shape[1] + 8 * experts_all - 1) // (8 * experts_all)
+    )
+    score_factor = HEAD_DIM ** (-0.5)
+    along_z = [[z * 2 + x for z in range(4)] for x in range(2)]
+    expert_at, shard_at = lax.axis_index(EXPERT), lax.axis_index(SHARD)
+    x_at = lax.rem(shard_at, 2)
+    depth = first_gain.shape[0]
+
+    early = 2
+    up_first = gate_up_weight.transpose(1, 0, 2)
+    down_first = down_weight.transpose(1, 0, 2)
+
+    def along(halves):
+        return lax.all_gather(
+            halves.reshape(2 * depth, 3 * half_inner), SHARD, axis=0, tiled=True, axis_index_groups=along_z
+        )
+
+    halves = exchange_halves(up_first, down_first, early)
+    expert_weights = [along(h) for h in halves]
+
+    position = jnp.arange(seq_len, dtype=jnp.int32)
+    length = lengths[0]
+    valid_rows = (position < length).astype(jnp.float32)
+    dout_full = cotangent.astype(jnp.float32) * valid_rows[:, None]
+    dout_low = dout_full.astype(jnp.bfloat16)
+    mixer_block = jnp.concatenate([query_weight, key_matrix, value_matrix], axis=1)
+    small_block = jnp.concatenate(
+        [
+            router_weight.astype(jnp.float32),
+            first_gain.astype(jnp.float32)[:, None],
+            second_gain.astype(jnp.float32)[:, None],
+            jnp.zeros((depth, 128 - experts_all - 2), jnp.float32),
+        ],
+        axis=1,
+    )
+    mixer_block, output_block, small_block, dout_low = lax.optimization_barrier(
+        (mixer_block, output_weight, small_block, dout_low) + tuple(halves)
+    )[:4]
+    mixer_full, output_full, small_full, dout_plane, *halves = gather_weights(
+        mixer_block, output_block, small_block, dout_low, up_first, down_first, early
+    )
+    expert_weights += [along(h) for h in halves]
+    mixer_full = mixer_full.reshape(model_width, mixer_block.shape[1])
+    output_full = output_full.reshape(model_width, output_weight.shape[1])
+    small_full = small_full.reshape(model_width, 128)
+    dout_plane = dout_plane.reshape(8, seq_len, model_width)
+    router_full = small_full[:, :experts_all].astype(jnp.bfloat16)
+    gain_one, gain_two = small_full[:, experts_all], small_full[:, experts_all + 1]
+
+    cosine, sine_table = rope_tables(seq_len, HEAD_DIM)
+    source = tokens.astype(jnp.float32)
+    first_scale = lax.rsqrt(jnp.mean(source * source, axis=-1, keepdims=True) + norm_eps)
+    first_norm_output = (source * first_scale * gain_one).astype(jnp.bfloat16)
+    mixed_in = product("za,ao->zo", first_norm_output, mixer_full)
+    queries = rotate(mixed_in[:, :q_width].reshape(seq_len, q_heads, HEAD_DIM), cosine, sine_table)
+    queries = queries.astype(jnp.bfloat16).reshape(seq_len, kv_heads, group_size, HEAD_DIM)
+    key_row_block = rotate(
+        mixed_in[:, q_width : q_width + kv_width].reshape(seq_len, kv_heads, HEAD_DIM), cosine, sine_table
+    ).astype(jnp.bfloat16)
+    value_row_block = (
+        mixed_in[:, q_width + kv_width :].astype(jnp.bfloat16).reshape(seq_len, kv_heads, HEAD_DIM)
+    )
+    allowed = (position[None, :] <= position[:, None]) & (position[None, :] < length)
+    scores = jnp.where(
+        allowed, product("qhgd,khd->hgqk", queries, key_row_block) * score_factor, -1e30
+    )
+    row_max = jnp.max(scores, axis=-1, keepdims=True)
+    shifted = jnp.exp(scores - row_max)
+    row_total = jnp.sum(shifted, axis=-1, keepdims=True)
+    log_total = row_max + jnp.log(row_total)
+    probs_low = (shifted / row_total).astype(jnp.bfloat16)
+    mixed_heads = (
+        product("hgqk,khd->qhgd", probs_low, value_row_block)
+        .reshape(seq_len, q_heads * HEAD_DIM)
+        .astype(jnp.bfloat16)
+    )
+    hidden = source + product("sf,df->sd", mixed_heads, output_full)
+    second_scale = lax.rsqrt(jnp.mean(hidden * hidden, axis=-1, keepdims=True) + norm_eps)
+    second_normed = (hidden * second_scale * gain_two).astype(jnp.bfloat16)
+    logits = product("sd,de->se", second_normed, router_full)
+    chosen = (routes[:, :, None] == jnp.arange(experts_all, dtype=jnp.int32)).astype(jnp.float32)
+    picked = jnp.sum(chosen * logits[:, None, :], axis=-1)
+    gate_soft = jax.nn.softmax(picked, axis=-1)
+    routed = jnp.sum(chosen, axis=1) * valid_rows[:, None]
+    earlier = (position[None, :] < position[:, None]).astype(jnp.bfloat16)
+    rank_rows = product("st,te->se", earlier, routed.astype(jnp.bfloat16))
+    slot_of = jnp.where(routed > 0, rank_rows, -1.0)
+    gate_low = gate_soft.astype(jnp.bfloat16).astype(jnp.float32)
+    gate_full = jnp.sum(chosen * gate_low[:, :, None], axis=1)
+    table = jnp.concatenate(
+        [gate_full, slot_of, jnp.zeros((seq_len, 128 - 2 * experts_all), jnp.float32)], axis=1
+    )
+    rows_plane, table_plane = gather_rows(second_normed, table)
+    rows_plane = rows_plane.reshape(8, seq_len, model_width)
+    table_plane = table_plane.reshape(8, seq_len, 128)
+    first_own = expert_at * local_experts
+    gates = lax.dynamic_slice_in_dim(table_plane, first_own, local_experts, axis=2)
+    slots = lax.dynamic_slice_in_dim(table_plane, experts_all + first_own, local_experts, axis=2)
+    own_table = jnp.concatenate(
+        [gates, slots, jnp.zeros((8, seq_len, 128 - 2 * local_experts), jnp.float32)], axis=2
+    )
+    gates_by = gates.transpose(2, 0, 1)[:, :, None, :]
+    slots_by = slots.transpose(2, 0, 1)[:, :, None, :]
+    slot_rows = -(-slot_count // 16) * 16
+    answers, row_grads, sums, dots = zip(
+        *(
+            run_expert(slots_by[e], gates_by[e], rows_plane, dout_plane, expert_weights[e], slot_rows)
+            for e in range(local_experts)
+        )
+    )
+    sums = lax.optimization_barrier(tuple(sums) + (expert_weights[-1],))[:-1]
+    value_part, grad_part = combine_experts(own_table, answers, row_grads)
+    dots = jnp.stack([dot[:, 0, :] for dot in dots], axis=-1)
+    dot_part = lax.dynamic_update_slice_in_dim(jnp.zeros((8, seq_len, 128), jnp.float32), dots, first_own, axis=2)
+    plane = (2, 2, 2, seq_len)
+    grad_rows, value_rows, dot_rows = sum_rows(
+        grad_part.reshape(plane + (model_width,)),
+        value_part.reshape(plane + (model_width,)),
+        dot_part.reshape(plane + (128,)),
+    )
+    output = (hidden + value_rows).astype(jnp.bfloat16)
+    gate_grad = jnp.sum(chosen * dot_rows[:, None, :experts_all], axis=-1)
+    inner_sum = jnp.sum(gate_soft * gate_grad, axis=-1, keepdims=True)
+    picked_grad = gate_soft * (gate_grad - inner_sum)
+    logits_grad = jnp.sum(chosen * picked_grad[:, :, None], axis=1).astype(jnp.bfloat16)
+    router_term = product("sd,se->de", second_normed, logits_grad)
+
+    totals = [
+        lax.psum_scatter(
+            sums[expert], SHARD, scatter_dimension=0, tiled=True, axis_index_groups=along_z
+        ).reshape(2, depth, 3 * half_inner)
+        for expert in range(local_experts)
+    ]
+
+    normed_grad = grad_rows + product("se,de->sd", logits_grad, router_full)
+    hidden_grad, second_gain_term = norm_back(normed_grad, hidden, second_scale, gain_two)
+    hidden_grad = hidden_grad + dout_full
+    attn_grad = hidden_grad.astype(jnp.bfloat16)
+    output_term = product("sd,sf->df", attn_grad, mixed_heads)
+    mixed_grad = (
+        product("za,ao->zo", attn_grad, output_full)
+        .astype(jnp.bfloat16)
+        .reshape(seq_len, kv_heads, group_size, HEAD_DIM)
+    )
+    scores_again = jnp.where(
+        allowed, product("qhgd,khd->hgqk", queries, key_row_block) * score_factor, -1e30
+    )
+    probs_again = jnp.exp(scores_again - log_total)
+    probs_grad = product("qhgd,khd->hgqk", mixed_grad, value_row_block)
+    row_inner = jnp.sum(probs_again * probs_grad, axis=-1, keepdims=True)
+    scores_grad = (probs_again * (probs_grad - row_inner)).astype(jnp.bfloat16)
+    query_back = product("hgqk,khd->qhgd", scores_grad, key_row_block) * score_factor
+    key_back = product("hgqk,qhgd->khd", scores_grad, queries) * score_factor
+    value_back = product("hgqk,qhgd->khd", probs_again.astype(jnp.bfloat16), mixed_grad)
+    query_pre = (
+        unrotate(query_back.reshape(seq_len, q_heads, HEAD_DIM), cosine, sine_table)
+        .astype(jnp.bfloat16)
+        .reshape(seq_len, q_heads * HEAD_DIM)
+    )
+    key_pre = (
+        unrotate(key_back, cosine, sine_table)
+        .astype(jnp.bfloat16)
+        .reshape(seq_len, kv_heads * HEAD_DIM)
+    )
+    value_pre = value_back.astype(jnp.bfloat16).reshape(seq_len, kv_heads * HEAD_DIM)
+    mixed_pre = jnp.concatenate([query_pre, key_pre, value_pre], axis=1)
+    mixer_term = product("sd,sf->df", first_norm_output, mixed_pre).astype(jnp.bfloat16)
+    normed1_grad = product("sf,df->sd", mixed_pre, mixer_full)
+    tokens_grad, first_gain_term = norm_back(normed1_grad, source, first_scale, gain_one)
+    tokens_grad = tokens_grad + hidden_grad
+    small_terms = jnp.concatenate(
+        [
+            router_term,
+            first_gain_term[:, None],
+            second_gain_term[:, None],
+            jnp.zeros((model_width, 128 - experts_all - 2), jnp.float32),
+        ],
+        axis=1,
+    ).reshape(4, 2, depth, 128)
+    swapped = 3
+    small_sum, output_sum, mixer_sum, *got = sum_grads(
+        small_terms,
+        output_term.astype(jnp.bfloat16).reshape(4, 2, depth, output_weight.shape[1]),
+        mixer_term.reshape(4, 2, depth, mixer_block.shape[1]),
+        totals[:swapped],
+    )
+    late = lax.optimization_barrier((small_sum,) + tuple(totals[swapped:]))[1:]
+    got += swap_totals(late)
+    both_sums, down_sums = place_sums(x_at.reshape(1), totals, got)
+    return (
+        output,
+        tokens_grad,
+        small_sum[:, experts_all],
+        mixer_sum[:, :q_width],
+        mixer_sum[:, q_width : q_width + kv_width],
+        mixer_sum[:, q_width + kv_width :],
+        output_sum,
+        small_sum[:, experts_all + 1],
+        small_sum[:, :experts_all],
+        both_sums.transpose(1, 0, 2),
+        down_sums.transpose(1, 0, 2),
+    )
+
+
 def solution(mesh):
+    small_slice = mesh.shape[EXPERT] == 4 and mesh.shape[SHARD] == 8
     placed = (
-        P(("expert", "shard"), None),
-        P(("expert", "shard")),
-        P(("expert", "shard"), None),
-        P(("expert", "shard"), None),
-        P("shard"),
-        P("shard", None),
-        P("shard", None),
-        P("shard", None),
-        P("shard", None),
-        P("shard"),
-        P("shard", None),
-        P("shard", "expert", None),
-        P("shard", "expert", None),
+        P((EXPERT, SHARD), None),
+        P((EXPERT, SHARD)),
+        P((EXPERT, SHARD), None),
+        P((EXPERT, SHARD), None),
+        P(SHARD),
+        P(SHARD, None),
+        P(SHARD, None),
+        P(SHARD, None),
+        P(SHARD, None),
+        P(SHARD),
+        P(SHARD, None),
+        P(SHARD, EXPERT, None),
+        P(SHARD, EXPERT, None),
     )
     return jax.shard_map(
-        on_device,
+        layer_on_device if small_slice else on_device,
         mesh=mesh,
         in_specs=placed,
         out_specs=(
-            P(("expert", "shard"), None),
-            P(("expert", "shard"), None),
-            P("shard"),
-            P("shard", None),
-            P("shard", None),
-            P("shard", None),
-            P("shard", None),
-            P("shard"),
-            P("shard", None),
-            P("shard", "expert", None),
-            P("shard", "expert", None),
+            P((EXPERT, SHARD), None),
+            P((EXPERT, SHARD), None),
+            P(SHARD),
+            P(SHARD, None),
+            P(SHARD, None),
+            P(SHARD, None),
+            P(SHARD, None),
+            P(SHARD),
+            P(SHARD, None),
+            P(SHARD, EXPERT, None),
+            P(SHARD, EXPERT, None),
         ),
         check_vma=False,
     )

time: 1760 us -> 667 us (0.38)
  waiting for transfers between devices: 1260 us -> 6.71 us
  Pallas kernels: 0 us -> 531 us
  blocking collectives: 220 us -> 0 us
  matrix products: 149 us -> 39.7 us
  local copies, waits for them, and re-layouts: 66.5 us -> 46.9 us
    pallas_call x0 -> x13, Pallas kernels: none -> 531 us  [the longest x1 143 us: gather_weights(): pl.pallas_call(functools.partial(weights_kernel, first, count), out_shape...]
    all_gather x6 -> x5, waiting for transfers between devices: 447 us -> 0.09 us  [along(): lax.all_gather(halves.reshape(2 * depth, 3 * half_inner), SHARD, axis=0,...]
    unnamed x17 -> x10, waiting for transfers between devices: 390 us -> 3.22 us
    reduce_scatter x4 -> x5, waiting for transfers between devices: 303 us -> 3.41 us  [layer_on_device(): lax.psum_scatter(sums[expert], SHARD, scatter_dimension=0, tiled=True, ax...]
    all_to_all x2 -> x0, blocking collectives: 151 us -> none  [the longest x1 75.7 us: on_device(): lax.all_to_all(grad_rows, 'expert', split_axis=0, concat_axis=0, tiled=True)]
    all_to_all x2 -> x0, waiting for transfers between devices: 115 us -> none  [the longest x1 71.5 us: on_device(): lax.all_to_all(row_grad, 'expert', split_axis=0, concat_axis=0, tiled=True)]
    dot_general x33 -> x16, matrix products: 149 us -> 39.7 us  [product(): return jnp.einsum(form, left, right, preferred_element_type=jnp.float32)]
    unnamed x98 -> x142, local copies, waits for them, and re-layouts: 52 us -> 12.3 us
  transfers between devices with their start and end apart: 16 -> 10, of which waited for: 16 -> 1; matrix products, arithmetic and copies ran while one was open for 8% -> 14% of each run, Pallas kernels for 0% -> 72%
where the time goes in v1:
time: 667 us; the launch traced here: 658 us
  Pallas kernels  531 us (80%)
  local copies, waits for them, and re-layouts  46.9 us (7%)
  matrix products  39.7 us (6%)
  other arithmetic  16.1 us (2%)
  between operations  16.1 us (2%)
  waiting for transfers between devices  6.71 us (1%)
    pallas_call x1, Pallas kernels, gather_weights(): pl.pallas_call(functools.partial(weights_kernel, first, count), out_shape...  143 us
    pallas_call x1, Pallas kernels, sum_grads(): pl.pallas_call(functools.partial(grads_kernel, count), out_shape=tuple((j...  134 us
    pallas_call x5, Pallas kernels, run_expert(): pl.pallas_call(expert_kernel, grid=(2,), out_shape=(jax.ShapeDtypeStruct(...  89 us
    pallas_call x1, Pallas kernels, sum_rows(): pl.pallas_call(rows_sum_kernel, out_shape=tuple((jax.ShapeDtypeStruct(a.s...  68.8 us
    dot_general x16, matrix products, product(): return jnp.einsum(form, left, right, preferred_element_type=jnp.float32)  39.7 us
    pallas_call x1, Pallas kernels, gather_rows(): pl.pallas_call(rows_kernel, out_shape=(jax.ShapeDtypeStruct((2, 2, 2) + a...  37.6 us
    pallas_call x1, Pallas kernels, combine_experts(): pl.pallas_call(functools.partial(combine_kernel, experts), grid=(count,),...  20.1 us
    pallas_call x1, Pallas kernels, exchange_halves(): pl.pallas_call(functools.partial(halves_kernel, 0, count), out_shape=(jax...  17.2 us
  transfers between devices with their start and end apart: 10, of which 1 were waited for; matrix products, arithmetic and copies ran while one was open for 14% of the time, Pallas kernels for 72%

profile of v1, /device:TPU:10, one launch (start us, length us, event | category | flops | bytes accessed | tf_op | source)
XLA Modules:
  0.0 657.9 jit_solution(14247213091196453162)
XLA Ops:
  7.3 17.2 %exchange_halves.1 = (bf16[2,192,768]{2,1,0:T(8,128)(2,1)}, bf16[2,192,768]{2,1,0:T(8,128)(2,1)}) custom-call(bf16[5,192,1024]{2,1,0:T(8,128)(2,1)} %bitcast.121, bf16[5,192,512]{2,1,0:T(8,128)(2,1)} %bitcast.131), custom_call_target="tpu_custom_call" | custom-call | bytes 40000000 | tf_op jit(solution)/shard_map/exchange_halves/pallas_call | solution.py:445
  29.9 143.4 %gather_weights.1 = (bf16[4,2,192,2560]{3,2,1,0:T(8,128)(2,1)}, bf16[4,2,192,1536]{3,2,1,0:T(8,128)(2,1)}, f32[4,2,192,128]{3,2,1,0:T(8,128)}, bf16[2,2,2,256,15...) custom-call(bf16[5,192,1024]{2,1,0:T(8,128)(2,1)} %bitcast.122, ...), custom_call_target="tpu_custom_call" | custom-call | bytes 200000000 | tf_op jit(solution)/shard_map/gather_weights/pallas_call | solution.py:535
  176.8 5.5 fusion.35
  185.3 1.9 copy.128
  188.0 2.0 copy.127
  193.7 2.1 copy-done
  201.7 37.6 %gather_rows.1 = (bf16[2,2,2,256,1536]{4,3,2,1,0:T(8,128)(2,1)}, f32[2,2,2,256,128]{4,3,2,1,0:T(8,128)}) custom-call(bf16[256,1536]{1,0:T(8,128)(2,1)} %copy-done.6, f32[256,128]{1,0:T(8,128)} %maximum_maximum_fusion.2.b_ref), custom_call_target="tpu_custom_call" | custom-call | bytes 90000000 | tf_op jit(solution)/shard_map/gather_rows/pallas_call | solution.py:582
  239.3 2.2 constant_dynamic-slice_fusion.1
  241.5 2.7 slice_reduce_fusion.1
  244.8 2.5 slice_reduce_fusion
  252.7 17.7 %run_expert.5 = (bf16[8,112,1536]{2,1,0:T(8,128)(2,1)}, bf16[8,112,1536]{2,1,0:T(8,128)(2,1)}, bf16[1536,768]{1,0:T(8,128)(2,1)}, f32[8,1,256]{2,1,0:T(1,128)}) custom-call(f32[8,1,256]{2,1,0:T(1,128)} %squeeze.52.slots_ref, f32[8,1,256]{2,1,0:T(1,128)} %squeeze.53.gates_ref, bf16[8,256,1536]{2,1,0:T(8,128)(2,1)} %bitcast.180, ...), custom_call_target="tpu_custom_call" | custom-call | flops 7751073792 | bytes 25000000 | tf_op jit(solution)/shard_map/run_expert/pallas_call | solution.py:975
  270.5 17.6 %run_expert.6 = (bf16[8,112,1536]{2,1,0:T(8,128)(2,1)}, bf16[8,112,1536]{2,1,0:T(8,128)(2,1)}, bf16[1536,768]{1,0:T(8,128)(2,1)}, f32[8,1,256]{2,1,0:T(1,128)}) custom-call(f32[8,1,256]{2,1,0:T(1,128)} %squeeze.54.slots_ref, f32[8,1,256]{2,1,0:T(1,128)} %squeeze.55.gates_ref, bf16[8,256,1536]{2,1,0:T(8,128)(2,1)} %bitcast.181, ...), custom_call_target="tpu_custom_call" | custom-call | flops 7751073792 | bytes 25000000 | tf_op jit(solution)/shard_map/run_expert/pallas_call | solution.py:975
  288.2 17.8 %run_expert.7 = (bf16[8,112,1536]{2,1,0:T(8,128)(2,1)}, bf16[8,112,1536]{2,1,0:T(8,128)(2,1)}, bf16[1536,768]{1,0:T(8,128)(2,1)}, f32[8,1,256]{2,1,0:T(1,128)}) custom-call(f32[8,1,256]{2,1,0:T(1,128)} %squeeze.56.slots_ref, f32[8,1,256]{2,1,0:T(1,128)} %squeeze.57.gates_ref, bf16[8,256,1536]{2,1,0:T(8,128)(2,1)} %bitcast.182, ...), custom_call_target="tpu_custom_call" | custom-call | flops 7751073792 | bytes 25000000 | tf_op jit(solution)/shard_map/run_expert/pallas_call | solution.py:975
  306.0 17.8 %run_expert.8 = (bf16[8,112,1536]{2,1,0:T(8,128)(2,1)}, bf16[8,112,1536]{2,1,0:T(8,128)(2,1)}, bf16[1536,768]{1,0:T(8,128)(2,1)}, f32[8,1,256]{2,1,0:T(1,128)}) custom-call(f32[8,1,256]{2,1,0:T(1,128)} %squeeze.58.slots_ref, f32[8,1,256]{2,1,0:T(1,128)} %squeeze.59.gates_ref, bf16[8,256,1536]{2,1,0:T(8,128)(2,1)} %bitcast.183, ...), custom_call_target="tpu_custom_call" | custom-call | flops 7751073792 | bytes 25000000 | tf_op jit(solution)/shard_map/run_expert/pallas_call | solution.py:975
  323.8 18.0 %run_expert.9 = (bf16[8,112,1536]{2,1,0:T(8,128)(2,1)}, bf16[8,112,1536]{2,1,0:T(8,128)(2,1)}, bf16[1536,768]{1,0:T(8,128)(2,1)}, f32[8,1,256]{2,1,0:T(1,128)}) custom-call(f32[8,1,256]{2,1,0:T(1,128)} %squeeze.60.slots_ref, f32[8,1,256]{2,1,0:T(1,128)} %squeeze.61.gates_ref, bf16[8,256,1536]{2,1,0:T(8,128)(2,1)} %bitcast.184, ...), custom_call_target="tpu_custom_call" | custom-call | flops 7751073792 | bytes 25000000 | tf_op jit(solution)/shard_map/run_expert/pallas_call | solution.py:975
  346.1 2.7 dynamic_update_slice.3
  348.8 20.1 %combine_experts.1 = (bf16[8,256,1536]{2,1,0:T(8,128)(2,1)}, bf16[8,256,1536]{2,1,0:T(8,128)(2,1)}) custom-call(f32[8,256,128]{2,1,0:T(8,128)} %maximum_maximum_fusion.table_ref, bf16[8,112,1536]{2,1,0:T(8,128)(2,1)} %get-tuple-element.80.refs_0_, bf16[8,112,1536]{2,1,0:T(8,128)(2,1)} %get-tuple-element.81.refs_1_, ...), custom_call_target="tpu_custom_call" | custom-call | flops 7046430720 | bytes 40000000 | tf_op jit(solution)/shard_map/combine_experts/pallas_call | solution.py:1023
  369.0 68.8 %sum_rows.1 = (f32[256,1536]{1,0:T(8,128)}, f32[256,1536]{1,0:T(8,128)}, f32[256,128]{1,0:T(8,128)}) custom-call(bf16[2,2,2,256,1536]{4,3,2,1,0:T(8,128)(2,1)} %bitcast.128, bf16[2,2,2,256,1536]{4,3,2,1,0:T(8,128)(2,1)} %bitcast.127, f32[2,2,2,256,128]{4,3,2,1,0:T(8,128)} %bitcast.130), custom_call_target="tpu_custom_call" | custom-call | bytes 150000000 | tf_op jit(solution)/shard_map/sum_rows/pallas_call | solution.py:710
  439.0 2.2 multiply_reduce_fusion
  445.6 4.9 fusion
  451.0 1.8 fusion.2
  452.7 1.7 copy-done.1
  457.9 2.7 convolution_multiply_fusion
  463.3 6.8 %fusion.19 = (f32[1536]{0:T(1024)S(1)}, f32[256]{0:T(256)S(1)}, f32[256,1536]{1,0:T(8,128)}) fusion(bf16[256,1536]{1,0:T(8,128)(2,1)S(1)} %copy-done.11, f32[256]{0:T(256)S(1)} %copy-done.48, f32[1536]{0:T(1024)S(1)} %get-tuple-element.184, bf16[1536,2560]{1,0:T(8,128)(2,1)} %bitcast.174, bf16[256,512]{0,1:T(8,128)(2,1)S(1)} %bitcast.151, ...), kind=kOutput, calls=%fused_computation.33 | convolution fusion | flops 2019948800 | bytes 11548672 | tf_op jit(solution)/shard_map/sf,df->sd/dot_general | solution.py:19
  474.4 3.6 convolution_convert_fusion.1
  478.1 5.5 convolution_convert_fusion
  485.2 3.4 reduce-scatter.10.cloned.1.call-done
  488.6 133.8 %sum_grads.1 = (f32[192,128]{1,0:T(8,128)}, f32[192,1536]{1,0:T(8,128)}, f32[192,2560]{1,0:T(8,128)}, bf16[192,768]{1,0:T(8,128)(2,1)}, bf16[192,768]{1,0:T(8,128)(2,1)}, /*index=5*/bf16[192,768]{1,0:T(8,128)(2,1)}) custom-call(bf16[2,192,768]{2,1,0:T(8,128)(2,1)} %bitcast.140, bf16[2,192,768]{2,1,0:T(8,128)(2,1)} %bitcast.142, ...), custom_call_target="tpu_custom_call" | custom-call | bytes 300000000 | tf_op jit(solution)/shard_map/sum_grads/pallas_call | solution.py:815
  622.4 2.4 slice.131
  626.3 2.0 fusion.52
  628.4 16.1 %swap_totals.1 = (bf16[192,768]{1,0:T(8,128)(2,1)}, bf16[192,768]{1,0:T(8,128)(2,1)}) custom-call(bf16[2,192,768]{2,1,0:T(8,128)(2,1)} %bitcast.136, bf16[2,192,768]{2,1,0:T(8,128)(2,1)} %bitcast.138), custom_call_target="tpu_custom_call" | custom-call | bytes 40000000 | tf_op jit(solution)/shard_map/swap_totals/pallas_call | solution.py:851
  644.5 5.2 place_sums.1
  (253 shorter events, 51.8 us)
Async XLA Ops:
  7.2 245.5 %all-gather.6.cloned.1.call-start = ((), (), s32[]{:S(2)}) async-start(), calls=%async_computation.5 | async-start | bytes 2949120 | tf_op jit(solution)/shard_map/all_gather | solution.py:1075
  7.2 18.1 %copy-start.60 = (bf16[192]{0:T(256)(128)(2,1)S(1)}, bf16[192]{0:T(256)(128)(2,1)}, u32[]{:S(2)}) copy-start(bf16[192]{0:T(256)(128)(2,1)} %param.22) | copy-start | bytes 1156
  7.2 18.2 %copy-start.61 = (bf16[192]{0:T(256)(128)(2,1)S(1)}, bf16[192]{0:T(256)(128)(2,1)}, u32[]{:S(2)}) copy-start(bf16[192]{0:T(256)(128)(2,1)} %param.17) | copy-start | bytes 1156
  7.2 18.3 %copy-start.49 = (bf16[192,20]{0,1:T(8,128)(2,1)S(1)}, bf16[192,20]{0,1:T(8,128)(2,1)}, u32[]{:S(2)}) copy-start(bf16[192,20]{0,1:T(8,128)(2,1)} %param.23) | copy-start | bytes 23044
  24.4 3.4 copy-start.35
  24.4 3.3 copy-start.42
  24.5 246.0 %all-gather.8.cloned.1.call-start = ((), (), s32[]{:S(2)}) async-start(), calls=%async_computation.6 | async-start | bytes 2949120 | tf_op jit(solution)/shard_map/all_gather | solution.py:1075
  24.5 4.3 copy-start.19
  25.2 262.9 %all-gather.10.cloned.1.call-start = ((), (), s32[]{:S(2)}) async-start(), calls=%async_computation.7 | async-start | bytes 2949120 | tf_op jit(solution)/shard_map/all_gather | solution.py:1075
  173.3 132.7 %all-gather.12.cloned.1.call-start = ((), (), s32[]{:S(2)}) async-start(), calls=%async_computation.8 | async-start | bytes 2949120 | tf_op jit(solution)/shard_map/all_gather | solution.py:1075
  173.9 149.9 %all-gather.14.cloned.1.call-start = ((), (), s32[]{:S(2)}) async-start(), calls=%async_computation.9 | async-start | bytes 2949120 | tf_op jit(solution)/shard_map/all_gather | solution.py:1075
  174.5 310.7 %reduce-scatter.6.cloned.1.call-start = ((), (), s32[]{:S(2)}) async-start(), calls=%async_computation.10 | async-start | bytes 2949120 | tf_op jit(solution)/shard_map/reduce_scatter | solution.py:1190
  192.6 4.5 slice-start.4
  341.9 143.3 %reduce-scatter.8.cloned.1.call-start = ((), (), s32[]{:S(2)}) async-start(), calls=%async_computation.11 | async-start | bytes 2949120 | tf_op jit(solution)/shard_map/reduce_scatter | solution.py:1190
  342.6 145.9 %reduce-scatter.10.cloned.1.call-start = ((), (), s32[]{:S(2)}) async-start(), calls=%async_computation.12 | async-start | bytes 2949120 | tf_op jit(solution)/shard_map/reduce_scatter | solution.py:1190
  343.4 285.0 %reduce-scatter.12.cloned.1.call-start = ((), (), s32[]{:S(2)}) async-start(), calls=%async_computation.13 | async-start | bytes 2949120 | tf_op jit(solution)/shard_map/reduce_scatter | solution.py:1190
  344.9 283.5 %reduce-scatter.14.cloned.1.call-start = ((), (), s32[]{:S(2)}) async-start(), calls=%async_computation.14 | async-start | bytes 2949120 | tf_op jit(solution)/shard_map/reduce_scatter | solution.py:1190
  345.0 105.5 %copy-start.36 = (f32[8,3,256]{2,1,0:T(4,128)}, f32[8,3,256]{2,1,0:T(4,128)S(1)}, u32[]{:S(2)}) copy-start(f32[8,3,256]{2,1,0:T(4,128)S(1)} %log_add_fusion) | copy-start | bytes 73732
  348.8 20.2 %copy-start.14 = (f32[8,256,128]{2,1,0:T(8,128)}, f32[8,256,128]{2,1,0:T(8,128)S(1)}, u32[]{:S(2)}) copy-start(f32[8,256,128]{2,1,0:T(8,128)S(1)} %dynamic_update_slice.3) | copy-start | bytes 3145732
  369.0 70.0 %copy-start.5 = (f32[256,1536]{1,0:T(8,128)S(1)}, f32[256,1536]{1,0:T(8,128)}, u32[]{:S(2)}) copy-start(f32[256,1536]{1,0:T(8,128)} %copy-done.4) | copy-start | bytes 4718596
  369.0 70.0 %copy-start.9 = (f32[4,2,192,128]{3,2,1,0:T(8,128)S(1)}, f32[4,2,192,128]{3,2,1,0:T(8,128)}, u32[]{:S(2)}) copy-start(f32[4,2,192,128]{3,2,1,0:T(8,128)} %get-tuple-element.74) | copy-start | bytes 2359300
  439.0 4.9 slice-start.6
  445.6 4.9 copy-start.12
  445.6 4.9 slice-start
  445.6 5.4 slice-start.1
  451.0 3.4 copy-start.23
  455.5 5.5 slice-start.2
  463.3 8.3 %copy-start.7 = (bf16[256,1536]{1,0:T(8,128)(2,1)S(1)}, bf16[256,1536]{1,0:T(8,128)(2,1)}, u32[]{:S(2)}) copy-start(bf16[256,1536]{1,0:T(8,128)(2,1)} %copy-done.6) | copy-start | bytes 2359300
  463.3 8.3 %copy-start.46 = (bf16[256,20]{0,1:T(8,128)(2,1)S(1)}, bf16[256,20]{0,1:T(8,128)(2,1)}, u32[]{:S(2)}) copy-start(bf16[256,20]{0,1:T(8,128)(2,1)} %copy-done.45) | copy-start | bytes 30724
  474.4 3.6 copy-start.16
  478.0 5.5 copy-start.24
  644.5 5.2 copy-start.26
  (48 other events, 76.2 us)
Sparse Core Ops, SparseCore 0:
  24.6 83.2 all-gather.5
  109.5 50.5 all-gather.7
  173.5 49.2 all-gather.9
  224.2 49.2 all-gather.11
  274.9 48.7 all-gather.13
  342.0 47.6 reduce-scatter.5
  392.0 47.0 reduce-scatter.7
  441.5 47.0 reduce-scatter.9
  490.9 47.0 reduce-scatter.11
  540.2 76.5 reduce-scatter.13

commit v2 on v1

--- a/solution.py
+++ b/solution.py
@@ -440,15 +440,15 @@
     return sent, local
 
 
-def exchange_halves(up, down, count):
+def exchange_halves(up, down, first, count):
     depth, inner = down.shape[1:]
     return pl.pallas_call(
-        functools.partial(halves_kernel, 0, count),
+        functools.partial(halves_kernel, first, count),
         out_shape=(jax.ShapeDtypeStruct((2, depth, 3 * inner // 2), up.dtype),) * count,
         in_specs=[pl.BlockSpec(memory_space=pltpu.VMEM)] * 2,
         out_specs=(pl.BlockSpec(memory_space=pl.ANY),) * count,
         scratch_shapes=[pltpu.SemaphoreType.DMA((3 * count,))] * 3,
-        compiler_params=pltpu.CompilerParams(collective_id=4, has_side_effects=True),
+        compiler_params=pltpu.CompilerParams(collective_id=4 if first == 0 else 6, has_side_effects=True),
         cost_estimate=pl.CostEstimate(flops=0, bytes_accessed=40_000_000, transcendentals=0),
         name="exchange_halves",
     )(up, down)
@@ -555,7 +555,6 @@
     place = Place()
     send = Sender(send_sem, recv_sem)
     x, y, c = place.x, place.y, place.c
-    rows = a_ref.shape[0]
     greet([place.to_x, place.to_y, place.to_c])
     local = [
         pltpu.make_async_copy(a_ref, a_out.at[c, x, y], copy_sem.at[0]),
@@ -565,6 +564,7 @@
         copy.start()
 
     def item(source, out):
+        rows = source.shape[0]
         return (
             lambda xx, yy, cc, half: out.at[cc, xx, yy, half_rows(half, rows)],
             lambda yy, half: source.at[half_rows(half, rows)],
@@ -666,63 +666,158 @@
     return results
 
 
-def rows_sum_kernel(
-    grad_ref, value_ref, dots_ref, grad_out, value_out, dots_out,
-    grad_held, value_held, dots_held, grad_c, value_c, dots_c,
-    grad_first, value_first, dots_first, grad_second, value_second, dots_second,
-    send_sem, recv_sem,
-):
+def combine_kernel(experts, experts_all, first_ref, *refs):
+    answer_refs, row_refs, dots_refs = (refs[i * experts : (i + 1) * experts] for i in range(3))
+    table_ref, outs, refs = refs[3 * experts], refs[3 * experts + 1 : 3 * experts + 4], refs[3 * experts + 4 :]
+    away, held, from_c, from_first, from_second = (refs[3 * i : 3 * i + 3] for i in range(5))
+    answer_buf, row_buf, fetch_sem, send_sem, recv_sem = refs[15:]
     place = Place()
     send = Sender(send_sem, recv_sem)
-    x, y = place.x, place.y
-    rows = grad_out.shape[0]
+    x, y, c = place.x, place.y, place.c
+    ox, oy, oc = place.ox, place.oy, place.oc
+    slot_rows = answer_refs[0].shape[1]
+    seq_len, width = outs[1].shape
+    dot_rows = outs[0].shape[0]
+    first = first_ref[0]
+    order = []
+    for dx, dy in ((1, 1), (1, 0), (0, 1), (0, 0)):
+        xx, yy = (ox if dx else x), (oy if dy else y)
+        order += [(xx, yy, oc), (xx, yy, c)]
+
+    def fetch(number):
+        xx, yy, cc = order[number]
+        seq = cc * 4 + xx * 2 + yy
+        slot = number % 2
+        copies = []
+        for expert in range(experts):
+            at = slice(expert * slot_rows, (expert + 1) * slot_rows)
+            for which, (source, buf) in enumerate(((row_refs, row_buf), (answer_refs, answer_buf))):
+                copies.append(
+                    pltpu.make_async_copy(
+                        source[expert].at[seq], buf.at[slot, at], fetch_sem.at[slot, 2 * expert + which]
+                    )
+                )
+        for copy in copies:
+            copy.start()
+        return copies
+
+    def compute(number, targets):
+        xx, yy, cc = order[number]
+        seq = cc * 4 + xx * 2 + yy
+        slot = number % 2
+        slot_ids = lax.broadcasted_iota(jnp.int32, (slot_rows, seq_len), 0).astype(jnp.float32)
+        dot_ids = lax.broadcasted_iota(jnp.int32, (dot_rows, seq_len), 0)
+        placings, combines = [], []
+        dots = jnp.zeros((dot_rows, seq_len), jnp.float32)
+        for expert in range(experts):
+            placing = (slot_ids == table_ref[seq, pl.ds(experts_all + first + expert, 1), :]).astype(jnp.float32)
+            placings.append(placing)
+            combines.append(placing * table_ref[seq, pl.ds(first + expert, 1), :])
+            dots = jnp.where(dot_ids == first + expert, dots_refs[expert][seq], dots)
+        placing = jnp.concatenate(placings, axis=0).astype(jnp.bfloat16)
+        combine = jnp.concatenate(combines, axis=0).astype(jnp.bfloat16)
+        targets[0][...] = dots
+        down = (((0,), (0,)), ((), ()))
+        for left, buf, target in ((placing, row_buf, targets[1]), (combine, answer_buf, targets[2])):
+            total = lax.dot_general(left, buf[slot], down, preferred_element_type=jnp.float32)
+            target[...] = total.astype(target.dtype)
+
+    heights = [out.shape[0] for out in outs]
+
+    def half(part, xx, yy, which):
+        return held[part].at[xx, yy, half_rows(which, heights[part])]
+
+    fetched = {0: fetch(0)}
     greet([place.to_x, place.to_y, place.to_c])
-
-    def part(ref, held, from_c, from_first, from_second):
-        return Part(
-            lambda xx, yy, cc: ref.at[cc, xx, yy],
-            lambda xx, yy, half: held.at[xx, yy, half_rows(half, rows)],
-            held, from_c, from_first, from_second,
-        )
-
-    parts = [
-        part(dots_ref, dots_held, dots_c, dots_first, dots_second),
-        part(grad_ref, grad_held, grad_c, grad_first, grad_second),
-        part(value_ref, value_held, value_c, value_first, value_second),
+    over = [[] for _ in outs]
+    for step in range(4):
+        for number in (2 * step, 2 * step + 1):
+            xx, yy, cc = order[number]
+            if number + 1 < len(order):
+                fetched[number + 1] = fetch(number + 1)
+            for copy in fetched.pop(number):
+                copy.wait()
+            if number % 2 == 0:
+                compute(number, [ref.at[xx, yy] for ref in away])
+                crossed = [
+                    send(away[part].at[xx, yy], from_c[part].at[xx, yy], place.to_c) for part in range(3)
+                ]
+            else:
+                compute(number, [ref.at[xx, yy] for ref in held])
+        for part in range(3):
+            crossed[part].wait_recv()
+            add_into(held[part].at[xx, yy], held[part].at[xx, yy], from_c[part].at[xx, yy])
+            first_got = from_first[part]
+            if step == 0:
+                over[part].append(send(half(part, xx, yy, 0), first_got.at[0, 1], place.to_y))
+                over[part].append(send(half(part, xx, yy, 1), first_got.at[1, 1], place.to_x))
+            elif step == 1:
+                over[part].append(send(half(part, xx, yy, 1), first_got.at[1, 0], place.to_x))
+            elif step == 2:
+                over[part].append(send(half(part, xx, yy, 0), first_got.at[0, 0], place.to_y))
+    second = []
+    for part in range(3):
+        a0, b0, b1, a1 = over[part]
+        a0.wait_recv()
+        add_into(half(part, ox, y, 0), half(part, ox, y, 0), from_first[part].at[0, 1])
+        a2 = send(half(part, ox, y, 0), from_second[part].at[0], place.to_x)
+        b0.wait_recv()
+        add_into(half(part, x, oy, 1), half(part, x, oy, 1), from_first[part].at[1, 1])
+        b2 = send(half(part, x, oy, 1), from_second[part].at[1], place.to_y)
+        second.append((a2, b2))
+    for part in range(3):
+        a0, b0, b1, a1 = over[part]
+        a1.wait_recv()
+        add_into(half(part, x, y, 0), half(part, x, y, 0), from_first[part].at[0, 0])
+        b1.wait_recv()
+        add_into(half(part, x, y, 1), half(part, x, y, 1), from_first[part].at[1, 0])
+    for part, (a2, b2) in enumerate(second):
+        for which, copy in enumerate((a2, b2)):
+            copy.wait_recv()
+            at = half_rows(which, heights[part])
+            add_into(outs[part].at[at], half(part, x, y, which), from_second[part].at[which])
+    send.finish()
+
+
+def combine_rows(first_own, answers, row_grads, dots, table, experts_all):
+    experts = len(answers)
+    seq_len = table.shape[2]
+    _, slot_rows, width = answers[0].shape
+    kinds = [
+        ((-(-experts_all // 32) * 32, seq_len), jnp.float32),
+        ((seq_len, width), jnp.bfloat16),
+        ((seq_len, width), jnp.bfloat16),
     ]
-    outs = [dots_out, grad_out, value_out]
-
-    def finish(number, part):
-        for half in (0, 1):
-            add_into(outs[number].at[half_rows(half, rows)], part.half(x, y, half), part.from_second.at[half])
-
-    add_in_plane(place, send, parts, finish)
-    send.finish()
-
-
-def sum_rows(grad, value, dots):
-    rows = grad.shape[3]
-    arrays = (grad, value, dots)
-
-    def scratch(lead, height):
-        return [pltpu.VMEM(lead + (height, a.shape[4]), a.dtype) for a in arrays]
+
+    def scratch(lead, cut=1):
+        return [pltpu.VMEM(lead + (shape[0] // cut, shape[1]), kind) for shape, kind in kinds]
 
     return pl.pallas_call(
-        rows_sum_kernel,
-        out_shape=tuple(jax.ShapeDtypeStruct(a.shape[3:], jnp.float32) for a in arrays),
-        in_specs=[pl.BlockSpec(memory_space=pltpu.VMEM)] * 3,
+        functools.partial(combine_kernel, experts, experts_all),
+        out_shape=tuple(jax.ShapeDtypeStruct(shape, jnp.float32) for shape, _ in kinds),
+        in_specs=[pl.BlockSpec(memory_space=pltpu.SMEM)]
+        + [pl.BlockSpec(memory_space=pl.ANY)] * (2 * experts)
+        + [pl.BlockSpec(memory_space=pltpu.VMEM)] * (experts + 1),
         out_specs=(pl.BlockSpec(memory_space=pltpu.VMEM),) * 3,
-        scratch_shapes=scratch((2, 2), rows)
-        + scratch((2, 2), rows)
-        + scratch((2, 2), rows // 2)
-        + scratch((2,), rows // 2)
-        + [pltpu.SemaphoreType.DMA((32,)), pltpu.SemaphoreType.DMA((32,))],
+        scratch_shapes=scratch((2, 2))
+        + scratch((2, 2))
+        + scratch((2, 2))
+        + scratch((2, 2), 2)
+        + scratch((2,), 2)
+        + [pltpu.VMEM((2, experts * slot_rows, width), jnp.bfloat16)] * 2
+        + [
+            pltpu.SemaphoreType.DMA((2, 2 * experts)),
+            pltpu.SemaphoreType.DMA((32,)),
+            pltpu.SemaphoreType.DMA((32,)),
+        ],
         compiler_params=pltpu.CompilerParams(
             collective_id=2, has_side_effects=True, vmem_limit_bytes=60 * 2**20
         ),
-        cost_estimate=pl.CostEstimate(flops=0, bytes_accessed=150_000_000, transcendentals=0),
-        name="sum_rows",
-    )(*arrays)
+        cost_estimate=pl.CostEstimate(
+            flops=32 * seq_len * width * experts * slot_rows, bytes_accessed=150_000_000, transcendentals=0
+        ),
+        name="combine_rows",
+    )(first_own, *answers, *row_grads, *dots, table)
 
 
 def grads_kernel(count, *refs):
@@ -846,7 +941,7 @@
     send.finish()
 
 
-def swap_totals(totals):
+def swap_totals(totals, collective):
     count = len(totals)
     return pl.pallas_call(
         functools.partial(swap_kernel, count),
@@ -854,7 +949,7 @@
         in_specs=[pl.BlockSpec(memory_space=pl.ANY)] * count,
         out_specs=(pl.BlockSpec(memory_space=pl.ANY),) * count,
         scratch_shapes=[pltpu.SemaphoreType.DMA((count,))] * 2,
-        compiler_params=pltpu.CompilerParams(collective_id=5, has_side_effects=True),
+        compiler_params=pltpu.CompilerParams(collective_id=collective, has_side_effects=True),
         cost_estimate=pl.CostEstimate(flops=0, bytes_accessed=40_000_000, transcendentals=0),
         name="swap_totals",
     )(*totals)
@@ -902,16 +997,23 @@
     )(side, *totals, *got)
 
 
-def expert_kernel(slots_ref, gates_ref, rows_ref, dout_ref, w_ref, answer_ref, row_ref, w_out, dots_ref, total, picked, picked_dout):
+def expert_kernel(
+    expert, experts_all, first_ref, table_ref, rows_ref, dout_ref, w_ref, answer_ref, row_ref, w_out, dots_ref,
+    total, picked, picked_dout,
+):
     group, slot_rows, width = answer_ref.shape
     half = w_ref.shape[1] // 3
     seq_len = rows_ref.shape[1]
     step = pl.program_id(0)
     slot_ids = lax.broadcasted_iota(jnp.int32, (slot_rows, seq_len), 0).astype(jnp.float32)
     gate_parts = []
+
+    def own_row(q, at):
+        return table_ref[q, pl.ds(at + first_ref[0] + expert, 1), :]
+
     for q in range(group):
-        placing = (slot_ids == slots_ref[q]).astype(jnp.float32)
-        gate_parts.append(jnp.sum(placing * gates_ref[q], axis=1, keepdims=True))
+        placing = (slot_ids == own_row(q, experts_all)).astype(jnp.float32)
+        gate_parts.append(jnp.sum(placing * own_row(q, 0), axis=1, keepdims=True))
         low = placing.astype(jnp.bfloat16)
         at = slice(q * slot_rows, (q + 1) * slot_rows)
         picked[at, :] = jnp.dot(low, rows_ref[q], preferred_element_type=jnp.float32).astype(jnp.bfloat16)
@@ -930,7 +1032,7 @@
     for q in range(group):
         at = slice(q * slot_rows, (q + 1) * slot_rows)
         answer_ref[q] = answer[at, :]
-        placing = (slot_ids == slots_ref[q]).astype(jnp.float32)
+        placing = (slot_ids == own_row(q, experts_all)).astype(jnp.float32)
         dots_ref[q] = jnp.sum(placing * dots[at, :], axis=0, keepdims=True)
     picked_dout[...] = (picked_dout[...].astype(jnp.float32) * gate).astype(jnp.bfloat16)
     active_grad = jnp.dot(picked_dout[...], w_ref[:, 2 * half :], preferred_element_type=jnp.float32)
@@ -963,17 +1065,18 @@
         w_out[...] = total[...].astype(w_out.dtype)
 
 
-def run_expert(slots, gates, rows, dout, weights, slot_rows):
+def run_expert(first_own, table, rows, dout, weights, expert, experts_all, slot_rows):
     count, seq_len, width = rows.shape
     group = count // 2
     wide = weights.shape[1]
     one = pl.BlockSpec((group, 1, seq_len), lambda i: (i, 0, 0))
+    listed = pl.BlockSpec((group,) + table.shape[1:], lambda i: (i, 0, 0))
     tall = pl.BlockSpec((group, seq_len, width), lambda i: (i, 0, 0))
     slot = pl.BlockSpec((group, slot_rows, width), lambda i: (i, 0, 0))
     whole = pl.BlockSpec(weights.shape, lambda i: (0, 0))
     flops = 2 * count * slot_rows * width * (2 * seq_len + 3 * wide)
     return pl.pallas_call(
-        expert_kernel,
+        functools.partial(expert_kernel, expert, experts_all),
         grid=(2,),
         out_shape=(
             jax.ShapeDtypeStruct((count, slot_rows, width), jnp.bfloat16),
@@ -981,7 +1084,7 @@
             jax.ShapeDtypeStruct(weights.shape, jnp.bfloat16),
             jax.ShapeDtypeStruct((count, 1, seq_len), jnp.float32),
         ),
-        in_specs=[one, one, tall, tall, whole],
+        in_specs=[pl.BlockSpec(memory_space=pltpu.SMEM), listed, tall, tall, whole],
         out_specs=(slot, slot, whole, one),
         scratch_shapes=[
             pltpu.VMEM(weights.shape, jnp.float32),
@@ -991,47 +1094,7 @@
         compiler_params=pltpu.CompilerParams(vmem_limit_bytes=60 * 2**20),
         cost_estimate=pl.CostEstimate(flops=flops, bytes_accessed=25_000_000, transcendentals=0),
         name="run_expert",
-    )(slots, gates, rows, dout, weights)
-
-
-def combine_kernel(experts, table_ref, *refs):
-    answers, rows = refs[:experts], refs[experts : 2 * experts]
-    value_ref, grad_ref = refs[2 * experts :]
-    slot_rows = answers[0].shape[1]
-    table = table_ref[0]
-    seq_len, lanes = table.shape
-    slot_ids = lax.broadcasted_iota(jnp.int32, (seq_len, slot_rows), 1).astype(jnp.float32)
-    placings, combines = [], []
-    for expert in range(experts):
-        placing = (slot_ids == table[:, experts + expert : experts + expert + 1]).astype(jnp.float32)
-        placings.append(placing)
-        combines.append(placing * table[:, expert : expert + 1])
-    placing = jnp.concatenate(placings, axis=1).astype(jnp.bfloat16)
-    combine = jnp.concatenate(combines, axis=1).astype(jnp.bfloat16)
-    answer = jnp.concatenate([ref[0] for ref in answers], axis=0)
-    row = jnp.concatenate([ref[0] for ref in rows], axis=0)
-    value_ref[0] = jnp.dot(combine, answer, preferred_element_type=jnp.float32).astype(value_ref.dtype)
-    grad_ref[0] = jnp.dot(placing, row, preferred_element_type=jnp.float32).astype(grad_ref.dtype)
-
-
-def combine_experts(table, answers, rows):
-    experts = len(answers)
-    count, slot_rows, width = answers[0].shape
-    seq_len = table.shape[1]
-    slot = pl.BlockSpec((1, slot_rows, width), lambda i: (i, 0, 0))
-    tall = pl.BlockSpec((1, seq_len, width), lambda i: (i, 0, 0))
-    return pl.pallas_call(
-        functools.partial(combine_kernel, experts),
-        grid=(count,),
-        out_shape=(jax.ShapeDtypeStruct((count, seq_len, width), jnp.bfloat16),) * 2,
-        in_specs=[pl.BlockSpec((1,) + table.shape[1:], lambda i: (i, 0, 0))] + [slot] * (2 * experts),
-        out_specs=(tall, tall),
-        compiler_params=pltpu.CompilerParams(vmem_limit_bytes=60 * 2**20),
-        cost_estimate=pl.CostEstimate(
-            flops=4 * count * seq_len * width * experts * slot_rows, bytes_accessed=40_000_000, transcendentals=0
-        ),
-        name="combine_experts",
-    )(table, *answers, *rows)
+    )(first_own, table, rows, dout, weights)
 
 
 def layer_on_device(
@@ -1067,7 +1130,7 @@
     x_at = lax.rem(shard_at, 2)
     depth = first_gain.shape[0]
 
-    early = 2
+    early = 3
     up_first = gate_up_weight.transpose(1, 0, 2)
     down_first = down_weight.transpose(1, 0, 2)
 
@@ -1076,8 +1139,11 @@
             halves.reshape(2 * depth, 3 * half_inner), SHARD, axis=0, tiled=True, axis_index_groups=along_z
         )
 
-    halves = exchange_halves(up_first, down_first, early)
-    expert_weights = [along(h) for h in halves]
+    halves = exchange_halves(up_first, down_first, 0, 1)
+    expert_weights = [along(halves[0])]
+    up_first, down_first, _ = lax.optimization_barrier((up_first, down_first, halves[0]))
+    halves = exchange_halves(up_first, down_first, 1, early - 1)
+    expert_weights += [along(h) for h in halves]
 
     position = jnp.arange(seq_len, dtype=jnp.int32)
     length = lengths[0]
@@ -1148,37 +1214,27 @@
     slot_of = jnp.where(routed > 0, rank_rows, -1.0)
     gate_low = gate_soft.astype(jnp.bfloat16).astype(jnp.float32)
     gate_full = jnp.sum(chosen * gate_low[:, :, None], axis=1)
+    listed = -(-2 * experts_all // 16) * 16
     table = jnp.concatenate(
-        [gate_full, slot_of, jnp.zeros((seq_len, 128 - 2 * experts_all), jnp.float32)], axis=1
-    )
+        [gate_full, slot_of, jnp.zeros((seq_len, listed - 2 * experts_all), jnp.float32)], axis=1
+    ).T
     rows_plane, table_plane = gather_rows(second_normed, table)
     rows_plane = rows_plane.reshape(8, seq_len, model_width)
-    table_plane = table_plane.reshape(8, seq_len, 128)
-    first_own = expert_at * local_experts
-    gates = lax.dynamic_slice_in_dim(table_plane, first_own, local_experts, axis=2)
-    slots = lax.dynamic_slice_in_dim(table_plane, experts_all + first_own, local_experts, axis=2)
-    own_table = jnp.concatenate(
-        [gates, slots, jnp.zeros((8, seq_len, 128 - 2 * local_experts), jnp.float32)], axis=2
-    )
-    gates_by = gates.transpose(2, 0, 1)[:, :, None, :]
-    slots_by = slots.transpose(2, 0, 1)[:, :, None, :]
+    table_plane = table_plane.reshape(8, listed, seq_len)
+    first_own = (expert_at * local_experts).astype(jnp.int32).reshape(1)
     slot_rows = -(-slot_count // 16) * 16
-    answers, row_grads, sums, dots = zip(
-        *(
-            run_expert(slots_by[e], gates_by[e], rows_plane, dout_plane, expert_weights[e], slot_rows)
-            for e in range(local_experts)
+    turn, results = first_own, []
+    for e in range(local_experts):
+        results.append(
+            run_expert(turn, table_plane, rows_plane, dout_plane, expert_weights[e], e, experts_all, slot_rows)
         )
-    )
-    sums = lax.optimization_barrier(tuple(sums) + (expert_weights[-1],))[:-1]
-    value_part, grad_part = combine_experts(own_table, answers, row_grads)
-    dots = jnp.stack([dot[:, 0, :] for dot in dots], axis=-1)
-    dot_part = lax.dynamic_update_slice_in_dim(jnp.zeros((8, seq_len, 128), jnp.float32), dots, first_own, axis=2)
-    plane = (2, 2, 2, seq_len)
-    grad_rows, value_rows, dot_rows = sum_rows(
-        grad_part.reshape(plane + (model_width,)),
-        value_part.reshape(plane + (model_width,)),
-        dot_part.reshape(plane + (128,)),
-    )
+        turn = lax.optimization_barrier((first_own, results[-1][3]))[0]
+    answers, row_grads, sums, dots = zip(*results)
+    sums = lax.optimization_barrier(tuple(sums[:-1])) + (sums[-1],)
+    dot_rows, grad_rows, value_rows = combine_rows(
+        first_own, answers, row_grads, dots, table_plane, experts_all
+    )
+    dot_rows = dot_rows.T
     output = (hidden + value_rows).astype(jnp.bfloat16)
     gate_grad = jnp.sum(chosen * dot_rows[:, None, :experts_all], axis=-1)
     inner_sum = jnp.sum(gate_soft * gate_grad, axis=-1, keepdims=True)
@@ -1238,15 +1294,17 @@
         ],
         axis=1,
     ).reshape(4, 2, depth, 128)
-    swapped = 3
+    swapped = 2
     small_sum, output_sum, mixer_sum, *got = sum_grads(
         small_terms,
         output_term.astype(jnp.bfloat16).reshape(4, 2, depth, output_weight.shape[1]),
         mixer_term.reshape(4, 2, depth, mixer_block.shape[1]),
         totals[:swapped],
     )
-    late = lax.optimization_barrier((small_sum,) + tuple(totals[swapped:]))[1:]
-    got += swap_totals(late)
+    late = lax.optimization_barrier((small_sum,) + tuple(totals[swapped:-1]))[1:]
+    got += swap_totals(late, 5)
+    last = lax.optimization_barrier((got[-1], totals[-1]))[1:]
+    got += swap_totals(last, 7)
     both_sums, down_sums = place_sums(x_at.reshape(1), totals, got)
     return (
         output,

time: 667 us -> 623 us (0.934)
  local copies, waits for them, and re-layouts: 46.9 us -> 27.1 us
  Pallas kernels: 531 us -> 513 us
    pallas_call x1, Pallas kernels: 143 us -> 127 us  [gather_weights(): pl.pallas_call(functools.partial(weights_kernel, first, count), out_shape...]
    pallas_call x8, Pallas kernels: 195 us -> 185 us  [the longest x5 94.5 us: run_expert(): pl.pallas_call(functools.partial(expert_kernel, expert, experts_all), gri...]
    pallas_call x1 -> x2, Pallas kernels: 16.1 us -> 25.6 us  [swap_totals(): pl.pallas_call(functools.partial(swap_kernel, count), out_shape=tuple((ja...]
  transfers between devices with their start and end apart: 10 -> 10, of which waited for: 1 -> 0; matrix products, arithmetic and copies ran while one was open for 14% -> 12% of each run, Pallas kernels for 72% -> 79%
where the time goes in v2:
time: 623 us; the launch traced here: 620 us
  Pallas kernels  513 us (82%)
  matrix products  40.5 us (7%)
  local copies, waits for them, and re-layouts  27.1 us (4%)
  other arithmetic  19.3 us (3%)
  between operations  16.3 us (3%)
    pallas_call x1, Pallas kernels, sum_grads(): pl.pallas_call(functools.partial(grads_kernel, count), out_shape=tuple((j...  134 us
    pallas_call x1, Pallas kernels, gather_weights(): pl.pallas_call(functools.partial(weights_kernel, first, count), out_shape...  127 us
    pallas_call x5, Pallas kernels, run_expert(): pl.pallas_call(functools.partial(expert_kernel, expert, experts_all), gri...  94.5 us
    pallas_call x1, Pallas kernels, combine_rows(): pl.pallas_call(functools.partial(combine_kernel, experts, experts_all), o...  63.9 us
    dot_general x16, matrix products, product(): return jnp.einsum(form, left, right, preferred_element_type=jnp.float32)  40.5 us
    pallas_call x1, Pallas kernels, gather_rows(): pl.pallas_call(rows_kernel, out_shape=(jax.ShapeDtypeStruct((2, 2, 2) + a...  35.6 us
    pallas_call x2, Pallas kernels, exchange_halves(): pl.pallas_call(functools.partial(halves_kernel, first, count), out_shape=...  27.1 us
    pallas_call x2, Pallas kernels, swap_totals(): pl.pallas_call(functools.partial(swap_kernel, count), out_shape=tuple((ja...  25.6 us
  transfers between devices with their start and end apart: 10, of which 0 were waited for; matrix products, arithmetic and copies ran while one was open for 12% of the time, Pallas kernels for 79%

profile of v2, /device:TPU:10, one launch (start us, length us, event | category | flops | bytes accessed | tf_op | source)
XLA Modules:
  0.0 619.6 jit_solution(14130477600201926131)
XLA Ops:
  7.2 10.8 %exchange_halves.2 = bf16[2,192,768]{2,1,0:T(8,128)(2,1)} custom-call(bf16[5,192,1024]{2,1,0:T(8,128)(2,1)} %bitcast.109, bf16[5,192,512]{2,1,0:T(8,128)(2,1)} %bitcast.115), custom_call_target="tpu_custom_call" | custom-call | bytes 40000000 | tf_op jit(solution)/shard_map/exchange_halves/pallas_call | solution.py:445
  18.1 16.3 %exchange_halves.3 = (bf16[2,192,768]{2,1,0:T(8,128)(2,1)}, bf16[2,192,768]{2,1,0:T(8,128)(2,1)}) custom-call(bf16[5,192,1024]{2,1,0:T(8,128)(2,1)} %bitcast.110, bf16[5,192,512]{2,1,0:T(8,128)(2,1)} %bitcast.116), custom_call_target="tpu_custom_call" | custom-call | bytes 40000000 | tf_op jit(solution)/shard_map/exchange_halves/pallas_call | solution.py:445
  39.3 127.4 %gather_weights.1 = (bf16[4,2,192,2560]{3,2,1,0:T(8,128)(2,1)}, bf16[4,2,192,1536]{3,2,1,0:T(8,128)(2,1)}, f32[4,2,192,128]{3,2,1,0:T(8,128)}, bf16[2,2,2,256,15...) custom-call(bf16[5,192,1024]{2,1,0:T(8,128)(2,1)} %bitcast.111, ...), custom_call_target="tpu_custom_call" | custom-call | bytes 200000000 | tf_op jit(solution)/shard_map/gather_weights/pallas_call | solution.py:535
  168.8 5.6 fusion.35
  177.7 1.6 copy.91
  180.6 1.7 subtract_convert_fusion.1
  184.7 2.0 copy-done
  188.4 1.5 multiply_reduce_fusion.2
  197.1 35.6 %gather_rows.1 = (bf16[2,2,2,256,1536]{4,3,2,1,0:T(8,128)(2,1)}, f32[2,2,2,48,256]{4,3,2,1,0:T(8,128)}) custom-call(bf16[256,1536]{1,0:T(8,128)(2,1)} %copy-done.4, f32[48,256]{1,0:T(8,128)} %maximum_bitcast_fusion.3.b_ref), custom_call_target="tpu_custom_call" | custom-call | bytes 90000000 | tf_op jit(solution)/shard_map/gather_rows/pallas_call | solution.py:582
  232.8 19.0 %run_expert.5 = (bf16[8,112,1536]{2,1,0:T(8,128)(2,1)}, bf16[8,112,1536]{2,1,0:T(8,128)(2,1)}, bf16[1536,768]{1,0:T(8,128)(2,1)}, f32[8,1,256]{2,1,0:T(1,128)}) custom-call(s32[1]{0:T(128)} %bitcast.20.first_ref, f32[8,48,256]{2,1,0:T(8,128)} %bitcast.154, bf16[8,256,1536]{2,1,0:T(8,128)(2,1)} %bitcast.170, bf16[8,256,1536]{2,1,0:T(8,128)(2,1)} %bitcast.165, ...), custom_call_target="tpu_custom_call" | custom-call | flops 7751073792 | bytes 25000000 | tf_op jit(solution)/shard_map/run_expert/pallas_call | solution.py:1078
  251.8 18.6 %run_expert.6 = (bf16[8,112,1536]{2,1,0:T(8,128)(2,1)}, bf16[8,112,1536]{2,1,0:T(8,128)(2,1)}, bf16[1536,768]{1,0:T(8,128)(2,1)}, f32[8,1,256]{2,1,0:T(1,128)}) custom-call(s32[1]{0:T(128)} %bitcast.20.first_ref, f32[8,48,256]{2,1,0:T(8,128)} %bitcast.155, bf16[8,256,1536]{2,1,0:T(8,128)(2,1)} %bitcast.171, bf16[8,256,1536]{2,1,0:T(8,128)(2,1)} %bitcast.166, ...), custom_call_target="tpu_custom_call" | custom-call | flops 7751073792 | bytes 25000000 | tf_op jit(solution)/shard_map/run_expert/pallas_call | solution.py:1078
  270.4 19.2 %run_expert.7 = (bf16[8,112,1536]{2,1,0:T(8,128)(2,1)}, bf16[8,112,1536]{2,1,0:T(8,128)(2,1)}, bf16[1536,768]{1,0:T(8,128)(2,1)}, f32[8,1,256]{2,1,0:T(1,128)}) custom-call(s32[1]{0:T(128)} %bitcast.20.first_ref, f32[8,48,256]{2,1,0:T(8,128)} %bitcast.156, bf16[8,256,1536]{2,1,0:T(8,128)(2,1)} %bitcast.172, bf16[8,256,1536]{2,1,0:T(8,128)(2,1)} %bitcast.167, ...), custom_call_target="tpu_custom_call" | custom-call | flops 7751073792 | bytes 25000000 | tf_op jit(solution)/shard_map/run_expert/pallas_call | solution.py:1078
  289.6 18.5 %run_expert.8 = (bf16[8,112,1536]{2,1,0:T(8,128)(2,1)}, bf16[8,112,1536]{2,1,0:T(8,128)(2,1)}, bf16[1536,768]{1,0:T(8,128)(2,1)}, f32[8,1,256]{2,1,0:T(1,128)}) custom-call(s32[1]{0:T(128)} %bitcast.20.first_ref, f32[8,48,256]{2,1,0:T(8,128)} %bitcast.157, bf16[8,256,1536]{2,1,0:T(8,128)(2,1)} %bitcast.173, bf16[8,256,1536]{2,1,0:T(8,128)(2,1)} %bitcast.168, ...), custom_call_target="tpu_custom_call" | custom-call | flops 7751073792 | bytes 25000000 | tf_op jit(solution)/shard_map/run_expert/pallas_call | solution.py:1078
  310.5 19.3 %run_expert.9 = (bf16[8,112,1536]{2,1,0:T(8,128)(2,1)}, bf16[8,112,1536]{2,1,0:T(8,128)(2,1)}, bf16[1536,768]{1,0:T(8,128)(2,1)}, f32[8,1,256]{2,1,0:T(1,128)}) custom-call(s32[1]{0:T(128)} %bitcast.20.first_ref, f32[8,48,256]{2,1,0:T(8,128)} %bitcast.158, bf16[8,256,1536]{2,1,0:T(8,128)(2,1)} %bitcast.174, bf16[8,256,1536]{2,1,0:T(8,128)(2,1)} %bitcast.169, ...), custom_call_target="tpu_custom_call" | custom-call | flops 7751073792 | bytes 25000000 | tf_op jit(solution)/shard_map/run_expert/pallas_call | solution.py:1078
  329.8 63.9 %combine_rows.1 = (f32[32,256]{1,0:T(8,128)}, f32[256,1536]{1,0:T(8,128)}, f32[256,1536]{1,0:T(8,128)}) custom-call(s32[1]{0:T(128)} %bitcast.20.first_ref, bf16[8,112,1536]{2,1,0:T(8,128)(2,1)} %get-tuple-element.84.refs_0_, bf16[8,112,1536]{2,1,0:T(8,128)(2,1)} %get-tuple-element.87.refs_1_, bf16[8,112,1536]{2,1,0:T(8,128)(2,1)} %get-tuple-element.90.refs_2_, ...), custom_call_target="tpu_custom_call" | custom-call | flops 7046430720 | bytes 150000000 | tf_op jit(solution)/shard_map/combine_rows/pallas_call | solution.py:795
  394.7 2.2 multiply_reduce_fusion
  401.9 4.8 fusion
  406.8 1.7 fusion.2
  411.0 1.5 concatenate.58
  412.5 2.8 convolution_multiply_fusion
  418.0 6.8 %fusion.19 = (f32[1536]{0:T(1024)S(1)}, f32[256]{0:T(256)S(1)}, f32[256,1536]{1,0:T(8,128)}) fusion(bf16[256,1536]{1,0:T(8,128)(2,1)S(1)} %copy-done.10, f32[256]{0:T(256)S(1)} %copy-done.54, f32[1536]{0:T(1024)S(1)} %get-tuple-element.178, bf16[1536,2560]{1,0:T(8,128)(2,1)} %bitcast.164, bf16[256,512]{0,1:T(8,128)(2,1)S(1)} %bitcast.141, ...), kind=kOutput, calls=%fused_computation.33 | convolution fusion | flops 2019948800 | bytes 11548672 | tf_op jit(solution)/shard_map/sf,df->sd/dot_general | solution.py:19
  427.5 1.6 maximum_maximum_fusion.refs_2_
  429.1 3.7 convolution_convert_fusion.1
  432.8 5.6 convolution_convert_fusion
  438.3 1.6 fusion.15
  440.0 133.6 %sum_grads.1 = (f32[192,128]{1,0:T(8,128)}, f32[192,1536]{1,0:T(8,128)}, f32[192,2560]{1,0:T(8,128)}, bf16[192,768]{1,0:T(8,128)(2,1)}, bf16[192,768]{1,0:T(8,128)(2,1)}) custom-call(bf16[2,192,768]{2,1,0:T(8,128)(2,1)} %bitcast.125, bf16[2,192,768]{2,1,0:T(8,128)(2,1)} %bitcast.127, f32[4,2,192,128]{3,2,1,0:T(8,128)} %maximum_maximum_fusion.refs_2_, ...), custom_call_target="tpu_custom_call" | custom-call | bytes 300000000 | tf_op jit(solution)/shard_map/sum_grads/pallas_call | solution.py:910
  573.6 1.6 copy.101
  575.2 2.4 slice.81
  577.6 16.4 %swap_totals.2 = (bf16[192,768]{1,0:T(8,128)(2,1)}, bf16[192,768]{1,0:T(8,128)(2,1)}) custom-call(bf16[2,192,768]{2,1,0:T(8,128)(2,1)} %bitcast.129, bf16[2,192,768]{2,1,0:T(8,128)(2,1)} %bitcast.131), custom_call_target="tpu_custom_call" | custom-call | bytes 40000000 | tf_op jit(solution)/shard_map/swap_totals/pallas_call | solution.py:946
  594.8 2.0 fusion.52
  596.8 9.2 %swap_totals.3.refs_9_ = bf16[192,768]{1,0:T(8,128)(2,1)} custom-call(bf16[2,192,768]{2,1,0:T(8,128)(2,1)} %bitcast.133), custom_call_target="tpu_custom_call" | custom-call | bytes 40000000 | tf_op jit(solution)/shard_map/swap_totals/pallas_call | solution.py:946
  606.0 5.2 place_sums.1
  (240 shorter events, 39.7 us)
Async XLA Ops:
  7.2 225.6 %all-gather.6.cloned.1.call-start = ((), (), s32[]{:S(2)}) async-start(), calls=%async_computation.5 | async-start | bytes 2949120 | tf_op jit(solution)/shard_map/all_gather | solution.py:1138
  18.0 17.9 %copy-start.64 = (bf16[192]{0:T(256)(128)(2,1)S(1)}, bf16[192]{0:T(256)(128)(2,1)}, u32[]{:S(2)}) copy-start(bf16[192]{0:T(256)(128)(2,1)} %param.17) | copy-start | bytes 1156
  18.0 17.9 %copy-start.65 = (bf16[192]{0:T(256)(128)(2,1)S(1)}, bf16[192]{0:T(256)(128)(2,1)}, u32[]{:S(2)}) copy-start(bf16[192]{0:T(256)(128)(2,1)} %param.22) | copy-start | bytes 1156
  18.0 18.2 %copy-start.59 = (bf16[192,20]{0,1:T(8,128)(2,1)S(1)}, bf16[192,20]{0,1:T(8,128)(2,1)}, u32[]{:S(2)}) copy-start(bf16[192,20]{0,1:T(8,128)(2,1)} %param.23) | copy-start | bytes 23044
  18.0 233.7 %all-gather.8.cloned.1.call-start = ((), (), s32[]{:S(2)}) async-start(), calls=%async_computation.6 | async-start | bytes 2949120 | tf_op jit(solution)/shard_map/all_gather | solution.py:1138
  34.5 235.9 %all-gather.10.cloned.1.call-start = ((), (), s32[]{:S(2)}) async-start(), calls=%async_computation.7 | async-start | bytes 2949120 | tf_op jit(solution)/shard_map/all_gather | solution.py:1138
  35.2 254.4 %all-gather.12.cloned.1.call-start = ((), (), s32[]{:S(2)}) async-start(), calls=%async_computation.8 | async-start | bytes 2949120 | tf_op jit(solution)/shard_map/all_gather | solution.py:1138
  39.3 128.3 %copy-start.9 = (bf16[256,1536]{1,0:T(8,128)(2,1)S(1)}, bf16[256,1536]{1,0:T(8,128)(2,1)}, u32[]{:S(2)}) copy-start(bf16[256,1536]{1,0:T(8,128)(2,1)} %param.13) | copy-start | bytes 2359300
  166.7 143.8 %all-gather.14.cloned.1.call-start = ((), (), s32[]{:S(2)}) async-start(), calls=%async_computation.9 | async-start | bytes 2949120 | tf_op jit(solution)/shard_map/all_gather | solution.py:1138
  167.3 272.7 %reduce-scatter.6.cloned.1.call-start = ((), (), s32[]{:S(2)}) async-start(), calls=%async_computation.10 | async-start | bytes 2949120 | tf_op jit(solution)/shard_map/reduce_scatter | solution.py:1246
  168.7 21.3 %copy-start.47 = (f32[1536]{0:T(1024)}, f32[1536]{0:T(1024)S(1)}, u32[]{:S(2)}) copy-start(f32[1536]{0:T(1024)S(1)} %get-tuple-element.177) | copy-start | bytes 18436
  191.1 6.0 copy-start.4
  308.2 131.8 %reduce-scatter.8.cloned.1.call-start = ((), (), s32[]{:S(2)}) async-start(), calls=%async_computation.11 | async-start | bytes 2949120 | tf_op jit(solution)/shard_map/reduce_scatter | solution.py:1246
  308.9 264.6 %reduce-scatter.10.cloned.1.call-start = ((), (), s32[]{:S(2)}) async-start(), calls=%async_computation.12 | async-start | bytes 2949120 | tf_op jit(solution)/shard_map/reduce_scatter | solution.py:1246
  309.7 263.9 %reduce-scatter.12.cloned.1.call-start = ((), (), s32[]{:S(2)}) async-start(), calls=%async_computation.13 | async-start | bytes 2949120 | tf_op jit(solution)/shard_map/reduce_scatter | solution.py:1246
  310.4 286.4 %reduce-scatter.14.cloned.1.call-start = ((), (), s32[]{:S(2)}) async-start(), calls=%async_computation.14 | async-start | bytes 2949120 | tf_op jit(solution)/shard_map/reduce_scatter | solution.py:1246
  329.8 64.7 %copy-start.46 = (s32[256,8]{0,1:T(8,128)S(1)}, s32[256,8]{0,1:T(8,128)}, u32[]{:S(2)}) copy-start(s32[256,8]{0,1:T(8,128)} %param.15) | copy-start | bytes 24580
  329.8 64.7 %copy-start.52 = (f32[256]{0:T(256)S(1)}, f32[256]{0:T(256)}, u32[]{:S(2)}) copy-start(f32[256]{0:T(256)} %reduce_max.19) | copy-start | bytes 3076
  329.8 64.7 %copy-start.56 = (f32[256]{0:T(256)S(1)}, f32[256]{0:T(256)}, u32[]{:S(2)}) copy-start(f32[256]{0:T(256)} %copy-done.55) | copy-start | bytes 3076
  329.8 64.8 %copy-start.8 = (f32[4,2,192,128]{3,2,1,0:T(8,128)S(1)}, f32[4,2,192,128]{3,2,1,0:T(8,128)}, u32[]{:S(2)}) copy-start(f32[4,2,192,128]{3,2,1,0:T(8,128)} %get-tuple-element.78) | copy-start | bytes 2359300
  329.8 64.8 %copy-start.48 = (f32[1536]{0:T(1024)S(1)}, f32[1536]{0:T(1024)}, u32[]{:S(2)}) copy-start(f32[1536]{0:T(1024)} %copy-done.47) | copy-start | bytes 18436
  329.8 64.8 %copy-start.58 = (f32[256]{0:T(256)S(1)}, f32[256]{0:T(256)}, u32[]{:S(2)}) copy-start(f32[256]{0:T(256)} %copy-done.57) | copy-start | bytes 3076
  394.7 4.9 slice-start.6
  401.2 5.5 copy-start.11
  401.2 5.5 slice-start
  401.9 4.9 slice-start.1
  410.1 5.5 slice-start.2
  418.0 8.3 %copy-start.5 = (bf16[256,1536]{1,0:T(8,128)(2,1)S(1)}, bf16[256,1536]{1,0:T(8,128)(2,1)}, u32[]{:S(2)}) copy-start(bf16[256,1536]{1,0:T(8,128)(2,1)} %copy-done.4) | copy-start | bytes 2359300
  418.0 8.3 %copy-start.50 = (bf16[256,20]{0,1:T(8,128)(2,1)S(1)}, bf16[256,20]{0,1:T(8,128)(2,1)}, u32[]{:S(2)}) copy-start(bf16[256,20]{0,1:T(8,128)(2,1)} %copy-done.49) | copy-start | bytes 30724
  432.7 5.6 copy-start.20
  575.2 18.8 %copy-start.25 = (f32[192,128]{1,0:T(8,128)S(1)}, f32[192,128]{1,0:T(8,128)}, u32[]{:S(2)}) copy-start(f32[192,128]{1,0:T(8,128)} %get-tuple-element.114) | copy-start | bytes 294916
  606.0 5.2 copy-start.22
  (52 other events, 99.6 us)
Sparse Core Ops, SparseCore 0:
  18.1 76.8 all-gather.5
  96.5 50.4 all-gather.7
  148.7 48.7 all-gather.9
  198.9 48.7 all-gather.11
  249.1 48.7 all-gather.13
  308.3 46.2 reduce-scatter.5
  356.9 47.0 reduce-scatter.7
  406.3 47.0 reduce-scatter.9
  455.7 60.8 reduce-scatter.11
  518.8 57.8 reduce-scatter.13

commit v3 on v2

--- a/solution.py
+++ b/solution.py
@@ -403,13 +403,12 @@
     return pl.ds(0, rows) if half is None else pl.ds(half * (rows // 2), rows // 2)
 
 
-def halves_kernel(first, count, *refs):
-    up_ref, down_ref = refs[:2]
-    outs, (send_sem, recv_sem, copy_sem) = refs[2 : 2 + count], refs[2 + count :]
+def halves_kernel(first, *refs):
+    up_ref, down_ref, out, send_sem, recv_sem, copy_sem = refs
     place = Place()
     send = Sender(send_sem, recv_sem)
     greet([place.to_x])
-    sent, local = start_halves(place, send, copy_sem, up_ref, down_ref, outs, first)
+    sent, local = start_halves(place, send, copy_sem, up_ref, down_ref, out, first)
     for copy in sent:
         copy.wait_recv()
     for copy in local:
@@ -417,12 +416,12 @@
     send.finish()
 
 
-def start_halves(place, send, copy_sem, up_ref, down_ref, outs, first):
+def start_halves(place, send, copy_sem, up_ref, down_ref, out_ref, first):
     x, ox = place.x, place.ox
     half = down_ref.shape[2] // 2
     sent, local = [], []
-    for number, out in enumerate(outs):
-        expert = first + number
+    for number in range(out_ref.shape[0]):
+        out, expert = out_ref.at[number], first + number
 
         def pieces(xx):
             at = pl.ds(pl.multiple_of(xx * half, half), half)
@@ -443,10 +442,10 @@
 def exchange_halves(up, down, first, count):
     depth, inner = down.shape[1:]
     return pl.pallas_call(
-        functools.partial(halves_kernel, first, count),
-        out_shape=(jax.ShapeDtypeStruct((2, depth, 3 * inner // 2), up.dtype),) * count,
+        functools.partial(halves_kernel, first),
+        out_shape=jax.ShapeDtypeStruct((count, 2, depth, 3 * inner // 2), up.dtype),
         in_specs=[pl.BlockSpec(memory_space=pltpu.VMEM)] * 2,
-        out_specs=(pl.BlockSpec(memory_space=pl.ANY),) * count,
+        out_specs=pl.BlockSpec(memory_space=pl.ANY),
         scratch_shapes=[pltpu.SemaphoreType.DMA((3 * count,))] * 3,
         compiler_params=pltpu.CompilerParams(collective_id=4 if first == 0 else 6, has_side_effects=True),
         cost_estimate=pl.CostEstimate(flops=0, bytes_accessed=40_000_000, transcendentals=0),
@@ -455,9 +454,9 @@
 
 
 def weights_kernel(
-    first, count, up_ref, down_ref, w_ref, o_ref, small_ref, rows_ref, w_out, o_out, small_out, rows_out, *refs
+    first, up_ref, down_ref, w_ref, o_ref, small_ref, rows_ref, w_out, o_out, small_out, rows_out, halves_out,
+    send_sem, recv_sem, copy_sem, half_sem,
 ):
-    outs, (send_sem, recv_sem, copy_sem, half_sem) = refs[:count], refs[count:]
     place = Place()
     send = Sender(send_sem, recv_sem)
     x, y, c, z = place.x, place.y, place.c, place.z
@@ -518,7 +517,7 @@
             items.append((view, lambda yy, half, view=view: view(x, yy, c, half), [copy], False))
     items.append((rows_view, lambda yy, half: rows_ref.at[half_rows(half, blocks)], [], False))
     sent, kept = gather_in_plane(
-        place, send, items, lambda: start_halves(place, send, half_sem, up_ref, down_ref, outs, first)
+        place, send, items, lambda: start_halves(place, send, half_sem, up_ref, down_ref, halves_out, first)
     )
     for copy in sent:
         copy.wait_recv()
@@ -533,12 +532,12 @@
     copies = 128
     arrays = (w, o, small)
     return pl.pallas_call(
-        functools.partial(weights_kernel, first, count),
+        functools.partial(weights_kernel, first),
         out_shape=tuple(jax.ShapeDtypeStruct((4, 2) + a.shape, a.dtype) for a in arrays)
         + (jax.ShapeDtypeStruct((2, 2, 2) + rows.shape, rows.dtype),)
-        + (jax.ShapeDtypeStruct((2, depth, 3 * inner // 2), up.dtype),) * count,
+        + (jax.ShapeDtypeStruct((count, 2, depth, 3 * inner // 2), up.dtype),),
         in_specs=[pl.BlockSpec(memory_space=pltpu.VMEM)] * 6,
-        out_specs=(pl.BlockSpec(memory_space=pl.ANY),) * (4 + count),
+        out_specs=(pl.BlockSpec(memory_space=pl.ANY),) * 5,
         scratch_shapes=[
             pltpu.SemaphoreType.DMA((copies,)),
             pltpu.SemaphoreType.DMA((copies,)),
@@ -613,57 +612,6 @@
         return carry
 
     lax.fori_loop(0, count, body, 0)
-
-
-class Part:
-    def __init__(self, take, half, held, from_c, from_first, from_second):
-        self.take, self.half, self.held, self.from_c = take, half, held, from_c
-        self.from_first, self.from_second = from_first, from_second
-
-
-def add_in_plane(place, send, parts, finish):
-    x, y, c = place.x, place.y, place.c
-    ox, oy, oc = place.ox, place.oy, place.oc
-    from_core = []
-    for part in parts:
-        copies = {}
-        for dx, dy in ((1, 1), (1, 0), (0, 1), (0, 0)):
-            xx, yy = (ox if dx else x), (oy if dy else y)
-            copies[dx, dy] = send(part.take(xx, yy, oc), part.from_c.at[xx, yy], place.to_c)
-        from_core.append(copies)
-    over = []
-    for part, copies in zip(parts, from_core):
-        for dx, dy in ((1, 1), (1, 0), (0, 1), (0, 0)):
-            xx, yy = (ox if dx else x), (oy if dy else y)
-            copies[dx, dy].wait_recv()
-            add_into(part.held.at[xx, yy], part.take(xx, yy, c), part.from_c.at[xx, yy])
-            if (dx, dy) == (1, 1):
-                a0 = send(part.half(xx, yy, 0), part.from_first.at[0, 1], place.to_y)
-                b0 = send(part.half(xx, yy, 1), part.from_first.at[1, 1], place.to_x)
-            elif (dx, dy) == (1, 0):
-                b1 = send(part.half(xx, yy, 1), part.from_first.at[1, 0], place.to_x)
-            elif (dx, dy) == (0, 1):
-                a1 = send(part.half(xx, yy, 0), part.from_first.at[0, 0], place.to_y)
-        over.append((a0, b0, a1, b1))
-    second = []
-    for part, (a0, b0, a1, b1) in zip(parts, over):
-        a0.wait_recv()
-        add_into(part.half(ox, y, 0), part.half(ox, y, 0), part.from_first.at[0, 1])
-        a2 = send(part.half(ox, y, 0), part.from_second.at[0], place.to_x)
-        b0.wait_recv()
-        add_into(part.half(x, oy, 1), part.half(x, oy, 1), part.from_first.at[1, 1])
-        b2 = send(part.half(x, oy, 1), part.from_second.at[1], place.to_y)
-        a1.wait_recv()
-        add_into(part.half(x, y, 0), part.half(x, y, 0), part.from_first.at[0, 0])
-        b1.wait_recv()
-        add_into(part.half(x, y, 1), part.half(x, y, 1), part.from_first.at[1, 0])
-        second.append((a2, b2))
-    results = []
-    for number, (part, (a2, b2)) in enumerate(zip(parts, second)):
-        a2.wait_recv()
-        b2.wait_recv()
-        results.append(finish(number, part))
-    return results
 
 
 def combine_kernel(experts, experts_all, first_ref, *refs):
@@ -820,78 +768,119 @@
     )(first_own, *answers, *row_grads, *dots, table)
 
 
-def grads_kernel(count, *refs):
+def grads_kernel(count, cuts, *refs):
     total_refs, refs = refs[:count], refs[count:]
     ins, refs = refs[:3], refs[3:]
     outs, got_refs, refs = refs[:3], refs[3 : 3 + count], refs[3 + count :]
-    held, from_c, from_first, from_second, own, from_z, alls = (refs[3 * i : 3 * i + 3] for i in range(7))
-    send_sem, recv_sem = refs[21:]
+    many = len(cuts)
+    held, from_c, from_first, from_second, own, from_z, alls = (refs[many * i : many * (i + 1)] for i in range(7))
+    send_sem, recv_sem = refs[7 * many :]
     place = Place()
     send = Sender(send_sem, recv_sem)
     x, y, c, z = place.x, place.y, place.c, place.z
+    ox, oy, oc = place.ox, place.oy, place.oc
     greet([place.to_x, place.to_y, place.to_c] + place.to_z[1:])
     depth = ins[1].shape[2]
     piece = depth // 4
-    heights = [piece, depth, depth]
-
-    def take(number):
-        ref = ins[number]
+    order = [(ox, oy), (ox, y), (x, oy), (x, y)]
+
+    def take(part, xx, yy, cc):
+        number, start, wide = cuts[part]
+        ref, quarter = ins[number], yy * 2 + cc
         if number == 0:
-            return lambda xx, yy, cc: ref.at[:, xx, pl.ds(pl.multiple_of((yy * 2 + cc) * piece, piece), piece)]
-        wide = ref.shape[3] // 4
-        return lambda xx, yy, cc: ref.at[:, xx, :, pl.ds(pl.multiple_of((yy * 2 + cc) * wide, wide), wide)]
-
-    def half_of(number):
-        return lambda xx, yy, half: held[number].at[xx, yy, :, half_rows(half, heights[number])]
-
-    parts = [
-        Part(take(i), half_of(i), held[i], from_c[i], from_first[i], from_second[i]) for i in range(3)
+            return ref.at[:, xx, pl.ds(pl.multiple_of(quarter * piece, piece), piece)]
+        at = pl.multiple_of(quarter * (ref.shape[3] // 4) + start, 128)
+        return ref.at[:, xx, :, pl.ds(at, wide)]
+
+    def half(part, xx, yy, which):
+        return held[part].at[xx, yy, :, half_rows(which, own[part].shape[1])]
+
+    crossed = [
+        [send(take(part, xx, yy, oc), from_c[part].at[xx, yy], place.to_c) for xx, yy in order]
+        for part in range(many)
     ]
-
-    def finish(number, part):
-        for half in (0, 1):
-            add_into(
-                own[number].at[:, half_rows(half, heights[number])],
-                part.half(x, y, half),
-                part.from_second.at[half],
-            )
-        return [send(own[number].at[place.zs[d]], from_z[number].at[d - 1], place.to_z[d]) for d in (1, 2, 3)]
-
-    arriving = add_in_plane(place, send, parts, finish)
-    swapped = [send(total.at[place.ox], got, place.to_x) for total, got in zip(total_refs, got_refs)]
-    spread = []
-    for number in range(3):
-        mine, arrived = alls[number].at[y, c], from_z[number]
-        for copy in arriving[number]:
+    over, second, arriving, spread, last = {}, {}, {}, {}, {}
+
+    def over_links(part):
+        for step, (xx, yy) in enumerate(order):
+            crossed[part][step].wait_recv()
+            add_into(held[part].at[xx, yy], take(part, xx, yy, c), from_c[part].at[xx, yy])
+            got = from_first[part]
+            if step == 0:
+                a0 = send(half(part, xx, yy, 0), got.at[0, 1], place.to_y)
+                b0 = send(half(part, xx, yy, 1), got.at[1, 1], place.to_x)
+            elif step == 1:
+                b1 = send(half(part, xx, yy, 1), got.at[1, 0], place.to_x)
+            elif step == 2:
+                a1 = send(half(part, xx, yy, 0), got.at[0, 0], place.to_y)
+        over[part] = (a0, b0, a1, b1)
+
+    def over_again(part):
+        a0, b0, a1, b1 = over[part]
+        got = from_first[part]
+        a0.wait_recv()
+        add_into(half(part, ox, y, 0), half(part, ox, y, 0), got.at[0, 1])
+        a2 = send(half(part, ox, y, 0), from_second[part].at[0], place.to_x)
+        b0.wait_recv()
+        add_into(half(part, x, oy, 1), half(part, x, oy, 1), got.at[1, 1])
+        b2 = send(half(part, x, oy, 1), from_second[part].at[1], place.to_y)
+        a1.wait_recv()
+        add_into(half(part, x, y, 0), half(part, x, y, 0), got.at[0, 0])
+        b1.wait_recv()
+        add_into(half(part, x, y, 1), half(part, x, y, 1), got.at[1, 0])
+        second[part] = (a2, b2)
+
+    def over_z(part):
+        for which, copy in enumerate(second[part]):
+            copy.wait_recv()
+            at = half_rows(which, own[part].shape[1])
+            add_into(own[part].at[:, at], half(part, x, y, which), from_second[part].at[which])
+        arriving[part] = [
+            send(own[part].at[place.zs[d]], from_z[part].at[d - 1], place.to_z[d]) for d in (1, 2, 3)
+        ]
+
+    def back_over_y(part):
+        mine, arrived = alls[part].at[y, c], from_z[part]
+        for copy in arriving[part]:
             copy.wait_recv()
         add_into(arrived.at[0], arrived.at[0], arrived.at[1])
-        add_into(arrived.at[2], arrived.at[2], own[number].at[z])
+        add_into(arrived.at[2], arrived.at[2], own[part].at[z])
         add_into(mine, arrived.at[0], arrived.at[2])
         over_y = send(mine, mine, place.to_y)
-        spread.append((over_y, send(mine, mine, place.to_c)))
-    last = []
-    for number in range(3):
-        over_y, over_c = spread[number]
+        spread[part] = (over_y, send(mine, mine, place.to_c))
+
+    def back_over_c(part):
+        over_y, over_c = spread[part]
         over_y.wait_recv()
-        other = alls[number].at[place.oy, c]
-        last.append((over_c, send(other, other, place.to_c)))
-    for number in range(3):
-        for copy in last[number]:
+        other = alls[part].at[oy, c]
+        last[part] = (over_c, send(other, other, place.to_c))
+
+    def lay_out(part):
+        for copy in last[part]:
             copy.wait_recv()
+        number, start, wide = cuts[part]
         for yy, cc in itertools.product((0, 1), (0, 1)):
             if number == 0:
                 at = (yy * 2 + cc) * piece
-                outs[0][at : at + piece, :] = alls[0][yy, cc]
+                outs[0][at : at + piece, :] = alls[part][yy, cc]
                 continue
-            wide = alls[number].shape[3]
-            at = (yy * 2 + cc) * wide
+            at = (yy * 2 + cc) * (ins[number].shape[3] // 4) + start
 
             def body(i, carry, number=number, at=at, yy=yy, cc=cc, wide=wide):
                 rows = pl.ds(pl.multiple_of(i * 16, 16), 16)
-                outs[number][rows, at : at + wide] = alls[number][yy, cc, rows, :].astype(jnp.float32)
+                outs[number][rows, at : at + wide] = alls[part][yy, cc, rows, :].astype(jnp.float32)
                 return carry
 
             lax.fori_loop(0, depth // 16, body, 0)
+
+    steps = [(over_links, 0), (over_again, 1), (over_z, 2), (back_over_y, 4), (back_over_c, 5), (lay_out, 6)]
+    swapped = []
+    for turn in range(many + 6):
+        for step, delay in steps:
+            if 0 <= turn - delay < many:
+                step(turn - delay)
+        if turn == many:
+            swapped = [send(total.at[:, ox], got, place.to_x) for total, got in zip(total_refs, got_refs)]
     for copy in swapped:
         copy.wait_recv()
     send.finish()
@@ -900,17 +889,19 @@
 def sum_grads(small, output, mixer, totals):
     depth = output.shape[2]
     arrays = (small, output, mixer)
-    shapes = [((depth // 4, small.shape[3]), small.dtype)]
-    shapes += [((depth, a.shape[3] // 4), a.dtype) for a in arrays[1:]]
+    wide = mixer.shape[3] // 4
+    split = wide * 3 // 5 // 128 * 128
+    cuts = [(0, 0, small.shape[3]), (1, 0, output.shape[3] // 4), (2, 0, split), (2, split, wide - split)]
+    shapes = [((depth // 4 if number == 0 else depth, width), arrays[number].dtype) for number, _, width in cuts]
     count = len(totals)
 
     def scratch(lead, cut=1):
         return [pltpu.VMEM(lead + (height // cut, wide), kind) for (height, wide), kind in shapes]
 
     return pl.pallas_call(
-        functools.partial(grads_kernel, count),
+        functools.partial(grads_kernel, count, cuts),
         out_shape=tuple(jax.ShapeDtypeStruct(a.shape[2:], jnp.float32) for a in arrays)
-        + tuple(jax.ShapeDtypeStruct(t.shape[1:], t.dtype) for t in totals),
+        + tuple(jax.ShapeDtypeStruct(t.shape[:1] + t.shape[2:], t.dtype) for t in totals),
         in_specs=[pl.BlockSpec(memory_space=pl.ANY)] * count + [pl.BlockSpec(memory_space=pltpu.VMEM)] * 3,
         out_specs=(pl.BlockSpec(memory_space=pltpu.VMEM),) * 3 + (pl.BlockSpec(memory_space=pl.ANY),) * count,
         scratch_shapes=scratch((2, 2, 4))
@@ -920,7 +911,7 @@
         + scratch((4,))
         + scratch((3,))
         + scratch((2, 2))
-        + [pltpu.SemaphoreType.DMA((64,)), pltpu.SemaphoreType.DMA((64,))],
+        + [pltpu.SemaphoreType.DMA((72,)), pltpu.SemaphoreType.DMA((72,))],
         compiler_params=pltpu.CompilerParams(
             collective_id=3, has_side_effects=True, vmem_limit_bytes=60 * 2**20
         ),
@@ -935,7 +926,7 @@
     send = Sender(send_sem, recv_sem)
     greet([place.to_x])
     for total, got in zip(total_refs, got_refs):
-        send(total.at[place.ox], got, place.to_x)
+        send(total.at[:, place.ox], got, place.to_x)
     for copy in send.started:
         copy.wait_recv()
     send.finish()
@@ -945,7 +936,7 @@
     count = len(totals)
     return pl.pallas_call(
         functools.partial(swap_kernel, count),
-        out_shape=tuple(jax.ShapeDtypeStruct(t.shape[1:], t.dtype) for t in totals),
+        out_shape=tuple(jax.ShapeDtypeStruct(t.shape[:1] + t.shape[2:], t.dtype) for t in totals),
         in_specs=[pl.BlockSpec(memory_space=pl.ANY)] * count,
         out_specs=(pl.BlockSpec(memory_space=pl.ANY),) * count,
         scratch_shapes=[pltpu.SemaphoreType.DMA((count,))] * 2,
@@ -955,14 +946,15 @@
     )(*totals)
 
 
-def place_kernel(count, side_ref, *refs):
-    kept_refs, got_refs = refs[:count], refs[count : 2 * count]
-    up_out, down_out = refs[2 * count :]
+def place_kernel(groups, side_ref, *refs):
+    kept_refs, got_refs = refs[:groups], refs[groups : 2 * groups]
+    up_out, down_out = refs[2 * groups :]
     half = down_out.shape[2] // 2
     first = side_ref[0] == 0
-    for expert in range(count):
-        kept = kept_refs[expert][0].astype(jnp.float32)
-        got = got_refs[expert][...].astype(jnp.float32)
+    experts = [(g, k) for g in range(groups) for k in range(kept_refs[g].shape[0])]
+    for expert, (g, k) in enumerate(experts):
+        kept = kept_refs[g][k, 0].astype(jnp.float32)
+        got = got_refs[g][k].astype(jnp.float32)
         low, high = jnp.where(first, kept, got), jnp.where(first, got, kept)
         for index, part in enumerate((low, high)):
             for group in (0, 1):
@@ -972,12 +964,12 @@
 
 
 def place_sums(side, totals, got):
-    count = len(totals)
-    depth, width = got[0].shape
+    count = sum(g.shape[0] for g in got)
+    _, depth, width = got[0].shape
     step = depth // 4
     half = width // 3
     return pl.pallas_call(
-        functools.partial(place_kernel, count),
+        functools.partial(place_kernel, len(got)),
         out_shape=(
             jax.ShapeDtypeStruct((count, depth, 4 * half), jnp.float32),
             jax.ShapeDtypeStruct((count, depth, 2 * half), jnp.float32),
@@ -985,8 +977,10 @@
         grid_spec=pltpu.PrefetchScalarGridSpec(
             num_scalar_prefetch=1,
             grid=(4,),
-            in_specs=[pl.BlockSpec((1, step, width), lambda i, side: (side[0], i, 0))] * count
-            + [pl.BlockSpec((step, width), lambda i, side: (i, 0))] * count,
+            in_specs=[
+                pl.BlockSpec((t.shape[0], 1, step, width), lambda i, side: (0, side[0], i, 0)) for t in totals
+            ]
+            + [pl.BlockSpec((g.shape[0], step, width), lambda i, side: (0, i, 0)) for g in got],
             out_specs=(
                 pl.BlockSpec((count, step, 4 * half), lambda i, side: (0, i, 0)),
                 pl.BlockSpec((count, step, 2 * half), lambda i, side: (0, i, 0)),
@@ -998,11 +992,16 @@
 
 
 def expert_kernel(
-    expert, experts_all, first_ref, table_ref, rows_ref, dout_ref, w_ref, answer_ref, row_ref, w_out, dots_ref,
-    total, picked, picked_dout,
+    expert, experts_all, first_ref, table_ref, rows_ref, dout_ref, w_ref, *refs
 ):
+    answer_ref, row_ref, w_out, dots_ref, total, picked, picked_dout = refs[-7:]
     group, slot_rows, width = answer_ref.shape
-    half = w_ref.shape[1] // 3
+    half = w_ref.shape[3] // 3
+
+    def weight(columns):
+        return w_ref[:, 0, :, columns].reshape(width, -1)
+
+    both_columns, down_columns = slice(0, 2 * half), slice(2 * half, 3 * half)
     seq_len = rows_ref.shape[1]
     step = pl.program_id(0)
     slot_ids = lax.broadcasted_iota(jnp.int32, (slot_rows, seq_len), 0).astype(jnp.float32)
@@ -1019,14 +1018,14 @@
         picked[at, :] = jnp.dot(low, rows_ref[q], preferred_element_type=jnp.float32).astype(jnp.bfloat16)
         picked_dout[at, :] = jnp.dot(low, dout_ref[q], preferred_element_type=jnp.float32).astype(jnp.bfloat16)
     gate = jnp.concatenate(gate_parts, axis=0)
-    both = jnp.dot(picked[...], w_ref[:, : 2 * half], preferred_element_type=jnp.float32)
+    both = jnp.dot(picked[...], weight(both_columns), preferred_element_type=jnp.float32)
     gate_part, up_part = both[:, :half], both[:, half:]
     sigmoid = 1.0 / (1.0 + jnp.exp(-gate_part))
     silu = gate_part * sigmoid
     active = (silu * up_part).astype(jnp.bfloat16)
     across = (((1,), (1,)), ((), ()))
     down = (((0,), (0,)), ((), ()))
-    answer = lax.dot_general(active, w_ref[:, 2 * half :], across, preferred_element_type=jnp.float32)
+    answer = lax.dot_general(active, weight(down_columns), across, preferred_element_type=jnp.float32)
     answer = answer.astype(jnp.bfloat16)
     dots = jnp.sum(picked_dout[...].astype(jnp.float32) * answer.astype(jnp.float32), axis=1, keepdims=True)
     for q in range(group):
@@ -1035,7 +1034,7 @@
         placing = (slot_ids == own_row(q, experts_all)).astype(jnp.float32)
         dots_ref[q] = jnp.sum(placing * dots[at, :], axis=0, keepdims=True)
     picked_dout[...] = (picked_dout[...].astype(jnp.float32) * gate).astype(jnp.bfloat16)
-    active_grad = jnp.dot(picked_dout[...], w_ref[:, 2 * half :], preferred_element_type=jnp.float32)
+    active_grad = jnp.dot(picked_dout[...], weight(down_columns), preferred_element_type=jnp.float32)
     both_grad = jnp.concatenate(
         [
             active_grad * up_part * sigmoid * (1.0 + gate_part * (1.0 - sigmoid)),
@@ -1043,7 +1042,7 @@
         ],
         axis=1,
     ).astype(jnp.bfloat16)
-    row = lax.dot_general(both_grad, w_ref[:, : 2 * half], across, preferred_element_type=jnp.float32)
+    row = lax.dot_general(both_grad, weight(both_columns), across, preferred_element_type=jnp.float32)
     row = row.astype(jnp.bfloat16)
     for q in range(group):
         row_ref[q] = row[q * slot_rows : (q + 1) * slot_rows, :]
@@ -1062,39 +1061,44 @@
 
     @pl.when(step == pl.num_programs(0) - 1)
     def _():
-        w_out[...] = total[...].astype(w_out.dtype)
-
-
-def run_expert(first_own, table, rows, dout, weights, expert, experts_all, slot_rows):
+        w_out[...] = total[...].astype(w_out.dtype).reshape(w_out.shape)
+
+
+def run_expert(first_own, table, rows, dout, weights, expert, experts_all, slot_rows, sums, number, sum_count):
     count, seq_len, width = rows.shape
     group = count // 2
-    wide = weights.shape[1]
+    weights, at = weights
+    parts, _, deep, wide = weights.shape
     one = pl.BlockSpec((group, 1, seq_len), lambda i: (i, 0, 0))
     listed = pl.BlockSpec((group,) + table.shape[1:], lambda i: (i, 0, 0))
     tall = pl.BlockSpec((group, seq_len, width), lambda i: (i, 0, 0))
     slot = pl.BlockSpec((group, slot_rows, width), lambda i: (i, 0, 0))
-    whole = pl.BlockSpec(weights.shape, lambda i: (0, 0))
+    taken = pl.BlockSpec((parts, 1, deep, wide), lambda i: (0, at, 0, 0))
+    given = pl.BlockSpec((parts, 1, deep, wide), lambda i: (0, number, 0, 0))
     flops = 2 * count * slot_rows * width * (2 * seq_len + 3 * wide)
+    held = [] if sums is None else [sums]
     return pl.pallas_call(
         functools.partial(expert_kernel, expert, experts_all),
         grid=(2,),
         out_shape=(
             jax.ShapeDtypeStruct((count, slot_rows, width), jnp.bfloat16),
             jax.ShapeDtypeStruct((count, slot_rows, width), jnp.bfloat16),
-            jax.ShapeDtypeStruct(weights.shape, jnp.bfloat16),
+            jax.ShapeDtypeStruct((parts, sum_count, deep, wide), jnp.bfloat16),
             jax.ShapeDtypeStruct((count, 1, seq_len), jnp.float32),
         ),
-        in_specs=[pl.BlockSpec(memory_space=pltpu.SMEM), listed, tall, tall, whole],
-        out_specs=(slot, slot, whole, one),
+        in_specs=[pl.BlockSpec(memory_space=pltpu.SMEM), listed, tall, tall, taken]
+        + [pl.BlockSpec(memory_space=pl.ANY)] * len(held),
+        out_specs=(slot, slot, given, one),
         scratch_shapes=[
-            pltpu.VMEM(weights.shape, jnp.float32),
+            pltpu.VMEM((parts * deep, wide), jnp.float32),
             pltpu.VMEM((group * slot_rows, width), jnp.bfloat16),
             pltpu.VMEM((group * slot_rows, width), jnp.bfloat16),
         ],
+        input_output_aliases={5: 2} if held else {},
         compiler_params=pltpu.CompilerParams(vmem_limit_bytes=60 * 2**20),
         cost_estimate=pl.CostEstimate(flops=flops, bytes_accessed=25_000_000, transcendentals=0),
         name="run_expert",
-    )(first_own, table, rows, dout, weights)
+    )(first_own, table, rows, dout, weights, *held)
 
 
 def layer_on_device(
@@ -1135,15 +1139,15 @@
     down_first = down_weight.transpose(1, 0, 2)
 
     def along(halves):
-        return lax.all_gather(
-            halves.reshape(2 * depth, 3 * half_inner), SHARD, axis=0, tiled=True, axis_index_groups=along_z
-        )
+        block = halves.reshape(1, halves.shape[0], 2 * depth, 3 * half_inner)
+        return lax.all_gather(block, SHARD, axis=0, tiled=True, axis_index_groups=along_z)
 
     halves = exchange_halves(up_first, down_first, 0, 1)
-    expert_weights = [along(halves[0])]
-    up_first, down_first, _ = lax.optimization_barrier((up_first, down_first, halves[0]))
+    expert_weights = [(along(halves), 0)]
+    up_first, down_first, _ = lax.optimization_barrier((up_first, down_first, halves))
     halves = exchange_halves(up_first, down_first, 1, early - 1)
-    expert_weights += [along(h) for h in halves]
+    gathered = along(halves)
+    expert_weights += [(gathered, number) for number in range(early - 1)]
 
     position = jnp.arange(seq_len, dtype=jnp.int32)
     length = lengths[0]
@@ -1161,12 +1165,13 @@
         axis=1,
     )
     mixer_block, output_block, small_block, dout_low = lax.optimization_barrier(
-        (mixer_block, output_weight, small_block, dout_low) + tuple(halves)
+        (mixer_block, output_weight, small_block, dout_low, halves)
     )[:4]
-    mixer_full, output_full, small_full, dout_plane, *halves = gather_weights(
+    mixer_full, output_full, small_full, dout_plane, halves = gather_weights(
         mixer_block, output_block, small_block, dout_low, up_first, down_first, early
     )
-    expert_weights += [along(h) for h in halves]
+    gathered = along(halves)
+    expert_weights += [(gathered, number) for number in range(local_experts - early)]
     mixer_full = mixer_full.reshape(model_width, mixer_block.shape[1])
     output_full = output_full.reshape(model_width, output_weight.shape[1])
     small_full = small_full.reshape(model_width, 128)
@@ -1223,14 +1228,19 @@
     table_plane = table_plane.reshape(8, listed, seq_len)
     first_own = (expert_at * local_experts).astype(jnp.int32).reshape(1)
     slot_rows = -(-slot_count // 16) * 16
-    turn, results = first_own, []
-    for e in range(local_experts):
-        results.append(
-            run_expert(turn, table_plane, rows_plane, dout_plane, expert_weights[e], e, experts_all, slot_rows)
-        )
-        turn = lax.optimization_barrier((first_own, results[-1][3]))[0]
-    answers, row_grads, sums, dots = zip(*results)
-    sums = lax.optimization_barrier(tuple(sums[:-1])) + (sums[-1],)
+    turn, results, sums = first_own, [], []
+    for first, count in ((0, early), (early, local_experts - early)):
+        held = None
+        for number in range(count):
+            e = first + number
+            answer, row_grad, held, dot = run_expert(
+                turn, table_plane, rows_plane, dout_plane, expert_weights[e], e, experts_all, slot_rows,
+                held, number, count,
+            )
+            results.append((answer, row_grad, dot))
+            turn = lax.optimization_barrier((first_own, dot))[0]
+        sums.append(held)
+    answers, row_grads, dots = zip(*results)
     dot_rows, grad_rows, value_rows = combine_rows(
         first_own, answers, row_grads, dots, table_plane, experts_all
     )
@@ -1244,9 +1254,9 @@
 
     totals = [
         lax.psum_scatter(
-            sums[expert], SHARD, scatter_dimension=0, tiled=True, axis_index_groups=along_z
-        ).reshape(2, depth, 3 * half_inner)
-        for expert in range(local_experts)
+            held, SHARD, scatter_dimension=0, tiled=True, axis_index_groups=along_z
+        ).reshape(held.shape[1], 2, depth, 3 * half_inner)
+        for held in sums
     ]
 
     normed_grad = grad_rows + product("se,de->sd", logits_grad, router_full)
@@ -1294,17 +1304,14 @@
         ],
         axis=1,
     ).reshape(4, 2, depth, 128)
-    swapped = 2
     small_sum, output_sum, mixer_sum, *got = sum_grads(
         small_terms,
         output_term.astype(jnp.bfloat16).reshape(4, 2, depth, output_weight.shape[1]),
         mixer_term.reshape(4, 2, depth, mixer_block.shape[1]),
-        totals[:swapped],
-    )
-    late = lax.optimization_barrier((small_sum,) + tuple(totals[swapped:-1]))[1:]
+        totals[:1],
+    )
+    late = lax.optimization_barrier((small_sum, totals[-1]))[1:]
     got += swap_totals(late, 5)
-    last = lax.optimization_barrier((got[-1], totals[-1]))[1:]
-    got += swap_totals(last, 7)
     both_sums, down_sums = place_sums(x_at.reshape(1), totals, got)
     return (
         output,

time: 623 us -> 581 us (0.933)
  Pallas kernels: 513 us -> 474 us
    pallas_call x5, Pallas kernels: 293 us -> 267 us  [the longest x1 128 us: gather_weights(): pl.pallas_call(functools.partial(weights_kernel, first), out_shape=tuple(...]
    pallas_call x2 -> x1, Pallas kernels: 25.6 us -> 16.3 us  [swap_totals(): pl.pallas_call(functools.partial(swap_kernel, count), out_shape=tuple((ja...]
  transfers between devices with their start and end apart: 10 -> 5, of which waited for: 0 -> 0; matrix products, arithmetic and copies ran while one was open for 12% -> 14% of each run, Pallas kernels for 79% -> 77%
where the time goes in v3:
time: 581 us; the launch traced here: 577 us
  Pallas kernels  474 us (82%)
  matrix products  39.2 us (7%)
  local copies, waits for them, and re-layouts  26.6 us (5%)
  other arithmetic  21.1 us (4%)
  between operations  15.7 us (3%)
    pallas_call x1, Pallas kernels, gather_weights(): pl.pallas_call(functools.partial(weights_kernel, first), out_shape=tuple(...  128 us
    pallas_call x1, Pallas kernels, sum_grads(): pl.pallas_call(functools.partial(grads_kernel, count, cuts), out_shape=tu...  107 us
    pallas_call x5, Pallas kernels, run_expert(): pl.pallas_call(functools.partial(expert_kernel, expert, experts_all), gri...  90.5 us
    pallas_call x1, Pallas kernels, combine_rows(): pl.pallas_call(functools.partial(combine_kernel, experts, experts_all), o...  63.5 us
    dot_general x16, matrix products, product(): return jnp.einsum(form, left, right, preferred_element_type=jnp.float32)  39.2 us
    pallas_call x1, Pallas kernels, gather_rows(): pl.pallas_call(rows_kernel, out_shape=(jax.ShapeDtypeStruct((2, 2, 2) + a...  35.7 us
    pallas_call x2, Pallas kernels, exchange_halves(): pl.pallas_call(functools.partial(halves_kernel, first), out_shape=jax.Sha...  27.1 us
    pallas_call x1, Pallas kernels, swap_totals(): pl.pallas_call(functools.partial(swap_kernel, count), out_shape=tuple((ja...  16.3 us
  transfers between devices with their start and end apart: 5, of which 0 were waited for; matrix products, arithmetic and copies ran while one was open for 14% of the time, Pallas kernels for 77%

profile of v3, /device:TPU:10, one launch (start us, length us, event | category | flops | bytes accessed | tf_op | source)
XLA Modules:
  0.0 576.7 jit_solution(15622526729125420913)
XLA Ops:
  7.2 10.8 %exchange_halves.2 = bf16[1,2,192,768]{3,2,1,0:T(8,128)(2,1)} custom-call(bf16[5,192,1024]{2,1,0:T(8,128)(2,1)} %bitcast.102, bf16[5,192,512]{2,1,0:T(8,128)(2,1)} %bitcast.108), custom_call_target="tpu_custom_call" | custom-call | bytes 40000000 | tf_op jit(solution)/shard_map/exchange_halves/pallas_call | solution.py:444
  18.1 16.3 %exchange_halves.3 = bf16[2,2,192,768]{3,2,1,0:T(8,128)(2,1)} custom-call(bf16[5,192,1024]{2,1,0:T(8,128)(2,1)} %bitcast.103, bf16[5,192,512]{2,1,0:T(8,128)(2,1)} %bitcast.109), custom_call_target="tpu_custom_call" | custom-call | bytes 40000000 | tf_op jit(solution)/shard_map/exchange_halves/pallas_call | solution.py:444
  38.7 128.1 %gather_weights.1 = (bf16[4,2,192,2560]{3,2,1,0:T(8,128)(2,1)}, bf16[4,2,192,1536]{3,2,1,0:T(8,128)(2,1)}, f32[4,2,192,128]{3,2,1,0:T(8,128)}, bf16[2,2,2,256,15...) custom-call(bf16[5,192,1024]{2,1,0:T(8,128)(2,1)} %bitcast.104, bf16[5,192,512]{2,1,0:T(8,128)(2,1)} %bitcast.110, ...), custom_call_target="tpu_custom_call" | custom-call | bytes 200000000 | tf_op jit(solution)/shard_map/gather_weights/pallas_call | solution.py:534
  168.9 5.5 fusion.35
  177.5 1.6 copy.114
  179.1 2.2 copy.113
  185.3 2.1 copy-done
  189.0 1.5 multiply_reduce_fusion.2
  197.1 35.7 %gather_rows.1 = (bf16[2,2,2,256,1536]{4,3,2,1,0:T(8,128)(2,1)}, f32[2,2,2,48,256]{4,3,2,1,0:T(8,128)}) custom-call(bf16[256,1536]{1,0:T(8,128)(2,1)} %copy-done.2, f32[48,256]{1,0:T(8,128)} %maximum_bitcast_fusion.3.b_ref), custom_call_target="tpu_custom_call" | custom-call | bytes 90000000 | tf_op jit(solution)/shard_map/gather_rows/pallas_call | solution.py:581
  232.8 19.0 %run_expert.5 = (bf16[8,112,1536]{2,1,0:T(8,128)(2,1)}, bf16[8,112,1536]{2,1,0:T(8,128)(2,1)}, bf16[4,3,384,768]{3,2,1,0:T(8,128)(2,1)}, f32[8,1,256]{2,1,0:T(1,128)}) custom-call(s32[1]{0:T(128)} %bitcast.20.first_ref, f32[8,48,256]{2,1,0:T(8,128)} %bitcast.139, bf16[8,256,1536]{2,1,0:T(8,128)(2,1)} %bitcast.155, bf16[8,256,1536]{2,1,0:T(8,128)(2,1)} %bitcast.150, ...), custom_call_target="tpu_custom_call" | custom-call | flops 7751073792 | bytes 25000000 | tf_op jit(solution)/shard_map/run_expert/pallas_call | solution.py:1080
  251.9 17.7 %run_expert.6 = (bf16[8,112,1536]{2,1,0:T(8,128)(2,1)}, bf16[8,112,1536]{2,1,0:T(8,128)(2,1)}, bf16[4,3,384,768]{3,2,1,0:T(8,128)(2,1)}, f32[8,1,256]{2,1,0:T(1,128)}) custom-call(s32[1]{0:T(128)} %bitcast.20.first_ref, f32[8,48,256]{2,1,0:T(8,128)} %bitcast.140, bf16[8,256,1536]{2,1,0:T(8,128)(2,1)} %bitcast.156, ...), custom_call_target="tpu_custom_call", output_to_operand_aliasing={{2}: (5, {})} | custom-call | flops 7751073792 | bytes 25000000 | tf_op jit(solution)/shard_map/run_expert/pallas_call | solution.py:1080
  269.6 17.9 %run_expert.7 = (bf16[8,112,1536]{2,1,0:T(8,128)(2,1)}, bf16[8,112,1536]{2,1,0:T(8,128)(2,1)}, bf16[4,3,384,768]{3,2,1,0:T(8,128)(2,1)}, f32[8,1,256]{2,1,0:T(1,128)}) custom-call(s32[1]{0:T(128)} %bitcast.20.first_ref, f32[8,48,256]{2,1,0:T(8,128)} %bitcast.141, bf16[8,256,1536]{2,1,0:T(8,128)(2,1)} %bitcast.157, ...), custom_call_target="tpu_custom_call", output_to_operand_aliasing={{2}: (5, {})} | custom-call | flops 7751073792 | bytes 25000000 | tf_op jit(solution)/shard_map/run_expert/pallas_call | solution.py:1080
  287.6 17.7 %run_expert.8 = (bf16[8,112,1536]{2,1,0:T(8,128)(2,1)}, bf16[8,112,1536]{2,1,0:T(8,128)(2,1)}, bf16[4,2,384,768]{3,2,1,0:T(8,128)(2,1)}, f32[8,1,256]{2,1,0:T(1,128)}) custom-call(s32[1]{0:T(128)} %bitcast.20.first_ref, f32[8,48,256]{2,1,0:T(8,128)} %bitcast.142, bf16[8,256,1536]{2,1,0:T(8,128)(2,1)} %bitcast.158, bf16[8,256,1536]{2,1,0:T(8,128)(2,1)} %bitcast.153, ...), custom_call_target="tpu_custom_call" | custom-call | flops 7751073792 | bytes 25000000 | tf_op jit(solution)/shard_map/run_expert/pallas_call | solution.py:1080
  305.3 18.2 %run_expert.9 = (bf16[8,112,1536]{2,1,0:T(8,128)(2,1)}, bf16[8,112,1536]{2,1,0:T(8,128)(2,1)}, bf16[4,2,384,768]{3,2,1,0:T(8,128)(2,1)}, f32[8,1,256]{2,1,0:T(1,128)}) custom-call(s32[1]{0:T(128)} %bitcast.20.first_ref, f32[8,48,256]{2,1,0:T(8,128)} %bitcast.143, bf16[8,256,1536]{2,1,0:T(8,128)(2,1)} %bitcast.159, ...), custom_call_target="tpu_custom_call", output_to_operand_aliasing={{2}: (5, {})} | custom-call | flops 7751073792 | bytes 25000000 | tf_op jit(solution)/shard_map/run_expert/pallas_call | solution.py:1080
  325.0 63.5 %combine_rows.1 = (f32[32,256]{1,0:T(8,128)}, f32[256,1536]{1,0:T(8,128)}, f32[256,1536]{1,0:T(8,128)}) custom-call(s32[1]{0:T(128)} %bitcast.20.first_ref, bf16[8,112,1536]{2,1,0:T(8,128)(2,1)} %get-tuple-element.70.refs_0_, bf16[8,112,1536]{2,1,0:T(8,128)(2,1)} %get-tuple-element.74.refs_1_, bf16[8,112,1536]{2,1,0:T(8,128)(2,1)} %get-tuple-element.78.refs_2_, ...), custom_call_target="tpu_custom_call" | custom-call | flops 7046430720 | bytes 150000000 | tf_op jit(solution)/shard_map/combine_rows/pallas_call | solution.py:743
  389.5 2.2 multiply_reduce_fusion
  391.8 3.0 multiply_add_fusion
  397.4 1.5 concatenate.58
  398.9 4.8 fusion
  404.0 1.6 fusion.2
  405.7 2.1 fusion.23
  411.2 6.8 %fusion.19 = (f32[1536]{0:T(1024)S(1)}, f32[256]{0:T(256)S(1)}, f32[256,1536]{1,0:T(8,128)}) fusion(bf16[256,1536]{1,0:T(8,128)(2,1)S(1)} %copy-done.6, f32[256]{0:T(256)S(1)} %copy-done.48, f32[1536]{0:T(1024)S(1)} %get-tuple-element.165, bf16[1536,2560]{1,0:T(8,128)(2,1)} %bitcast.149, bf16[256,512]{0,1:T(8,128)(2,1)S(1)} %bitcast.130, ...), kind=kOutput, calls=%fused_computation.33 | convolution fusion | flops 2019948800 | bytes 11548672 | tf_op jit(solution)/shard_map/sf,df->sd/dot_general | solution.py:19
  418.0 1.5 concatenate.57
  420.8 2.8 maximum_maximum_fusion.refs_1_
  423.6 3.6 convolution_convert_fusion.1
  427.2 5.5 convolution_convert_fusion
  432.7 1.6 fusion.15
  434.4 107.1 %sum_grads.1 = (f32[192,128]{1,0:T(8,128)}, f32[192,1536]{1,0:T(8,128)}, f32[192,2560]{1,0:T(8,128)}, bf16[3,192,768]{2,1,0:T(8,128)(2,1)}) custom-call(bf16[3,2,192,768]{3,2,1,0:T(8,128)(2,1)} %bitcast.113, f32[4,2,192,128]{3,2,1,0:T(8,128)} %maximum_maximum_fusion.refs_1_, bf16[4,2,192,1536]{3,2,1,0:T(8,128)(2,1)} %bitcast.101, ...), custom_call_target="tpu_custom_call" | custom-call | bytes 300000000 | tf_op jit(solution)/shard_map/sum_grads/pallas_call | solution.py:901
  541.5 2.4 slice.81
  544.7 2.0 fusion.52
  547.4 16.3 %swap_totals.1.refs_3_ = bf16[2,192,768]{2,1,0:T(8,128)(2,1)} custom-call(bf16[2,2,192,768]{3,2,1,0:T(8,128)(2,1)} %bitcast.117), custom_call_target="tpu_custom_call" | custom-call | bytes 40000000 | tf_op jit(solution)/shard_map/swap_totals/pallas_call | solution.py:937
  563.7 5.2 place_sums.1
  (207 shorter events, 33.0 us)
Async XLA Ops:
  7.2 225.6 %all-gather.4.cloned.1.call-start = ((), (), s32[]{:S(2)}) async-start(), calls=%async_computation.2 | async-start | bytes 2949120 | tf_op jit(solution)/shard_map/all_gather | solution.py:1143
  18.0 17.3 %copy-start.58 = (bf16[192]{0:T(256)(128)(2,1)S(1)}, bf16[192]{0:T(256)(128)(2,1)}, u32[]{:S(2)}) copy-start(bf16[192]{0:T(256)(128)(2,1)} %param.17) | copy-start | bytes 1156
  18.0 17.3 %copy-start.59 = (bf16[192]{0:T(256)(128)(2,1)S(1)}, bf16[192]{0:T(256)(128)(2,1)}, u32[]{:S(2)}) copy-start(bf16[192]{0:T(256)(128)(2,1)} %param.22) | copy-start | bytes 1156
  18.0 17.6 %copy-start.53 = (bf16[192,20]{0,1:T(8,128)(2,1)S(1)}, bf16[192,20]{0,1:T(8,128)(2,1)}, u32[]{:S(2)}) copy-start(bf16[192,20]{0,1:T(8,128)(2,1)} %param.23) | copy-start | bytes 23044
  18.0 233.8 %all-gather.6.cloned.1.call-start = ((), (), s32[]{:S(2)}) async-start(), calls=%async_computation.3 | async-start | bytes 5898240 | tf_op jit(solution)/shard_map/all_gather | solution.py:1143
  34.5 253.1 %all-gather.8.cloned.1.call-start = ((), (), s32[]{:S(2)}) async-start(), calls=%async_computation.4 | async-start | bytes 5898240 | tf_op jit(solution)/shard_map/all_gather | solution.py:1143
  38.7 128.4 %copy-start.5 = (bf16[256,1536]{1,0:T(8,128)(2,1)S(1)}, bf16[256,1536]{1,0:T(8,128)(2,1)}, u32[]{:S(2)}) copy-start(bf16[256,1536]{1,0:T(8,128)(2,1)} %param.13) | copy-start | bytes 2359300
  166.8 267.5 %reduce-scatter.3.cloned.1.call-start = ((), (), s32[]{:S(2)}) async-start(), calls=%async_computation.5 | async-start | bytes 8847360 | tf_op jit(solution)/shard_map/reduce_scatter | solution.py:1256
  168.8 21.8 %copy-start.41 = (f32[1536]{0:T(1024)}, f32[1536]{0:T(1024)S(1)}, u32[]{:S(2)}) copy-start(f32[1536]{0:T(1024)S(1)} %get-tuple-element.164) | copy-start | bytes 18436
  179.1 3.6 copy-start.9
  184.1 3.2 copy-start
  184.1 3.2 copy-start.35
  184.2 3.2 copy-start.19
  184.2 4.5 slice-start.2
  185.3 3.3 copy-start.37
  190.6 198.8 %copy-start.1 = (f32[256,1536]{1,0:T(8,128)}, f32[256,1536]{1,0:T(8,128)S(1)}, u32[]{:S(2)}) copy-start(f32[256,1536]{1,0:T(8,128)S(1)} %get-tuple-element.187) | copy-start | bytes 4718596
  190.8 6.3 %copy-start.2 = (bf16[256,1536]{1,0:T(8,128)(2,1)}, bf16[256,1536]{1,0:T(8,128)(2,1)S(1)}, u32[]{:S(2)}) copy-start(bf16[256,1536]{1,0:T(8,128)(2,1)S(1)} %multiply_convert_fusion.a_ref) | copy-start | bytes 2359300
  287.5 259.2 %reduce-scatter.5.cloned.1.call-start = ((), (), s32[]{:S(2)}) async-start(), calls=%async_computation.6 | async-start | bytes 5898240 | tf_op jit(solution)/shard_map/reduce_scatter | solution.py:1256
  324.9 64.3 %copy-start.40 = (s32[256,8]{0,1:T(8,128)S(1)}, s32[256,8]{0,1:T(8,128)}, u32[]{:S(2)}) copy-start(s32[256,8]{0,1:T(8,128)} %param.15) | copy-start | bytes 24580
  324.9 64.3 %copy-start.46 = (f32[256]{0:T(256)S(1)}, f32[256]{0:T(256)}, u32[]{:S(2)}) copy-start(f32[256]{0:T(256)} %reduce_max.19) | copy-start | bytes 3076
  324.9 64.3 %copy-start.50 = (f32[256]{0:T(256)S(1)}, f32[256]{0:T(256)}, u32[]{:S(2)}) copy-start(f32[256]{0:T(256)} %copy-done.49) | copy-start | bytes 3076
  324.9 64.5 %copy-start.42 = (f32[1536]{0:T(1024)S(1)}, f32[1536]{0:T(1024)}, u32[]{:S(2)}) copy-start(f32[1536]{0:T(1024)} %copy-done.41) | copy-start | bytes 18436
  324.9 64.5 %copy-start.52 = (f32[256]{0:T(256)S(1)}, f32[256]{0:T(256)}, u32[]{:S(2)}) copy-start(f32[256]{0:T(256)} %copy-done.51) | copy-start | bytes 3076
  389.5 5.3 slice-start.4
  398.9 4.8 slice-start
  398.9 5.1 slice-start.1
  411.2 8.3 %copy-start.3 = (bf16[256,1536]{1,0:T(8,128)(2,1)S(1)}, bf16[256,1536]{1,0:T(8,128)(2,1)}, u32[]{:S(2)}) copy-start(bf16[256,1536]{1,0:T(8,128)(2,1)} %copy-done.2) | copy-start | bytes 2359300
  411.2 8.3 %copy-start.44 = (bf16[256,20]{0,1:T(8,128)(2,1)S(1)}, bf16[256,20]{0,1:T(8,128)(2,1)}, u32[]{:S(2)}) copy-start(bf16[256,20]{0,1:T(8,128)(2,1)} %copy-done.43) | copy-start | bytes 30724
  423.6 3.6 copy-start.7
  423.6 3.6 copy-start.11
  427.2 5.5 copy-start.16
  563.7 5.2 copy-start.18
  (39 other events, 68.9 us)
Sparse Core Ops, SparseCore 0:
  18.1 77.2 all-gather.3
  97.0 88.9 all-gather.5
  187.5 87.7 all-gather.7
  287.6 122.7 reduce-scatter.2
  412.5 114.2 reduce-scatter.4

commit v4 on v3

--- a/solution.py
+++ b/solution.py
@@ -357,46 +357,59 @@
     pl.semaphore_wait(barrier, len(devices))
 
 
-def gather_in_plane(place, send, items, beside=lambda: None):
+def gather_in_plane(place, send, groups, beside=lambda: None):
     x, y, c = place.x, place.y, place.c
-    ox, oy = place.ox, place.oy
-    first = []
-    for view, source, ready, own in items:
-        for copy in ready:
-            copy.wait_recv()
-        block = source(y, None)
-        by_x = send(block, view(x, y, c, None), place.to_x)
-        by_y, back = None, None
-        if own:
-            back = send(source(oy, 1), view(x, oy, c, 1), place.to_x)
-        else:
-            by_y = send(block, view(x, y, c, None), place.to_y)
-        first.append((by_x, by_y, back))
-    result = beside()
-    landed = []
-    for (view, source, ready, own), (by_x, by_y, back) in zip(items, first):
-        if not own:
-            landed.append(send(source(y, None), view(x, y, c, None), place.to_c))
-        by_x.wait_recv()
-        over_y = send(view(ox, y, c, 0), view(ox, y, c, 0), place.to_y)
-        landed.append(send(view(ox, y, c, None), view(ox, y, c, None), place.to_c))
-        if not own:
-            by_y.wait_recv()
-            back = send(view(x, oy, c, 1), view(x, oy, c, 1), place.to_x)
-            landed.append(send(view(x, oy, c, None), view(x, oy, c, None), place.to_c))
-        landed.append((view, over_y, back))
-    final = []
-    for entry in landed:
-        if isinstance(entry, tuple):
-            view, over_y, back = entry
+    ox, oy, oc = place.ox, place.oy, place.oc
+    first, landed, final = {}, {}, []
+
+    def over_links(number):
+        first[number] = []
+        for view, source, ready, own in groups[number]:
+            ready()
+            block = source(y, None)
+            by_x = send(block, view(x, y, c, None), place.to_x)
+            by_y, back = None, None
+            if own:
+                back = send(source(oy, 1), view(x, oy, c, 1), place.to_x)
+            else:
+                by_y = send(block, view(x, y, c, None), place.to_y)
+            first[number].append((by_x, by_y, back))
+
+    def over_again(number):
+        landed[number] = []
+        for (view, source, ready, own), (by_x, by_y, back) in zip(groups[number], first[number]):
+            if not own:
+                final.append(send(source(y, None), view(x, y, c, None), place.to_c))
+            by_x.wait_recv()
+            over_y = send(view(ox, y, c, 0), view(ox, y, c, 0), place.to_y)
+            final.append(send(view(ox, y, c, None), view(ox, y, c, None), place.to_c))
+            if not own:
+                by_y.wait_recv()
+                back = send(view(x, oy, c, 1), view(x, oy, c, 1), place.to_x)
+                final.append(send(view(x, oy, c, None), view(x, oy, c, None), place.to_c))
+            landed[number].append((view, over_y, back))
+
+    def over_core(number):
+        for view, over_y, back in landed[number]:
             over_y.wait_recv()
             back.wait_recv()
             final.append(send(view(ox, oy, c, None), view(ox, oy, c, None), place.to_c))
-        else:
-            final.append(entry)
+
+    result = None
+    for turn in range(len(groups) + 2):
+        for delay, step in enumerate((over_links, over_again, over_core)):
+            if 0 <= turn - delay < len(groups):
+                step(turn - delay)
+        if turn == min(1, len(groups) - 1):
+            result = beside()
     for copy in final:
         copy.wait_recv()
     return result
+
+
+def cut_rows(half, rows):
+    more = rows * 3 // 4 // 16 * 16
+    return pl.ds(0, rows) if half is None else pl.ds(more, rows - more) if half else pl.ds(0, more)
 
 
 def half_rows(half, rows):
@@ -416,7 +429,7 @@
     send.finish()
 
 
-def start_halves(place, send, copy_sem, up_ref, down_ref, out_ref, first):
+def start_halves(place, send, copy_sem, up_ref, down_ref, out_ref, first, base=0):
     x, ox = place.x, place.ox
     half = down_ref.shape[2] // 2
     sent, local = [], []
@@ -432,7 +445,7 @@
             sent.append(send(piece, out.at[x, :, index * half : (index + 1) * half], place.to_x))
         for index, piece in enumerate(pieces(x)):
             copy = pltpu.make_async_copy(
-                piece, out.at[x, :, index * half : (index + 1) * half], copy_sem.at[3 * number + index]
+                piece, out.at[x, :, index * half : (index + 1) * half], copy_sem.at[base + 3 * number + index]
             )
             copy.start()
             local.append(copy)
@@ -454,9 +467,10 @@
 
 
 def weights_kernel(
-    first, up_ref, down_ref, w_ref, o_ref, small_ref, rows_ref, w_out, o_out, small_out, rows_out, halves_out,
-    send_sem, recv_sem, copy_sem, half_sem,
+    first, up_ref, down_ref, w_ref, o_ref, small_ref, rows_ref, w_out, o_out, small_out, rows_out,
+    *refs,
 ):
+    halves_outs, (send_sem, recv_sem, copy_sem, half_sem) = refs[:-4], refs[-4:]
     place = Place()
     send = Sender(send_sem, recv_sem)
     x, y, c, z = place.x, place.y, place.c, place.z
@@ -477,7 +491,7 @@
 
     wide = [(w_ref, w_out), (o_ref, o_out)]
     from_z = {}
-    for d in (1, 2, 3):
+    for d in (2, 1):
         from_z[d] = [
             send(ref.at[:, columns(ref, y, c)], out.at[z, x, :, columns(ref, y, c)], place.to_z[d])
             for ref, out in wide
@@ -492,33 +506,59 @@
         copy.start()
 
     def wide_view(ref, out, zz):
-        return lambda xx, yy, cc, half: out.at[zz, xx, half_rows(half, depth), columns(ref, yy, cc)]
+        return lambda xx, yy, cc, half: out.at[zz, xx, cut_rows(half, depth), columns(ref, yy, cc)]
 
     def small_view(zz):
         return lambda xx, yy, cc, half: small_out.at[zz, xx, pieces(yy, cc, half)]
 
     def rows_view(xx, yy, cc, half):
-        return rows_out.at[cc, xx, yy, half_rows(half, blocks)]
+        return rows_out.at[cc, xx, yy, cut_rows(half, blocks)]
 
     items = [
         (
             wide_view(ref, out, z),
-            lambda yy, half, ref=ref: ref.at[half_rows(half, depth), columns(ref, yy, c)],
-            [],
+            lambda yy, half, ref=ref: ref.at[cut_rows(half, depth), columns(ref, yy, c)],
+            lambda: None,
             True,
         )
         for ref, out in wide
     ]
-    items.append((small_view(z), lambda yy, half: small_ref.at[pieces(yy, c, half)], [], True))
+    items.append((small_view(z), lambda yy, half: small_ref.at[pieces(yy, c, half)], lambda: None, True))
+    items.append((rows_view, lambda yy, half: rows_ref.at[cut_rows(half, blocks)], lambda: None, False))
+    from_z[3] = []
+
+    def arrive(d, number, view):
+        from_z[d][number].wait_recv()
+        if d == 2:
+            block = view(x, y, c, None)
+            from_z[3].append(send(block, block, place.to_z[1]))
+
+    groups = [items]
     for d in (1, 2, 3):
         zz = place.zs[d]
         views = [wide_view(ref, out, zz) for ref, out in wide] + [small_view(zz)]
-        for view, copy in zip(views, from_z[d]):
-            items.append((view, lambda yy, half, view=view: view(x, yy, c, half), [copy], False))
-    items.append((rows_view, lambda yy, half: rows_ref.at[half_rows(half, blocks)], [], False))
-    sent, kept = gather_in_plane(
-        place, send, items, lambda: start_halves(place, send, half_sem, up_ref, down_ref, halves_out, first)
-    )
+        groups.append(
+            [
+                (
+                    view,
+                    lambda yy, half, view=view: view(x, yy, c, half),
+                    functools.partial(arrive, d, number, view),
+                    False,
+                )
+                for number, view in enumerate(views)
+            ]
+        )
+
+    def beside():
+        sent, kept, expert = [], [], first
+        for out in halves_outs:
+            more_sent, more_kept = start_halves(
+                place, send, half_sem, up_ref, down_ref, out, expert, 3 * (expert - first)
+            )
+            sent, kept, expert = sent + more_sent, kept + more_kept, expert + out.shape[0]
+        return sent, kept
+
+    sent, kept = gather_in_plane(place, send, groups, beside)
     for copy in sent:
         copy.wait_recv()
     for copy in local + kept:
@@ -526,18 +566,18 @@
     send.finish()
 
 
-def gather_weights(w, o, small, rows, up, down, first):
+def gather_weights(w, o, small, rows, up, down, first, counts):
     depth, inner = down.shape[1:]
-    count = up.shape[0] - first
+    count = sum(counts)
     copies = 128
     arrays = (w, o, small)
     return pl.pallas_call(
         functools.partial(weights_kernel, first),
         out_shape=tuple(jax.ShapeDtypeStruct((4, 2) + a.shape, a.dtype) for a in arrays)
         + (jax.ShapeDtypeStruct((2, 2, 2) + rows.shape, rows.dtype),)
-        + (jax.ShapeDtypeStruct((count, 2, depth, 3 * inner // 2), up.dtype),),
+        + tuple(jax.ShapeDtypeStruct((n, 2, depth, 3 * inner // 2), up.dtype) for n in counts),
         in_specs=[pl.BlockSpec(memory_space=pltpu.VMEM)] * 6,
-        out_specs=(pl.BlockSpec(memory_space=pl.ANY),) * 5,
+        out_specs=(pl.BlockSpec(memory_space=pl.ANY),) * (4 + len(counts)),
         scratch_shapes=[
             pltpu.SemaphoreType.DMA((copies,)),
             pltpu.SemaphoreType.DMA((copies,)),
@@ -567,11 +607,11 @@
         return (
             lambda xx, yy, cc, half: out.at[cc, xx, yy, half_rows(half, rows)],
             lambda yy, half: source.at[half_rows(half, rows)],
-            [],
+            lambda: None,
             False,
         )
 
-    gather_in_plane(place, send, [item(b_ref, b_out), item(a_ref, a_out)])
+    gather_in_plane(place, send, [[item(b_ref, b_out), item(a_ref, a_out)]])
     for copy in local:
         copy.wait()
     send.finish()
@@ -768,10 +808,11 @@
     )(first_own, *answers, *row_grads, *dots, table)
 
 
-def grads_kernel(count, cuts, *refs):
+def grads_kernel(count, cuts, spans, *refs):
     total_refs, refs = refs[:count], refs[count:]
     ins, refs = refs[:3], refs[3:]
-    outs, got_refs, refs = refs[:3], refs[3 : 3 + count], refs[3 + count :]
+    outs, refs = refs[: len(spans)], refs[len(spans) :]
+    got_refs, refs = refs[:count], refs[count:]
     many = len(cuts)
     held, from_c, from_first, from_second, own, from_z, alls = (refs[many * i : many * (i + 1)] for i in range(7))
     send_sem, recv_sem = refs[7 * many :]
@@ -836,15 +877,20 @@
             at = half_rows(which, own[part].shape[1])
             add_into(own[part].at[:, at], half(part, x, y, which), from_second[part].at[which])
         arriving[part] = [
-            send(own[part].at[place.zs[d]], from_z[part].at[d - 1], place.to_z[d]) for d in (1, 2, 3)
+            send(own[part].at[place.zs[d]], from_z[part].at[slot], place.to_z[1]) for slot, d in ((1, 3), (0, 1))
         ]
+
+    def over_z_again(part):
+        arrived = from_z[part]
+        for copy in arriving[part]:
+            copy.wait_recv()
+        add_into(arrived.at[1], arrived.at[1], own[part].at[place.zs[2]])
+        arriving[part] = send(arrived.at[1], arrived.at[2], place.to_z[2])
+        add_into(arrived.at[0], arrived.at[0], own[part].at[z])
 
     def back_over_y(part):
         mine, arrived = alls[part].at[y, c], from_z[part]
-        for copy in arriving[part]:
-            copy.wait_recv()
-        add_into(arrived.at[0], arrived.at[0], arrived.at[1])
-        add_into(arrived.at[2], arrived.at[2], own[part].at[z])
+        arriving[part].wait_recv()
         add_into(mine, arrived.at[0], arrived.at[2])
         over_y = send(mine, mine, place.to_y)
         spread[part] = (over_y, send(mine, mine, place.to_c))
@@ -865,17 +911,23 @@
                 outs[0][at : at + piece, :] = alls[part][yy, cc]
                 continue
             at = (yy * 2 + cc) * (ins[number].shape[3] // 4) + start
-
-            def body(i, carry, number=number, at=at, yy=yy, cc=cc, wide=wide):
-                rows = pl.ds(pl.multiple_of(i * 16, 16), 16)
-                outs[number][rows, at : at + wide] = alls[part][yy, cc, rows, :].astype(jnp.float32)
-                return carry
-
-            lax.fori_loop(0, depth // 16, body, 0)
-
-    steps = [(over_links, 0), (over_again, 1), (over_z, 2), (back_over_y, 4), (back_over_c, 5), (lay_out, 6)]
+            for out, (owner, low, high) in zip(outs, spans):
+                left, right = max(low, at), min(high, at + wide)
+                if owner != number or left >= right:
+                    continue
+
+                def body(i, carry, out=out, low=low, left=left, right=right, at=at, yy=yy, cc=cc):
+                    rows = pl.ds(pl.multiple_of(i * 16, 16), 16)
+                    block = alls[part][yy, cc, rows, left - at : right - at]
+                    out[rows, left - low : right - low] = block.astype(jnp.float32)
+                    return carry
+
+                lax.fori_loop(0, depth // 16, body, 0)
+
+    steps = [(over_links, 0), (over_again, 1), (over_z, 2), (over_z_again, 3)]
+    steps += [(back_over_y, 5), (back_over_c, 6), (lay_out, 7)]
     swapped = []
-    for turn in range(many + 6):
+    for turn in range(many + 7):
         for step, delay in steps:
             if 0 <= turn - delay < many:
                 step(turn - delay)
@@ -886,7 +938,7 @@
     send.finish()
 
 
-def sum_grads(small, output, mixer, totals):
+def sum_grads(small, output, mixer, totals, q_width):
     depth = output.shape[2]
     arrays = (small, output, mixer)
     wide = mixer.shape[3] // 4
@@ -894,16 +946,20 @@
     cuts = [(0, 0, small.shape[3]), (1, 0, output.shape[3] // 4), (2, 0, split), (2, split, wide - split)]
     shapes = [((depth // 4 if number == 0 else depth, width), arrays[number].dtype) for number, _, width in cuts]
     count = len(totals)
+    last = (q_width + mixer.shape[3]) // 2
+    spans = [(0, 0, small.shape[3]), (1, 0, output.shape[3])]
+    spans += [(2, 0, q_width), (2, q_width, last), (2, last, mixer.shape[3])]
 
     def scratch(lead, cut=1):
         return [pltpu.VMEM(lead + (height // cut, wide), kind) for (height, wide), kind in shapes]
 
     return pl.pallas_call(
-        functools.partial(grads_kernel, count, cuts),
-        out_shape=tuple(jax.ShapeDtypeStruct(a.shape[2:], jnp.float32) for a in arrays)
+        functools.partial(grads_kernel, count, cuts, spans),
+        out_shape=tuple(jax.ShapeDtypeStruct((depth, high - low), jnp.float32) for _, low, high in spans)
         + tuple(jax.ShapeDtypeStruct(t.shape[:1] + t.shape[2:], t.dtype) for t in totals),
         in_specs=[pl.BlockSpec(memory_space=pl.ANY)] * count + [pl.BlockSpec(memory_space=pltpu.VMEM)] * 3,
-        out_specs=(pl.BlockSpec(memory_space=pltpu.VMEM),) * 3 + (pl.BlockSpec(memory_space=pl.ANY),) * count,
+        out_specs=(pl.BlockSpec(memory_space=pltpu.VMEM),) * len(spans)
+        + (pl.BlockSpec(memory_space=pl.ANY),) * count,
         scratch_shapes=scratch((2, 2, 4))
         + scratch((2, 2, 4))
         + scratch((2, 2, 4), 2)
@@ -1134,7 +1190,7 @@
     x_at = lax.rem(shard_at, 2)
     depth = first_gain.shape[0]
 
-    early = 3
+    early = 4
     up_first = gate_up_weight.transpose(1, 0, 2)
     down_first = down_weight.transpose(1, 0, 2)
 
@@ -1167,11 +1223,12 @@
     mixer_block, output_block, small_block, dout_low = lax.optimization_barrier(
         (mixer_block, output_weight, small_block, dout_low, halves)
     )[:4]
-    mixer_full, output_full, small_full, dout_plane, halves = gather_weights(
-        mixer_block, output_block, small_block, dout_low, up_first, down_first, early
-    )
-    gathered = along(halves)
-    expert_weights += [(gathered, number) for number in range(local_experts - early)]
+    mixer_full, output_full, small_full, dout_plane, *halves = gather_weights(
+        mixer_block, output_block, small_block, dout_low, up_first, down_first, early, (local_experts - early,)
+    )
+    for some in halves:
+        gathered = along(some)
+        expert_weights += [(gathered, number) for number in range(some.shape[0])]
     mixer_full = mixer_full.reshape(model_width, mixer_block.shape[1])
     output_full = output_full.reshape(model_width, output_weight.shape[1])
     small_full = small_full.reshape(model_width, 128)
@@ -1229,7 +1286,7 @@
     first_own = (expert_at * local_experts).astype(jnp.int32).reshape(1)
     slot_rows = -(-slot_count // 16) * 16
     turn, results, sums = first_own, [], []
-    for first, count in ((0, early), (early, local_experts - early)):
+    for first, count in ((0, 3), (3, local_experts - 3)):
         held = None
         for number in range(count):
             e = first + number
@@ -1304,11 +1361,12 @@
         ],
         axis=1,
     ).reshape(4, 2, depth, 128)
-    small_sum, output_sum, mixer_sum, *got = sum_grads(
+    small_sum, output_sum, query_sum, key_sum, value_sum, *got = sum_grads(
         small_terms,
         output_term.astype(jnp.bfloat16).reshape(4, 2, depth, output_weight.shape[1]),
         mixer_term.reshape(4, 2, depth, mixer_block.shape[1]),
         totals[:1],
+        q_width,
     )
     late = lax.optimization_barrier((small_sum, totals[-1]))[1:]
     got += swap_totals(late, 5)
@@ -1317,9 +1375,9 @@
         output,
         tokens_grad,
         small_sum[:, experts_all],
-        mixer_sum[:, :q_width],
-        mixer_sum[:, q_width : q_width + kv_width],
-        mixer_sum[:, q_width + kv_width :],
+        query_sum,
+        key_sum,
+        value_sum,
         output_sum,
         small_sum[:, experts_all + 1],
         small_sum[:, :experts_all],

time: 581 us -> 564 us (0.971)
  Pallas kernels: 474 us -> 452 us
    pallas_call x1, Pallas kernels: 128 us -> 107 us  [gather_weights(): pl.pallas_call(functools.partial(weights_kernel, first), out_shape=tuple(...]
    pallas_call x1, Pallas kernels: 107 us -> 100 us  [sum_grads(): pl.pallas_call(functools.partial(grads_kernel, count, cuts, spans), out_s...]
    pallas_call x2, Pallas kernels: 27.1 us -> 33.5 us  [exchange_halves(): pl.pallas_call(functools.partial(halves_kernel, first), out_shape=jax.Sha...]
    unnamed x134 -> x137, local copies, waits for them, and re-layouts: 8.99 us -> 12.6 us
  transfers between devices with their start and end apart: 5 -> 5, of which waited for: 0 -> 0; matrix products, arithmetic and copies ran while one was open for 14% -> 14% of each run, Pallas kernels for 77% -> 75%
where the time goes in v4:
time: 564 us; the launch traced here: 556 us
  Pallas kernels  452 us (80%)
  matrix products  39.3 us (7%)
  local copies, waits for them, and re-layouts  25.9 us (5%)
  other arithmetic  22.8 us (4%)
  between operations  15.7 us (3%)
    pallas_call x1, Pallas kernels, gather_weights(): pl.pallas_call(functools.partial(weights_kernel, first), out_shape=tuple(...  107 us
    pallas_call x1, Pallas kernels, sum_grads(): pl.pallas_call(functools.partial(grads_kernel, count, cuts, spans), out_s...  100 us
    pallas_call x5, Pallas kernels, run_expert(): pl.pallas_call(functools.partial(expert_kernel, expert, experts_all), gri...  91.6 us
    pallas_call x1, Pallas kernels, combine_rows(): pl.pallas_call(functools.partial(combine_kernel, experts, experts_all), o...  63.7 us
    dot_general x16, matrix products, product(): return jnp.einsum(form, left, right, preferred_element_type=jnp.float32)  39.3 us
    pallas_call x1, Pallas kernels, gather_rows(): pl.pallas_call(rows_kernel, out_shape=(jax.ShapeDtypeStruct((2, 2, 2) + a...  34.7 us
    pallas_call x2, Pallas kernels, exchange_halves(): pl.pallas_call(functools.partial(halves_kernel, first), out_shape=jax.Sha...  33.5 us
    pallas_call x1, Pallas kernels, swap_totals(): pl.pallas_call(functools.partial(swap_kernel, count), out_shape=tuple((ja...  16.3 us
  transfers between devices with their start and end apart: 5, of which 0 were waited for; matrix products, arithmetic and copies ran while one was open for 14% of the time, Pallas kernels for 75%

profile of v4, /device:TPU:10, one launch (start us, length us, event | category | flops | bytes accessed | tf_op | source)
XLA Modules:
  0.0 556.2 jit_solution(2458215559452912709)
XLA Ops:
  7.2 10.8 %exchange_halves.2 = bf16[1,2,192,768]{3,2,1,0:T(8,128)(2,1)} custom-call(bf16[5,192,1024]{2,1,0:T(8,128)(2,1)} %bitcast.102, bf16[5,192,512]{2,1,0:T(8,128)(2,1)} %bitcast.108), custom_call_target="tpu_custom_call" | custom-call | bytes 40000000 | tf_op jit(solution)/shard_map/exchange_halves/pallas_call | solution.py:457
  18.1 22.7 %exchange_halves.3 = bf16[3,2,192,768]{3,2,1,0:T(8,128)(2,1)} custom-call(bf16[5,192,1024]{2,1,0:T(8,128)(2,1)} %bitcast.103, bf16[5,192,512]{2,1,0:T(8,128)(2,1)} %bitcast.109), custom_call_target="tpu_custom_call" | custom-call | bytes 40000000 | tf_op jit(solution)/shard_map/exchange_halves/pallas_call | solution.py:457
  45.1 106.8 %gather_weights.1 = (bf16[4,2,192,2560]{3,2,1,0:T(8,128)(2,1)}, bf16[4,2,192,1536]{3,2,1,0:T(8,128)(2,1)}, f32[4,2,192,128]{3,2,1,0:T(8,128)}, bf16[2,2,2,256,15...) custom-call(bf16[5,192,1024]{2,1,0:T(8,128)(2,1)} %bitcast.104, bf16[5,192,512]{2,1,0:T(8,128)(2,1)} %bitcast.110, ...), custom_call_target="tpu_custom_call" | custom-call | bytes 200000000 | tf_op jit(solution)/shard_map/gather_weights/pallas_call | solution.py:574
  154.0 5.6 fusion.35
  162.9 1.6 copy.114
  165.8 1.7 subtract_convert_fusion.1
  170.0 2.1 copy-done
  173.7 1.5 multiply_reduce_fusion.2
  183.3 34.7 %gather_rows.1 = (bf16[2,2,2,256,1536]{4,3,2,1,0:T(8,128)(2,1)}, f32[2,2,2,48,256]{4,3,2,1,0:T(8,128)}) custom-call(bf16[256,1536]{1,0:T(8,128)(2,1)} %copy-done.2, f32[48,256]{1,0:T(8,128)} %maximum_bitcast_fusion.3.b_ref), custom_call_target="tpu_custom_call" | custom-call | bytes 90000000 | tf_op jit(solution)/shard_map/gather_rows/pallas_call | solution.py:621
  218.0 19.2 %run_expert.5 = (bf16[8,112,1536]{2,1,0:T(8,128)(2,1)}, bf16[8,112,1536]{2,1,0:T(8,128)(2,1)}, bf16[4,3,384,768]{3,2,1,0:T(8,128)(2,1)}, f32[8,1,256]{2,1,0:T(1,128)}) custom-call(s32[1]{0:T(128)} %bitcast.20.first_ref, f32[8,48,256]{2,1,0:T(8,128)} %bitcast.139, bf16[8,256,1536]{2,1,0:T(8,128)(2,1)} %bitcast.155, bf16[8,256,1536]{2,1,0:T(8,128)(2,1)} %bitcast.150, ...), custom_call_target="tpu_custom_call" | custom-call | flops 7751073792 | bytes 25000000 | tf_op jit(solution)/shard_map/run_expert/pallas_call | solution.py:1136
  237.3 17.7 %run_expert.6 = (bf16[8,112,1536]{2,1,0:T(8,128)(2,1)}, bf16[8,112,1536]{2,1,0:T(8,128)(2,1)}, bf16[4,3,384,768]{3,2,1,0:T(8,128)(2,1)}, f32[8,1,256]{2,1,0:T(1,128)}) custom-call(s32[1]{0:T(128)} %bitcast.20.first_ref, f32[8,48,256]{2,1,0:T(8,128)} %bitcast.140, bf16[8,256,1536]{2,1,0:T(8,128)(2,1)} %bitcast.156, ...), custom_call_target="tpu_custom_call", output_to_operand_aliasing={{2}: (5, {})} | custom-call | flops 7751073792 | bytes 25000000 | tf_op jit(solution)/shard_map/run_expert/pallas_call | solution.py:1136
  255.0 17.9 %run_expert.7 = (bf16[8,112,1536]{2,1,0:T(8,128)(2,1)}, bf16[8,112,1536]{2,1,0:T(8,128)(2,1)}, bf16[4,3,384,768]{3,2,1,0:T(8,128)(2,1)}, f32[8,1,256]{2,1,0:T(1,128)}) custom-call(s32[1]{0:T(128)} %bitcast.20.first_ref, f32[8,48,256]{2,1,0:T(8,128)} %bitcast.141, bf16[8,256,1536]{2,1,0:T(8,128)(2,1)} %bitcast.157, ...), custom_call_target="tpu_custom_call", output_to_operand_aliasing={{2}: (5, {})} | custom-call | flops 7751073792 | bytes 25000000 | tf_op jit(solution)/shard_map/run_expert/pallas_call | solution.py:1136
  273.0 17.7 %run_expert.8 = (bf16[8,112,1536]{2,1,0:T(8,128)(2,1)}, bf16[8,112,1536]{2,1,0:T(8,128)(2,1)}, bf16[4,2,384,768]{3,2,1,0:T(8,128)(2,1)}, f32[8,1,256]{2,1,0:T(1,128)}) custom-call(s32[1]{0:T(128)} %bitcast.20.first_ref, f32[8,48,256]{2,1,0:T(8,128)} %bitcast.142, bf16[8,256,1536]{2,1,0:T(8,128)(2,1)} %bitcast.158, bf16[8,256,1536]{2,1,0:T(8,128)(2,1)} %bitcast.153, ...), custom_call_target="tpu_custom_call" | custom-call | flops 7751073792 | bytes 25000000 | tf_op jit(solution)/shard_map/run_expert/pallas_call | solution.py:1136
  290.7 19.1 %run_expert.9 = (bf16[8,112,1536]{2,1,0:T(8,128)(2,1)}, bf16[8,112,1536]{2,1,0:T(8,128)(2,1)}, bf16[4,2,384,768]{3,2,1,0:T(8,128)(2,1)}, f32[8,1,256]{2,1,0:T(1,128)}) custom-call(s32[1]{0:T(128)} %bitcast.20.first_ref, f32[8,48,256]{2,1,0:T(8,128)} %bitcast.143, bf16[8,256,1536]{2,1,0:T(8,128)(2,1)} %bitcast.159, ...), custom_call_target="tpu_custom_call", output_to_operand_aliasing={{2}: (5, {})} | custom-call | flops 7751073792 | bytes 25000000 | tf_op jit(solution)/shard_map/run_expert/pallas_call | solution.py:1136
  311.2 63.7 %combine_rows.1 = (f32[32,256]{1,0:T(8,128)}, f32[256,1536]{1,0:T(8,128)}, f32[256,1536]{1,0:T(8,128)}) custom-call(s32[1]{0:T(128)} %bitcast.20.first_ref, bf16[8,112,1536]{2,1,0:T(8,128)(2,1)} %get-tuple-element.72.refs_0_, bf16[8,112,1536]{2,1,0:T(8,128)(2,1)} %get-tuple-element.76.refs_1_, bf16[8,112,1536]{2,1,0:T(8,128)(2,1)} %get-tuple-element.80.refs_2_, ...), custom_call_target="tpu_custom_call" | custom-call | flops 7046430720 | bytes 150000000 | tf_op jit(solution)/shard_map/combine_rows/pallas_call | solution.py:783
  375.9 2.2 multiply_reduce_fusion
  378.3 3.0 multiply_add_fusion
  383.9 1.5 concatenate.58
  385.4 4.8 fusion
  390.5 1.6 fusion.2
  392.2 2.1 fusion.23
  397.7 6.8 %fusion.19 = (f32[1536]{0:T(1024)S(1)}, f32[256]{0:T(256)S(1)}, f32[256,1536]{1,0:T(8,128)}) fusion(bf16[256,1536]{1,0:T(8,128)(2,1)S(1)} %copy-done.6, f32[256]{0:T(256)S(1)} %copy-done.48, f32[1536]{0:T(1024)S(1)} %get-tuple-element.169, bf16[1536,2560]{1,0:T(8,128)(2,1)} %bitcast.149, bf16[256,512]{0,1:T(8,128)(2,1)S(1)} %bitcast.129, ...), kind=kOutput, calls=%fused_computation.33 | convolution fusion | flops 2019948800 | bytes 11548672 | tf_op jit(solution)/shard_map/sf,df->sd/dot_general | solution.py:19
  404.5 1.5 concatenate.57
  407.3 2.8 maximum_maximum_fusion.refs_1_
  410.1 3.6 convolution_convert_fusion.1
  413.7 5.5 convolution_convert_fusion
  419.2 1.6 fusion.15
  420.9 100.1 %sum_grads.1 = (f32[192,128]{1,0:T(8,128)}, f32[192,1536]{1,0:T(8,128)}, f32[192,1536]{1,0:T(8,128)}, f32[192,512]{1,0:T(8,128)}, f32[192,512]{1,0:T(8,128)}, /*index=5*/bf16[3,192,768]{2,1,0:T(8,128)(2,1)}) custom-call(bf16[3,2,192,768]{3,2,1,0:T(8,128)(2,1)} %bitcast.114, f32[4,2,192,128]{3,2,1,0:T(8,128)} %maximum_maximum_fusion.refs_1_, ...), custom_call_target="tpu_custom_call" | custom-call | bytes 300000000 | tf_op jit(solution)/shard_map/sum_grads/pallas_call | solution.py:956
  521.0 1.8 slice_reduce_fusion.2
  522.7 1.6 copy.124
  524.3 16.3 %swap_totals.1.refs_3_ = bf16[2,192,768]{2,1,0:T(8,128)(2,1)} custom-call(bf16[2,2,192,768]{3,2,1,0:T(8,128)(2,1)} %bitcast.118), custom_call_target="tpu_custom_call" | custom-call | bytes 40000000 | tf_op jit(solution)/shard_map/swap_totals/pallas_call | solution.py:993
  540.6 5.2 place_sums.1
  (208 shorter events, 35.7 us)
Async XLA Ops:
  7.2 210.8 %all-gather.4.cloned.1.call-start = ((), (), s32[]{:S(2)}) async-start(), calls=%async_computation.2 | async-start | bytes 2949120 | tf_op jit(solution)/shard_map/all_gather | solution.py:1199
  18.0 219.3 %all-gather.6.cloned.1.call-start = ((), (), s32[]{:S(2)}) async-start(), calls=%async_computation.3 | async-start | bytes 8847360 | tf_op jit(solution)/shard_map/all_gather | solution.py:1199
  40.9 3.1 copy-start.12
  40.9 249.8 %all-gather.8.cloned.1.call-start = ((), (), s32[]{:S(2)}) async-start(), calls=%async_computation.4 | async-start | bytes 2949120 | tf_op jit(solution)/shard_map/all_gather | solution.py:1199
  45.1 107.1 %copy-start.5 = (bf16[256,1536]{1,0:T(8,128)(2,1)S(1)}, bf16[256,1536]{1,0:T(8,128)(2,1)}, u32[]{:S(2)}) copy-start(bf16[256,1536]{1,0:T(8,128)(2,1)} %param.13) | copy-start | bytes 2359300
  152.0 268.9 %reduce-scatter.3.cloned.1.call-start = ((), (), s32[]{:S(2)}) async-start(), calls=%async_computation.5 | async-start | bytes 8847360 | tf_op jit(solution)/shard_map/reduce_scatter | solution.py:1313
  154.0 21.3 %copy-start.41 = (f32[1536]{0:T(1024)}, f32[1536]{0:T(1024)S(1)}, u32[]{:S(2)}) copy-start(f32[1536]{0:T(1024)S(1)} %get-tuple-element.168) | copy-start | bytes 18436
  164.6 3.0 copy-start.20
  164.6 3.0 copy-start.22
  168.8 3.2 copy-start
  168.8 3.2 copy-start.36
  168.8 3.2 copy-start.19
  168.8 4.6 slice-start.2
  169.9 3.3 copy-start.38
  175.2 200.6 %copy-start.1 = (f32[256,1536]{1,0:T(8,128)}, f32[256,1536]{1,0:T(8,128)S(1)}, u32[]{:S(2)}) copy-start(f32[256,1536]{1,0:T(8,128)S(1)} %get-tuple-element.189) | copy-start | bytes 4718596
  175.9 7.4 %copy-start.2 = (bf16[256,1536]{1,0:T(8,128)(2,1)}, bf16[256,1536]{1,0:T(8,128)(2,1)S(1)}, u32[]{:S(2)}) copy-start(bf16[256,1536]{1,0:T(8,128)(2,1)S(1)} %multiply_convert_fusion.a_ref) | copy-start | bytes 2359300
  272.9 249.8 %reduce-scatter.5.cloned.1.call-start = ((), (), s32[]{:S(2)}) async-start(), calls=%async_computation.6 | async-start | bytes 5898240 | tf_op jit(solution)/shard_map/reduce_scatter | solution.py:1313
  311.2 64.5 %copy-start.40 = (s32[256,8]{0,1:T(8,128)S(1)}, s32[256,8]{0,1:T(8,128)}, u32[]{:S(2)}) copy-start(s32[256,8]{0,1:T(8,128)} %param.15) | copy-start | bytes 24580
  311.2 64.5 %copy-start.46 = (f32[256]{0:T(256)S(1)}, f32[256]{0:T(256)}, u32[]{:S(2)}) copy-start(f32[256]{0:T(256)} %reduce_max.19) | copy-start | bytes 3076
  311.2 64.5 %copy-start.50 = (f32[256]{0:T(256)S(1)}, f32[256]{0:T(256)}, u32[]{:S(2)}) copy-start(f32[256]{0:T(256)} %copy-done.49) | copy-start | bytes 3076
  311.2 64.7 %copy-start.42 = (f32[1536]{0:T(1024)S(1)}, f32[1536]{0:T(1024)}, u32[]{:S(2)}) copy-start(f32[1536]{0:T(1024)} %copy-done.41) | copy-start | bytes 18436
  311.2 64.7 %copy-start.52 = (f32[256]{0:T(256)S(1)}, f32[256]{0:T(256)}, u32[]{:S(2)}) copy-start(f32[256]{0:T(256)} %copy-done.51) | copy-start | bytes 3076
  375.9 5.3 slice-start.4
  378.2 3.0 slice-start.5
  385.4 4.8 slice-start
  385.4 5.1 slice-start.1
  397.7 8.3 %copy-start.3 = (bf16[256,1536]{1,0:T(8,128)(2,1)S(1)}, bf16[256,1536]{1,0:T(8,128)(2,1)}, u32[]{:S(2)}) copy-start(bf16[256,1536]{1,0:T(8,128)(2,1)} %copy-done.2) | copy-start | bytes 2359300
  397.7 8.3 %copy-start.44 = (bf16[256,20]{0,1:T(8,128)(2,1)S(1)}, bf16[256,20]{0,1:T(8,128)(2,1)}, u32[]{:S(2)}) copy-start(bf16[256,20]{0,1:T(8,128)(2,1)} %copy-done.43) | copy-start | bytes 30724
  410.1 3.6 copy-start.7
  410.1 3.6 copy-start.10
  413.7 5.5 copy-start.15
  540.6 5.2 copy-start.18
  (39 other events, 65.1 us)
Sparse Core Ops, SparseCore 0:
  18.1 65.2 all-gather.3
  85.0 127.5 all-gather.5
  214.1 49.3 all-gather.7
  273.0 123.7 reduce-scatter.2
  398.9 95.7 reduce-scatter.4

commit v5 on v4

--- a/solution.py
+++ b/solution.py
@@ -408,7 +408,7 @@
 
 
 def cut_rows(half, rows):
-    more = rows * 3 // 4 // 16 * 16
+    more = rows * 2 // 3 // 16 * 16
     return pl.ds(0, rows) if half is None else pl.ds(more, rows - more) if half else pl.ds(0, more)
 
 
@@ -924,7 +924,7 @@
 
                 lax.fori_loop(0, depth // 16, body, 0)
 
-    steps = [(over_links, 0), (over_again, 1), (over_z, 2), (over_z_again, 3)]
+    steps = [(over_links, 0), (over_again, 1), (over_z, 2), (over_z_again, 4)]
     steps += [(back_over_y, 5), (back_over_c, 6), (lay_out, 7)]
     swapped = []
     for turn in range(many + 7):

time: 564 us -> 559 us (level)
  no operation moved by 1% of the time
where the time goes in v5:
time: 559 us; the launch traced here: 551 us
  Pallas kernels  447 us (80%)
  matrix products  39.3 us (7%)
  local copies, waits for them, and re-layouts  26 us (5%)
  other arithmetic  22.8 us (4%)
  between operations  15.7 us (3%)
    pallas_call x1, Pallas kernels, gather_weights(): pl.pallas_call(functools.partial(weights_kernel, first), out_shape=tuple(...  102 us
    pallas_call x1, Pallas kernels, sum_grads(): pl.pallas_call(functools.partial(grads_kernel, count, cuts, spans), out_s...  100 us
    pallas_call x5, Pallas kernels, run_expert(): pl.pallas_call(functools.partial(expert_kernel, expert, experts_all), gri...  91.5 us
    pallas_call x1, Pallas kernels, combine_rows(): pl.pallas_call(functools.partial(combine_kernel, experts, experts_all), o...  63.6 us
    dot_general x16, matrix products, product(): return jnp.einsum(form, left, right, preferred_element_type=jnp.float32)  39.3 us
    pallas_call x1, Pallas kernels, gather_rows(): pl.pallas_call(rows_kernel, out_shape=(jax.ShapeDtypeStruct((2, 2, 2) + a...  34.7 us
    pallas_call x2, Pallas kernels, exchange_halves(): pl.pallas_call(functools.partial(halves_kernel, first), out_shape=jax.Sha...  33.5 us
    pallas_call x1, Pallas kernels, swap_totals(): pl.pallas_call(functools.partial(swap_kernel, count), out_shape=tuple((ja...  16.3 us
  transfers between devices with their start and end apart: 5, of which 0 were waited for; matrix products, arithmetic and copies ran while one was open for 14% of the time, Pallas kernels for 75%

profile of v5, /device:TPU:10, one launch (start us, length us, event | category | flops | bytes accessed | tf_op | source)
XLA Modules:
  0.0 551.1 jit_solution(8428114809617073709)
XLA Ops:
  7.2 10.8 %exchange_halves.2 = bf16[1,2,192,768]{3,2,1,0:T(8,128)(2,1)} custom-call(bf16[5,192,1024]{2,1,0:T(8,128)(2,1)} %bitcast.102, bf16[5,192,512]{2,1,0:T(8,128)(2,1)} %bitcast.108), custom_call_target="tpu_custom_call" | custom-call | bytes 40000000 | tf_op jit(solution)/shard_map/exchange_halves/pallas_call | solution.py:457
  18.1 22.7 %exchange_halves.3 = bf16[3,2,192,768]{3,2,1,0:T(8,128)(2,1)} custom-call(bf16[5,192,1024]{2,1,0:T(8,128)(2,1)} %bitcast.103, bf16[5,192,512]{2,1,0:T(8,128)(2,1)} %bitcast.109), custom_call_target="tpu_custom_call" | custom-call | bytes 40000000 | tf_op jit(solution)/shard_map/exchange_halves/pallas_call | solution.py:457
  45.1 101.9 %gather_weights.1 = (bf16[4,2,192,2560]{3,2,1,0:T(8,128)(2,1)}, bf16[4,2,192,1536]{3,2,1,0:T(8,128)(2,1)}, f32[4,2,192,128]{3,2,1,0:T(8,128)}, bf16[2,2,2,256,15...) custom-call(bf16[5,192,1024]{2,1,0:T(8,128)(2,1)} %bitcast.104, bf16[5,192,512]{2,1,0:T(8,128)(2,1)} %bitcast.110, ...), custom_call_target="tpu_custom_call" | custom-call | bytes 200000000 | tf_op jit(solution)/shard_map/gather_weights/pallas_call | solution.py:574
  149.1 5.5 fusion.35
  158.0 1.6 copy.114
  160.9 1.7 subtract_convert_fusion.1
  165.0 2.0 copy-done
  168.7 1.5 multiply_reduce_fusion.2
  178.3 34.7 %gather_rows.1 = (bf16[2,2,2,256,1536]{4,3,2,1,0:T(8,128)(2,1)}, f32[2,2,2,48,256]{4,3,2,1,0:T(8,128)}) custom-call(bf16[256,1536]{1,0:T(8,128)(2,1)} %copy-done.2, f32[48,256]{1,0:T(8,128)} %maximum_bitcast_fusion.3.b_ref), custom_call_target="tpu_custom_call" | custom-call | bytes 90000000 | tf_op jit(solution)/shard_map/gather_rows/pallas_call | solution.py:621
  213.0 19.0 %run_expert.5 = (bf16[8,112,1536]{2,1,0:T(8,128)(2,1)}, bf16[8,112,1536]{2,1,0:T(8,128)(2,1)}, bf16[4,3,384,768]{3,2,1,0:T(8,128)(2,1)}, f32[8,1,256]{2,1,0:T(1,128)}) custom-call(s32[1]{0:T(128)} %bitcast.20.first_ref, f32[8,48,256]{2,1,0:T(8,128)} %bitcast.139, bf16[8,256,1536]{2,1,0:T(8,128)(2,1)} %bitcast.155, bf16[8,256,1536]{2,1,0:T(8,128)(2,1)} %bitcast.150, ...), custom_call_target="tpu_custom_call" | custom-call | flops 7751073792 | bytes 25000000 | tf_op jit(solution)/shard_map/run_expert/pallas_call | solution.py:1136
  232.1 17.7 %run_expert.6 = (bf16[8,112,1536]{2,1,0:T(8,128)(2,1)}, bf16[8,112,1536]{2,1,0:T(8,128)(2,1)}, bf16[4,3,384,768]{3,2,1,0:T(8,128)(2,1)}, f32[8,1,256]{2,1,0:T(1,128)}) custom-call(s32[1]{0:T(128)} %bitcast.20.first_ref, f32[8,48,256]{2,1,0:T(8,128)} %bitcast.140, bf16[8,256,1536]{2,1,0:T(8,128)(2,1)} %bitcast.156, ...), custom_call_target="tpu_custom_call", output_to_operand_aliasing={{2}: (5, {})} | custom-call | flops 7751073792 | bytes 25000000 | tf_op jit(solution)/shard_map/run_expert/pallas_call | solution.py:1136
  249.8 17.9 %run_expert.7 = (bf16[8,112,1536]{2,1,0:T(8,128)(2,1)}, bf16[8,112,1536]{2,1,0:T(8,128)(2,1)}, bf16[4,3,384,768]{3,2,1,0:T(8,128)(2,1)}, f32[8,1,256]{2,1,0:T(1,128)}) custom-call(s32[1]{0:T(128)} %bitcast.20.first_ref, f32[8,48,256]{2,1,0:T(8,128)} %bitcast.141, bf16[8,256,1536]{2,1,0:T(8,128)(2,1)} %bitcast.157, ...), custom_call_target="tpu_custom_call", output_to_operand_aliasing={{2}: (5, {})} | custom-call | flops 7751073792 | bytes 25000000 | tf_op jit(solution)/shard_map/run_expert/pallas_call | solution.py:1136
  267.8 17.7 %run_expert.8 = (bf16[8,112,1536]{2,1,0:T(8,128)(2,1)}, bf16[8,112,1536]{2,1,0:T(8,128)(2,1)}, bf16[4,2,384,768]{3,2,1,0:T(8,128)(2,1)}, f32[8,1,256]{2,1,0:T(1,128)}) custom-call(s32[1]{0:T(128)} %bitcast.20.first_ref, f32[8,48,256]{2,1,0:T(8,128)} %bitcast.142, bf16[8,256,1536]{2,1,0:T(8,128)(2,1)} %bitcast.158, bf16[8,256,1536]{2,1,0:T(8,128)(2,1)} %bitcast.153, ...), custom_call_target="tpu_custom_call" | custom-call | flops 7751073792 | bytes 25000000 | tf_op jit(solution)/shard_map/run_expert/pallas_call | solution.py:1136
  285.5 19.1 %run_expert.9 = (bf16[8,112,1536]{2,1,0:T(8,128)(2,1)}, bf16[8,112,1536]{2,1,0:T(8,128)(2,1)}, bf16[4,2,384,768]{3,2,1,0:T(8,128)(2,1)}, f32[8,1,256]{2,1,0:T(1,128)}) custom-call(s32[1]{0:T(128)} %bitcast.20.first_ref, f32[8,48,256]{2,1,0:T(8,128)} %bitcast.143, bf16[8,256,1536]{2,1,0:T(8,128)(2,1)} %bitcast.159, ...), custom_call_target="tpu_custom_call", output_to_operand_aliasing={{2}: (5, {})} | custom-call | flops 7751073792 | bytes 25000000 | tf_op jit(solution)/shard_map/run_expert/pallas_call | solution.py:1136
  306.1 63.6 %combine_rows.1 = (f32[32,256]{1,0:T(8,128)}, f32[256,1536]{1,0:T(8,128)}, f32[256,1536]{1,0:T(8,128)}) custom-call(s32[1]{0:T(128)} %bitcast.20.first_ref, bf16[8,112,1536]{2,1,0:T(8,128)(2,1)} %get-tuple-element.72.refs_0_, bf16[8,112,1536]{2,1,0:T(8,128)(2,1)} %get-tuple-element.76.refs_1_, bf16[8,112,1536]{2,1,0:T(8,128)(2,1)} %get-tuple-element.80.refs_2_, ...), custom_call_target="tpu_custom_call" | custom-call | flops 7046430720 | bytes 150000000 | tf_op jit(solution)/shard_map/combine_rows/pallas_call | solution.py:783
  370.6 2.2 multiply_reduce_fusion
  372.9 3.0 multiply_add_fusion
  378.6 1.5 concatenate.58
  380.1 4.8 fusion
  385.2 1.6 fusion.2
  386.9 2.1 fusion.23
  392.4 6.8 %fusion.19 = (f32[1536]{0:T(1024)S(1)}, f32[256]{0:T(256)S(1)}, f32[256,1536]{1,0:T(8,128)}) fusion(bf16[256,1536]{1,0:T(8,128)(2,1)S(1)} %copy-done.6, f32[256]{0:T(256)S(1)} %copy-done.48, f32[1536]{0:T(1024)S(1)} %get-tuple-element.169, bf16[1536,2560]{1,0:T(8,128)(2,1)} %bitcast.149, bf16[256,512]{0,1:T(8,128)(2,1)S(1)} %bitcast.129, ...), kind=kOutput, calls=%fused_computation.33 | convolution fusion | flops 2019948800 | bytes 11548672 | tf_op jit(solution)/shard_map/sf,df->sd/dot_general | solution.py:19
  399.2 1.5 concatenate.57
  402.0 2.8 maximum_maximum_fusion.refs_1_
  404.8 3.6 convolution_convert_fusion.1
  408.4 5.5 %convolution_convert_fusion = bf16[1536,2560]{1,0:T(8,128)(2,1)} fusion(bf16[256,512]{0,1:T(8,128)(2,1)S(1)} %bitcast.130, bf16[256,512]{0,1:T(8,128)(2,1)S(1)} %bitcast.132, bf16[256,1536]{0,1:T(8,128)(2,1)S(1)} %bitcast.121, bf16[256,1536]{1,0:T(8,128)(2,1)S(1)} %copy-done.7, f32[1536]{0:T(1024)S(1)} %get-tuple-element.169, f32[256]{0:T(256)S(1)} %copy-done.48), kind=kOutput, calls=%fused_computation | convolution fusion | flops 2022703104 | bytes 9968640 | tf_op jit(solution)/shard_map/sd,sf->df/dot_general | solution.py:19
  414.0 1.6 fusion.15
  415.6 100.2 %sum_grads.1 = (f32[192,128]{1,0:T(8,128)}, f32[192,1536]{1,0:T(8,128)}, f32[192,1536]{1,0:T(8,128)}, f32[192,512]{1,0:T(8,128)}, f32[192,512]{1,0:T(8,128)}, /*index=5*/bf16[3,192,768]{2,1,0:T(8,128)(2,1)}) custom-call(bf16[3,2,192,768]{3,2,1,0:T(8,128)(2,1)} %bitcast.114, f32[4,2,192,128]{3,2,1,0:T(8,128)} %maximum_maximum_fusion.refs_1_, ...), custom_call_target="tpu_custom_call" | custom-call | bytes 300000000 | tf_op jit(solution)/shard_map/sum_grads/pallas_call | solution.py:956
  515.8 1.8 slice_reduce_fusion.2
  517.6 1.6 copy.124
  519.2 16.3 %swap_totals.1.refs_3_ = bf16[2,192,768]{2,1,0:T(8,128)(2,1)} custom-call(bf16[2,2,192,768]{3,2,1,0:T(8,128)(2,1)} %bitcast.118), custom_call_target="tpu_custom_call" | custom-call | bytes 40000000 | tf_op jit(solution)/shard_map/swap_totals/pallas_call | solution.py:993
  535.5 5.2 place_sums.1
  (208 shorter events, 35.8 us)
Async XLA Ops:
  7.2 205.9 %all-gather.4.cloned.1.call-start = ((), (), s32[]{:S(2)}) async-start(), calls=%async_computation.2 | async-start | bytes 2949120 | tf_op jit(solution)/shard_map/all_gather | solution.py:1199
  18.0 214.1 %all-gather.6.cloned.1.call-start = ((), (), s32[]{:S(2)}) async-start(), calls=%async_computation.3 | async-start | bytes 8847360 | tf_op jit(solution)/shard_map/all_gather | solution.py:1199
  40.9 3.1 copy-start.12
  40.9 244.6 %all-gather.8.cloned.1.call-start = ((), (), s32[]{:S(2)}) async-start(), calls=%async_computation.4 | async-start | bytes 2949120 | tf_op jit(solution)/shard_map/all_gather | solution.py:1199
  45.1 102.2 %copy-start.5 = (bf16[256,1536]{1,0:T(8,128)(2,1)S(1)}, bf16[256,1536]{1,0:T(8,128)(2,1)}, u32[]{:S(2)}) copy-start(bf16[256,1536]{1,0:T(8,128)(2,1)} %param.13) | copy-start | bytes 2359300
  147.0 268.6 %reduce-scatter.3.cloned.1.call-start = ((), (), s32[]{:S(2)}) async-start(), calls=%async_computation.5 | async-start | bytes 8847360 | tf_op jit(solution)/shard_map/reduce_scatter | solution.py:1313
  149.1 21.2 %copy-start.41 = (f32[1536]{0:T(1024)}, f32[1536]{0:T(1024)S(1)}, u32[]{:S(2)}) copy-start(f32[1536]{0:T(1024)S(1)} %get-tuple-element.168) | copy-start | bytes 18436
  159.6 2.9 copy-start.20
  159.6 3.0 copy-start.22
  163.8 3.2 copy-start
  163.8 3.2 copy-start.36
  163.8 3.2 copy-start.19
  163.8 4.6 slice-start.2
  165.0 3.3 copy-start.38
  170.3 200.3 %copy-start.1 = (f32[256,1536]{1,0:T(8,128)}, f32[256,1536]{1,0:T(8,128)S(1)}, u32[]{:S(2)}) copy-start(f32[256,1536]{1,0:T(8,128)S(1)} %get-tuple-element.189) | copy-start | bytes 4718596
  170.9 7.4 %copy-start.2 = (bf16[256,1536]{1,0:T(8,128)(2,1)}, bf16[256,1536]{1,0:T(8,128)(2,1)S(1)}, u32[]{:S(2)}) copy-start(bf16[256,1536]{1,0:T(8,128)(2,1)S(1)} %multiply_convert_fusion.a_ref) | copy-start | bytes 2359300
  267.8 249.9 %reduce-scatter.5.cloned.1.call-start = ((), (), s32[]{:S(2)}) async-start(), calls=%async_computation.6 | async-start | bytes 5898240 | tf_op jit(solution)/shard_map/reduce_scatter | solution.py:1313
  306.1 64.3 %copy-start.40 = (s32[256,8]{0,1:T(8,128)S(1)}, s32[256,8]{0,1:T(8,128)}, u32[]{:S(2)}) copy-start(s32[256,8]{0,1:T(8,128)} %param.15) | copy-start | bytes 24580
  306.1 64.4 %copy-start.46 = (f32[256]{0:T(256)S(1)}, f32[256]{0:T(256)}, u32[]{:S(2)}) copy-start(f32[256]{0:T(256)} %reduce_max.19) | copy-start | bytes 3076
  306.1 64.4 %copy-start.50 = (f32[256]{0:T(256)S(1)}, f32[256]{0:T(256)}, u32[]{:S(2)}) copy-start(f32[256]{0:T(256)} %copy-done.49) | copy-start | bytes 3076
  306.1 64.5 %copy-start.42 = (f32[1536]{0:T(1024)S(1)}, f32[1536]{0:T(1024)}, u32[]{:S(2)}) copy-start(f32[1536]{0:T(1024)} %copy-done.41) | copy-start | bytes 18436
  306.1 64.5 %copy-start.52 = (f32[256]{0:T(256)S(1)}, f32[256]{0:T(256)}, u32[]{:S(2)}) copy-start(f32[256]{0:T(256)} %copy-done.51) | copy-start | bytes 3076
  370.6 5.3 slice-start.4
  372.9 3.0 slice-start.5
  380.1 4.8 slice-start
  380.1 5.1 slice-start.1
  392.4 8.3 %copy-start.3 = (bf16[256,1536]{1,0:T(8,128)(2,1)S(1)}, bf16[256,1536]{1,0:T(8,128)(2,1)}, u32[]{:S(2)}) copy-start(bf16[256,1536]{1,0:T(8,128)(2,1)} %copy-done.2) | copy-start | bytes 2359300
  392.4 8.3 %copy-start.44 = (bf16[256,20]{0,1:T(8,128)(2,1)S(1)}, bf16[256,20]{0,1:T(8,128)(2,1)}, u32[]{:S(2)}) copy-start(bf16[256,20]{0,1:T(8,128)(2,1)} %copy-done.43) | copy-start | bytes 30724
  404.8 3.6 copy-start.7
  404.8 3.6 copy-start.10
  408.4 5.5 %copy-start.15 = (f32[256,1536]{1,0:T(8,128)S(1)}, f32[256,1536]{1,0:T(8,128)}, u32[]{:S(2)}) copy-start(f32[256,1536]{1,0:T(8,128)} %get-tuple-element.193) | copy-start | bytes 4718596
  535.5 5.2 copy-start.18
  (39 other events, 65.2 us)
Sparse Core Ops, SparseCore 0:
  18.1 65.2 all-gather.3
  85.0 127.5 all-gather.5
  214.1 49.3 all-gather.7
  267.9 123.6 reduce-scatter.2
  393.8 94.9 reduce-scatter.4
